TPU v7x, 512 devices: a whole 4x4x16 slice. The times are simulated.
512 devices in a mesh: sub: 64 (over z_hi, x, y, core), chan: 8 (over z_lo).
Axes of the slice: x: 4, y: 4, z: 16 (z_hi: 2, z_lo: 8; z = z_hi * 8 + z_lo), core: 2. Of those that a mesh axis runs over, the one named last changes fastest.
Arguments:
- raw_pulses: bfloat16 [2, 2048, 8, 2048], P(None, 'sub', 'chan'), may hold values from -6 to 6
- range_filter: bfloat16 [2, 2048, 1024], P(None, ('sub', 'chan')), may hold values from -0.09375 to 0.09375
- channel_mix: float32 [2, 32, 8, 8], replicated, may hold values from -1.5 to 1.5
- steer_angles: float32 [256], replicated, may hold values from -3.140625 to 3.140625
- band_offsets: int32 [4, 512], replicated, may hold values from 0 to 248
- band_weights: float32 [4, 2, 2, 512, 8], replicated, may hold values from -1 to 1
- smoothing: float32 [16384], P('sub'), may hold values from 0.3 to 0.5
Outputs:
- despeckled: float32 [16384, 1024], P('sub', 'chan')
All inputs are finite; a program needn't handle non-finite values.
Results may differ from a plain program's by a relative error of at most 0.0036.
Values may be sent and summed in bfloat16 or wider, within the bound.
No kernel may reach another device: no remote copies, remote signals or barrier semaphores. Data moves between devices by JAX's collectives and lax.ppermute only.
A program may use at most 64 MiB of HBM per device.

v0:
```python
import jax
import jax.numpy as jnp
import numpy as np
from jax import lax
from jax.sharding import Mesh
from jax.sharding import PartitionSpec as P

ANG = 256
LEVELS = 4
PASSES = 3
SUB = ("sub_0", "sub_1", "sub_2", "sub_3")
SUB_CHAN = ("sub_0", "sub_1", "sub_2", "sub_3", "chan")


HIGH = lax.Precision.HIGHEST


def partner_2(value, axis, stride):
    mask = 2**stride
    pairs = [(source, source ^ mask) for source in range(lax.axis_size(axis))]
    return lax.ppermute(value, axis, pairs)


def cut_rows(length, count):
    unit = 8 if length >= 8 * count else 1
    return [length // unit * k // count * unit for k in range(1, count)]


def all_blocks(array, axes, sequence):
    pieces = array
    for k in sequence:
        pieces = lax.all_gather(pieces, axes[k])
    done = sequence[::-1]
    back = [done.index(k) for k in range(len(axes))]
    pieces = pieces.transpose(*back, *range(len(axes), pieces.ndim))
    return pieces.reshape(-1, *array.shape)


def in_order(pieces, dim):
    dims = list(pieces.shape[1:])
    dims[dim] *= pieces.shape[0]
    return jnp.moveaxis(pieces, 0, dim).reshape(dims)


def spread_gather(array, axes, dim):
    numbers = list(range(len(axes)))[::-1]
    cut = array.shape.index(max(array.shape[:-1] or array.shape))
    edges = [0, *cut_rows(array.shape[cut], len(axes)), array.shape[cut]]
    gathered = []
    for k, (start, end) in enumerate(zip(edges, edges[1:])):
        if end > start:
            slab = lax.slice_in_dim(array, start, end, axis=cut)
            gathered.append(all_blocks(slab, axes, numbers[k:] + numbers[:k]))
    return in_order(jnp.concatenate(gathered, axis=cut + 1), dim)


def padded_2(array, sides, width):
    for axis, dim in sides:
        devices, length = (lax.axis_size(axis), array.shape[dim])
        up = [(i, (i + 1) % devices) for i in range(devices - 1)]
        down = [(j, i) for i, j in up]
        last = lax.slice_in_dim(array, length - width, length, axis=dim)
        initial = lax.slice_in_dim(array, 0, width, axis=dim)
        before = lax.ppermute(last, axis, up)
        after = lax.ppermute(initial, axis, down)
        array = jnp.concatenate([before, array, after], axis=dim)
    return array


def doppler_table(count):
    index_row = jnp.arange(count, dtype=jnp.int32)
    product = index_row[:, None] * index_row[None, :] % count
    phase = 2.0 * np.pi / count * product.astype(jnp.float32)
    factor = 1.0 / np.sqrt(count)
    return (
        (jnp.cos(phase) * factor).astype(jnp.bfloat16),
        (-jnp.sin(phase) * factor).astype(jnp.bfloat16),
    )


def steer_table(steer_angles, count):
    offsets = jnp.arange(count, dtype=jnp.int32).astype(jnp.float32) - 0.5 * count
    phase = steer_angles[:, None] * offsets[None, :]
    factor = 1.0 / np.sqrt(count)
    return (
        (jnp.cos(phase) * factor).astype(jnp.bfloat16),
        (jnp.sin(phase) * factor).astype(jnp.bfloat16),
    )


def low_dot(left, right):
    return jnp.dot(left, right, preferred_element_type=jnp.float32)


def range_terms(echo_rows, filter_rows):
    real_part = low_dot(echo_rows[0], filter_rows[0]) - low_dot(echo_rows[1], filter_rows[1])
    imag_part = low_dot(echo_rows[0], filter_rows[1]) + low_dot(echo_rows[1], filter_rows[0])
    return jnp.stack([real_part, imag_part])


def form_image(compressed, dop_real, dop_imag, channel_mix, beam_real, beam_imag):
    pulse_count = compressed.shape[1]
    channels = compressed.shape[2]
    cells = compressed.shape[3]
    flat = compressed.reshape(2, pulse_count, channels * cells)
    spec_real = (low_dot(dop_real, flat[0]) - low_dot(dop_imag, flat[1])).reshape(
        pulse_count, channels, cells
    )
    spec_imag = (low_dot(dop_real, flat[1]) + low_dot(dop_imag, flat[0])).reshape(
        pulse_count, channels, cells
    )
    mix_real = jnp.einsum("fkc,fcb->kfb", channel_mix[0], spec_real, precision=HIGH) - jnp.einsum(
        "fkc,fcb->kfb", channel_mix[1], spec_imag, precision=HIGH
    )
    mix_imag = jnp.einsum("fkc,fcb->kfb", channel_mix[0], spec_imag, precision=HIGH) + jnp.einsum(
        "fkc,fcb->kfb", channel_mix[1], spec_real, precision=HIGH
    )
    recon = (
        jnp.stack([mix_real, mix_imag])
        .astype(jnp.bfloat16)
        .reshape(2, channels * pulse_count, cells)
    )
    image_real = low_dot(beam_real, recon[0]) - low_dot(beam_imag, recon[1])
    image_imag = low_dot(beam_real, recon[1]) + low_dot(beam_imag, recon[0])
    return jnp.stack([image_real, image_imag])


def band_matrix(offsets, weights, count):
    band_width = weights.shape[-1]
    columns = jnp.arange(count, dtype=jnp.int32)
    stepping = jnp.arange(band_width, dtype=jnp.int32)
    target = offsets[:, None, None] + stepping[None, :, None]
    hitting = (columns[None, None, :] == target).astype(jnp.float32)
    return jnp.einsum("crkj,kja->crka", weights, hitting, precision=HIGH)


def complex_apply(matrices, field):
    real_part = jnp.dot(matrices[0], field[0], precision=HIGH) - jnp.dot(
        matrices[1], field[1], precision=HIGH
    )
    imag_part = jnp.dot(matrices[0], field[1], precision=HIGH) + jnp.dot(
        matrices[1], field[0], precision=HIGH
    )
    return jnp.stack([real_part, imag_part])


def merge_child(image, offsets_level, weights_level, upper, merge_level):
    own_offsets = lax.dynamic_slice_in_dim(offsets_level, upper * ANG, ANG, 0)
    own_weights = lax.dynamic_slice_in_dim(weights_level, upper * ANG, ANG, 2)
    own_band = band_matrix(own_offsets, own_weights, ANG)
    partner = partner_2(image, SUB, merge_level)
    first_child = jnp.where(upper == 0, image, partner)
    second_child = jnp.where(upper == 0, partner, image)
    return complex_apply(own_band[0], first_child) + complex_apply(own_band[1], second_child)


def local(
    raw_pulses, range_filter, channel_mix, steer_angles, band_offsets, band_weights, smoothing
):
    pulse_count = raw_pulses.shape[1]
    local_channels = raw_pulses.shape[2]
    sample_count = raw_pulses.shape[3]
    all_channels = channel_mix.shape[2]
    echo_rows = raw_pulses.reshape(2, pulse_count * local_channels, sample_count)
    summed = range_terms(echo_rows, spread_gather(range_filter, SUB_CHAN, 1))
    own_channel = summed.astype(jnp.bfloat16).reshape(
        2, pulse_count, local_channels, range_filter.shape[2]
    )
    compressed = lax.all_to_all(own_channel, "chan", split_axis=3, concat_axis=2, tiled=True)
    dop_real, dop_imag = doppler_table(pulse_count)
    beam_real, beam_imag = steer_table(steer_angles, all_channels * pulse_count)
    image = form_image(compressed, dop_real, dop_imag, channel_mix, beam_real, beam_imag)
    position = lax.axis_index(SUB)
    for merge_level in range(LEVELS):
        upper = position >> merge_level & 1
        image = merge_child(
            image, band_offsets[merge_level], band_weights[merge_level], upper, merge_level
        )
    power = image[0] * image[0] + image[1] * image[1]
    rate = smoothing[:, None]
    width_local = power.shape[1]
    padded = padded_2(power, (("chan", 1),), PASSES)
    first_cell = lax.axis_index("chan") * width_local - PASSES
    cell_index = first_cell + jnp.arange(width_local + 2 * PASSES, dtype=jnp.int32)
    inside = ((cell_index >= 0) & (cell_index < width_local * lax.axis_size("chan"))).astype(
        jnp.float32
    )
    current = padded
    for sweep in range(PASSES):
        middle = current[:, 1:-1]
        window = inside[sweep + 1 : inside.shape[0] - sweep - 1]
        current = (middle + rate * (current[:, :-2] - 2.0 * middle + current[:, 2:])) * window[
            None, :
        ]
    power = current
    return power


def solution(mesh):
    split = Mesh(
        mesh.devices.reshape(2, 4, 4, 2, mesh.shape["chan"]),
        ("sub_0", "sub_1", "sub_2", "sub_3", "chan"),
    )
    placed = (P(None, SUB, "chan", None), P(None, SUB_CHAN, None), P(), P(), P(), P(), P(SUB))
    return jax.shard_map(
        local, mesh=split, in_specs=placed, out_specs=P(SUB, "chan"), check_vma=False
    )
```

profile of v0, /device:TPU:1, one launch (start us, length us, event | category | flops | bytes accessed | tf_op | source)
XLA Modules:
  0.0 439.2 jit_solution(1204910239806027530)
XLA Ops:
  7.4 10.4 %all-gather.5 = bf16[8,1,1024]{2,1,0:T(2,128)(2,1)S(1)} all-gather(bf16[2,1,1024]{2,1,0:T(2,128)(2,1)S(1)} %get-tuple-element.42), channel_id=7, replica_groups=mesh['sub_0'=2,'sub_1'=4,'sub_2'=4,'sub_3'=2,'chan'=8] {'sub_2'}, dimensions={0}, use_global_device_ids=true | all-gather | bytes 20480 | tf_op jit(solution)/shard_map/all_gather | solution.py:32
  17.9 9.3 %all-gather.6 = bf16[16,2,1,1024]{3,1,2,0:T(2,128)(2,1)S(1)} all-gather(bf16[4,2,1,1024]{3,1,2,0:T(2,128)(2,1)S(1)} %bitcast.374), channel_id=8, replica_groups=mesh['sub_0'=2,'sub_1'=4,'sub_2'=4,'sub_3'=2,'chan'=8] {'sub_1'}, dimensions={0}, use_global_device_ids=true | all-gather | bytes 81920 | tf_op jit(solution)/shard_map/all_gather | solution.py:32
  27.3 16.2 %all-gather.7 = bf16[8,4,2,1,1024]{4,1,3,2,0:T(4,128)(2,1)} all-gather(bf16[4,4,2,1,1024]{4,1,3,2,0:T(4,128)(2,1)S(1)} %copy.118), channel_id=9, replica_groups=mesh['sub_0'=2,'sub_1'=4,'sub_2'=4,'sub_3'=2,'chan'=8] {'sub_0'}, dimensions={0}, use_global_device_ids=true | all-gather | bytes 196608 | tf_op jit(solution)/shard_map/all_gather | solution.py:32
  43.5 10.2 %all-gather = bf16[4,1,1024]{2,1,0:T(2,128)(2,1)S(1)} all-gather(bf16[2,1,1024]{2,1,0:T(2,128)(2,1)S(1)} %get-tuple-element.41), channel_id=2, replica_groups=mesh['sub_0'=2,'sub_1'=4,'sub_2'=4,'sub_3'=2,'chan'=8] {'sub_3'}, dimensions={0}, use_global_device_ids=true | all-gather | bytes 12288 | tf_op jit(solution)/shard_map/all_gather | solution.py:32
  53.8 9.0 %all-gather.1 = bf16[8,2,1,1024]{3,1,2,0:T(2,128)(2,1)S(1)} all-gather(bf16[2,2,1,1024]{3,1,2,0:T(2,128)(2,1)S(1)} %bitcast.376), channel_id=3, replica_groups=mesh['sub_0'=2,'sub_1'=4,'sub_2'=4,'sub_3'=2,'chan'=8] {'sub_2'}, dimensions={0}, use_global_device_ids=true | all-gather | bytes 40960 | tf_op jit(solution)/shard_map/all_gather | solution.py:32
  62.8 9.2 %all-gather.2 = bf16[16,2,2,1,1024]{4,2,3,1,0:T(2,128)(2,1)S(1)} all-gather(bf16[4,2,2,1,1024]{4,2,3,1,0:T(2,128)(2,1)S(1)} %bitcast.372), channel_id=4, replica_groups=mesh['sub_0'=2,'sub_1'=4,'sub_2'=4,'sub_3'=2,'chan'=8] {'sub_1'}, dimensions={0}, use_global_device_ids=true | all-gather | bytes 163840 | tf_op jit(solution)/shard_map/all_gather | solution.py:32
  72.1 18.1 %all-gather.3 = bf16[8,4,2,2,1,1024]{5,1,4,3,2,0:T(4,128)(2,1)} all-gather(bf16[4,4,2,2,1,1024]{5,1,4,3,2,0:T(4,128)(2,1)S(1)} %copy.113), channel_id=5, replica_groups=mesh['sub_0'=2,'sub_1'=4,'sub_2'=4,'sub_3'=2,'chan'=8] {'sub_0'}, dimensions={0}, use_global_device_ids=true | all-gather | bytes 393216 | tf_op jit(solution)/shard_map/all_gather | solution.py:32
  90.2 25.2 %all-gather.28.cloned.1.call-done = bf16[16,4,4,2,1,1024]{5,2,4,3,1,0:T(4,128)(2,1)} async-done(((bf16[2,4,4,2,1,1024]{5,2,4,3,1,0:T(4,128)(2,1)}), bf16[16,4,4,2,1,1024]{5,2,4,3,1,0:T(4,128)(2,1)}) %all-gather.28.cloned.1.call-update) | async-done | bytes 1048592 | tf_op jit(solution)/shard_map/all_gather | solution.py:32
  115.5 9.2 %all-gather.10 = bf16[8,1,1024]{2,1,0:T(2,128)(2,1)S(1)} all-gather(bf16[2,1,1024]{2,1,0:T(2,128)(2,1)S(1)} %get-tuple-element.44), channel_id=12, replica_groups=mesh['sub_0'=2,'sub_1'=4,'sub_2'=4,'sub_3'=2,'chan'=8] {'sub_1'}, dimensions={0}, use_global_device_ids=true | all-gather | bytes 20480 | tf_op jit(solution)/shard_map/all_gather | solution.py:32
  124.8 12.0 %all-gather.11 = bf16[8,2,1,1024]{3,1,2,0:T(2,128)(2,1)S(1)} all-gather(bf16[4,2,1,1024]{3,1,2,0:T(2,128)(2,1)S(1)} %bitcast.375), channel_id=13, replica_groups=mesh['sub_0'=2,'sub_1'=4,'sub_2'=4,'sub_3'=2,'chan'=8] {'sub_0'}, dimensions={0}, use_global_device_ids=true | all-gather | bytes 49152 | tf_op jit(solution)/shard_map/all_gather | solution.py:32
  136.8 43.7 %all-gather.12 = bf16[16,4,2,1,1024]{4,1,3,2,0:T(4,128)(2,1)S(1)} all-gather(bf16[2,4,2,1,1024]{4,1,3,2,0:T(4,128)(2,1)S(1)} %copy.124), channel_id=14, replica_groups=mesh['sub_0'=2,'sub_1'=4,'sub_2'=4,'sub_3'=2,'chan'=8] {'chan'}, dimensions={0}, use_global_device_ids=true | all-gather | bytes 294912 | tf_op jit(solution)/shard_map/all_gather | solution.py:32
  180.5 15.5 %all-gather.13 = bf16[16,2,4,2,1,1024]{5,2,4,3,1,0:T(4,128)(2,1)S(1)} all-gather(bf16[8,2,4,2,1,1024]{5,2,4,3,1,0:T(4,128)(2,1)S(1)} %bitcast.360), channel_id=15, replica_groups=mesh['sub_0'=2,'sub_1'=4,'sub_2'=4,'sub_3'=2,'chan'=8] {'sub_3'}, dimensions={0}, use_global_device_ids=true | all-gather | bytes 786432 | tf_op jit(solution)/shard_map/all_gather | solution.py:32
  197.1 11.9 %all-gather.15 = bf16[4,1,1024]{2,1,0:T(2,128)(2,1)S(1)} all-gather(bf16[2,1,1024]{2,1,0:T(2,128)(2,1)S(1)} %get-tuple-element.43), channel_id=17, replica_groups=mesh['sub_0'=2,'sub_1'=4,'sub_2'=4,'sub_3'=2,'chan'=8] {'sub_0'}, dimensions={0}, use_global_device_ids=true | all-gather | bytes 12288 | tf_op jit(solution)/shard_map/all_gather | solution.py:32
  209.1 39.8 %all-gather.16 = bf16[16,2,1,1024]{3,1,2,0:T(2,128)(2,1)S(1)} all-gather(bf16[2,2,1,1024]{3,1,2,0:T(2,128)(2,1)S(1)} %bitcast.377), channel_id=18, replica_groups=mesh['sub_0'=2,'sub_1'=4,'sub_2'=4,'sub_3'=2,'chan'=8] {'chan'}, dimensions={0}, use_global_device_ids=true | all-gather | bytes 73728 | tf_op jit(solution)/shard_map/all_gather | solution.py:32
  248.9 9.4 %all-gather.17 = bf16[16,2,2,1,1024]{4,2,3,1,0:T(2,128)(2,1)S(1)} all-gather(bf16[8,2,2,1,1024]{4,2,3,1,0:T(2,128)(2,1)S(1)} %bitcast.370), channel_id=19, replica_groups=mesh['sub_0'=2,'sub_1'=4,'sub_2'=4,'sub_3'=2,'chan'=8] {'sub_3'}, dimensions={0}, use_global_device_ids=true | all-gather | bytes 196608 | tf_op jit(solution)/shard_map/all_gather | solution.py:32
  258.4 11.6 %all-gather.18 = bf16[8,8,2,2,1,1024]{5,1,4,3,2,0:T(8,128)(2,1)S(1)} all-gather(bf16[2,8,2,2,1,1024]{5,1,4,3,2,0:T(8,128)(2,1)S(1)} %copy.129), channel_id=20, replica_groups=mesh['sub_0'=2,'sub_1'=4,'sub_2'=4,'sub_3'=2,'chan'=8] {'sub_2'}, dimensions={0}, use_global_device_ids=true | all-gather | bytes 655360 | tf_op jit(solution)/shard_map/all_gather | solution.py:32
  273.6 3.2 fusion.21
  282.0 3.8 copy.115
  287.1 4.2 copy.122
  291.2 14.6 %all-gather.34.cloned.1.call-done = bf16[16,2,8,2,2,1,1024]{6,2,1,0,3,4,5:T(8,128)(2,1)} async-done(((bf16[4,2,8,2,2,1,1024]{6,2,1,0,3,4,5:T(8,128)(2,1)}), bf16[16,2,8,2,2,1,1024]{6,2,1,0,3,4,5:T(8,128)(2,1)}) %all-gather.34.cloned.1.call-update) | async-done | bytes 2097168 | tf_op jit(solution)/shard_map/all_gather | solution.py:32
  305.8 3.8 maximum_bitcast_fusion
  312.2 5.3 %copy.131 = bf16[1,512,4,1024]{3,2,1,0:T(4,128)(2,1)} copy(bf16[1,512,4,1024]{3,1,0,2:T(8,128)(2,1)S(1)} %get-tuple-element.5) | data formatting | bytes 8388608 | tf_op jit(solution)/shard_map/slice | solution.py:96
  317.5 7.3 %squeeze.88 = bf16[2048,1024]{1,0:T(8,128)(2,1)} reshape(bf16[1,512,4,1024]{3,2,1,0:T(4,128)(2,1)} %copy.131) | data formatting | bytes 8388608 | tf_op jit(solution)/shard_map/squeeze | solution.py:96
  324.8 7.4 %copy.132 = bf16[1,512,4,1024]{3,2,1,0:T(4,128)(2,1)} copy(bf16[1,512,4,1024]{3,1,0,2:T(8,128)(2,1)} %get-tuple-element.6) | data formatting | bytes 8388608 | tf_op jit(solution)/shard_map/slice | solution.py:96
  332.2 7.0 %squeeze.90 = bf16[2048,1024]{1,0:T(8,128)(2,1)} reshape(bf16[1,512,4,1024]{3,2,1,0:T(4,128)(2,1)} %copy.132) | data formatting | bytes 8388608 | tf_op jit(solution)/shard_map/squeeze | solution.py:96
  347.2 9.7 %all-to-all-start = ((bf16[8,2,4096]{2,1,0:T(2,128)(2,1)}), bf16[8,2,4096]{2,1,0:T(2,128)(2,1)S(1)}, u32[]{:S(2)}, u32[]{:S(2)}) async-start(bf16[8,2,4096]{2,1,0:T(2,128)(2,1)} %reshape.281), calls=%async_computation | async-start | bytes 262144 | tf_op jit(solution)/shard_map/all_to_all | solution.py:169
  360.1 7.2 %all-to-all-done = bf16[8,2,4096]{2,1,0:T(2,128)(2,1)S(1)} async-done(((bf16[8,2,4096]{2,1,0:T(2,128)(2,1)}), bf16[8,2,4096]{2,1,0:T(2,128)(2,1)S(1)}, u32[]{:S(2)}, u32[]{:S(2)}) %all-to-all-start) | async-done | bytes 131104 | tf_op jit(solution)/shard_map/all_to_all | solution.py:169
  375.6 4.8 %collective-permute-start = (f32[2,256,128]{2,1,0:T(8,128)S(1)}, f32[2,256,128]{2,1,0:T(8,128)S(1)}, u32[]{:S(2)}, u32[]{:S(2)}) collective-permute-start(f32[2,256,128]{2,1,0:T(8,128)S(1)} %pad_maximum_fusion), channel_id=1, source_target_pairs={{0,8},{8,0},{16,24},{24,16},{32,40},{40,32},{48,56},{56,48},{64,72... | collective-permute-start | bytes 786440 | tf_op jit(solution)/shard_map/ppermute | solution.py:21
  390.1 5.9 %collective-permute-done.1 = f32[2,256,128]{2,1,0:T(8,128)S(1)} collective-permute-done((f32[2,256,128]{2,1,0:T(8,128)S(1)}, f32[2,256,128]{2,1,0:T(8,128)S(1)}, u32[]{:S(2)}, u32[]{:S(2)}) %collective-permute-start.1) | collective-permute-done | bytes 262176 | tf_op jit(solution)/shard_map/ppermute | solution.py:21
  399.1 4.8 %collective-permute-start.2 = (f32[2,256,128]{2,1,0:T(8,128)S(1)}, f32[2,256,128]{2,1,0:T(8,128)S(1)}, u32[]{:S(2)}, u32[]{:S(2)}) collective-permute-start(f32[2,256,128]{2,1,0:T(8,128)S(1)} %maximum_add_fusion.1), channel_id=1, source_target_pairs={{0,32},{8,40},{16,48},{24,56},{32,0},{40,8},{48,16},{56,24},{64,96... | collective-permute-start | bytes 786440 | tf_op jit(solution)/shard_map/ppermute | solution.py:21
  404.7 5.0 %collective-permute-done.2 = f32[2,256,128]{2,1,0:T(8,128)S(1)} collective-permute-done((f32[2,256,128]{2,1,0:T(8,128)S(1)}, f32[2,256,128]{2,1,0:T(8,128)S(1)}, u32[]{:S(2)}, u32[]{:S(2)}) %collective-permute-start.2) | collective-permute-done | bytes 262176 | tf_op jit(solution)/shard_map/ppermute | solution.py:21
  416.0 4.8 %collective-permute-done.3 = f32[2,256,128]{2,1,0:T(8,128)S(1)} collective-permute-done((f32[2,256,128]{2,1,0:T(8,128)S(1)}, f32[2,256,128]{2,1,0:T(8,128)S(1)}, u32[]{:S(2)}, u32[]{:S(2)}) %collective-permute-start.3) | collective-permute-done | bytes 262176 | tf_op jit(solution)/shard_map/ppermute | solution.py:21
  (163 shorter events, 65.8 us)
Async XLA Ops:
  6.5 108.9 %all-gather.28.cloned.1.call-start = ((), (), s32[]{:S(2)}) async-start(), calls=%async_computation.2 | async-start | bytes 1179648 | tf_op jit(solution)/shard_map/all_gather | solution.py:32
  27.3 243.7 %copy-start.7 = (f32[2,32,8,8]{1,3,2,0:T(8,128)S(1)}, f32[2,32,8,8]{1,3,2,0:T(8,128)}, u32[]{:S(2)}) copy-start(f32[2,32,8,8]{1,3,2,0:T(8,128)} %param.9) | copy-start | bytes 49156
  43.5 238.5 %all-gather.26.cloned.1.call-start = ((), (), s32[]{:S(2)}) async-start(), calls=%async_computation.1 | async-start | bytes 2359296 | tf_op jit(solution)/shard_map/all_gather | solution.py:32
  62.8 208.4 %copy-start.6 = (f32[4,2,2,512,8]{3,4,2,1,0:T(8,128)S(1)}, f32[4,2,2,512,8]{3,4,2,1,0:T(8,128)}, u32[]{:S(2)}) copy-start(f32[4,2,2,512,8]{3,4,2,1,0:T(8,128)} %param.12) | copy-start | bytes 786436
  90.2 196.9 %all-gather.30.cloned.1.call-start = ((), (), s32[]{:S(2)}) async-start(), calls=%async_computation.3 | async-start | bytes 3145728 | tf_op jit(solution)/shard_map/all_gather | solution.py:32
  115.4 175.8 %all-gather.32.cloned.1.call-start = ((), (), s32[]{:S(2)}) async-start(), calls=%async_computation.4 | async-start | bytes 2621440 | tf_op jit(solution)/shard_map/all_gather | solution.py:32
  195.9 77.3 %copy-start.9 = (s32[4,512]{1,0:T(4,128)S(1)}, s32[4,512]{1,0:T(4,128)}, u32[]{:S(2)}) copy-start(s32[4,512]{1,0:T(4,128)} %param.11) | copy-start | bytes 24580
  197.0 108.8 %all-gather.34.cloned.1.call-start = ((), (), s32[]{:S(2)}) async-start(), calls=%async_computation.5 | async-start | bytes 2621440 | tf_op jit(solution)/shard_map/all_gather | solution.py:32
  332.2 7.0 %copy-start.2 = (bf16[2,32,1,2048]{3,1,2,0:T(8,128)(2,1)S(1)}, bf16[2,32,1,2048]{3,1,2,0:T(8,128)(2,1)}, u32[]{:S(2)}) copy-start(bf16[2,32,1,2048]{3,1,2,0:T(8,128)(2,1)} %param.7) | copy-start | bytes 786436
  339.2 3.4 copy-start.1
  342.6 2.2 copy-start
  344.8 12.2 %copy-start.5 = (f32[1,2,2,256,8]{4,2,1,3,0:T(2,128)S(1)}, f32[1,2,2,256,8]{4,2,1,3,0:T(2,128)}, u32[]{:S(2)}) copy-start(f32[1,2,2,256,8]{4,2,1,3,0:T(2,128)} %copy.107) | copy-start | bytes 98308
  347.2 20.0 %all-to-all-start = ((bf16[8,2,4096]{2,1,0:T(2,128)(2,1)}), bf16[8,2,4096]{2,1,0:T(2,128)(2,1)S(1)}, u32[]{:S(2)}, u32[]{:S(2)}) async-start(bf16[8,2,4096]{2,1,0:T(2,128)(2,1)} %reshape.281), calls=%async_computation | async-start | bytes 262144 | tf_op jit(solution)/shard_map/all_to_all | solution.py:169
  360.1 11.2 %copy-start.10 = (f32[256]{0:T(256)S(1)}, f32[256]{0:T(256)}, u32[]{:S(2)}) copy-start(f32[256]{0:T(256)} %param.10) | copy-start | bytes 3076
  375.6 13.7 %copy-start.4 = (f32[2,2,256,256]{3,1,0,2:T(2,128)S(1)}, f32[2,2,256,256]{3,1,0,2:T(2,128)}, u32[]{:S(2)}) copy-start(f32[2,2,256,256]{3,1,0,2:T(2,128)} %fusion.18) | copy-start | bytes 3145732
  375.6 7.4 %collective-permute-start = (f32[2,256,128]{2,1,0:T(8,128)S(1)}, f32[2,256,128]{2,1,0:T(8,128)S(1)}, u32[]{:S(2)}, u32[]{:S(2)}) collective-permute-start(f32[2,256,128]{2,1,0:T(8,128)S(1)} %pad_maximum_fusion), channel_id=1, source_target_pairs={{0,8},{8,0},{16,24},{24,16},{32,40},{40,32},{48,56},{56,48},{64,72... | collective-permute-start | bytes 786440 | tf_op jit(solution)/shard_map/ppermute | solution.py:21
  386.2 9.8 %collective-permute-start.1 = (f32[2,256,128]{2,1,0:T(8,128)S(1)}, f32[2,256,128]{2,1,0:T(8,128)S(1)}, u32[]{:S(2)}, u32[]{:S(2)}) collective-permute-start(f32[2,256,128]{2,1,0:T(8,128)S(1)} %maximum_add_fusion), channel_id=1, source_target_pairs={{0,16},{8,24},{16,0},{24,8},{32,48},{40,56},{48,32},{56,40},{64,80... | collective-permute-start | bytes 786440 | tf_op jit(solution)/shard_map/ppermute | solution.py:21
  399.1 16.1 %copy-start.3 = (f32[2,2,256,256]{3,1,0,2:T(2,128)S(1)}, f32[2,2,256,256]{3,1,0,2:T(2,128)}, u32[]{:S(2)}) copy-start(f32[2,2,256,256]{3,1,0,2:T(2,128)} %fusion.12) | copy-start | bytes 3145732
  399.1 10.6 %collective-permute-start.2 = (f32[2,256,128]{2,1,0:T(8,128)S(1)}, f32[2,256,128]{2,1,0:T(8,128)S(1)}, u32[]{:S(2)}, u32[]{:S(2)}) collective-permute-start(f32[2,256,128]{2,1,0:T(8,128)S(1)} %maximum_add_fusion.1), channel_id=1, source_target_pairs={{0,32},{8,40},{16,48},{24,56},{32,0},{40,8},{48,16},{56,24},{64,96... | collective-permute-start | bytes 786440 | tf_op jit(solution)/shard_map/ppermute | solution.py:21
  412.9 8.0 %collective-permute-start.3 = (f32[2,256,128]{2,1,0:T(8,128)S(1)}, f32[2,256,128]{2,1,0:T(8,128)S(1)}, u32[]{:S(2)}, u32[]{:S(2)}) collective-permute-start(f32[2,256,128]{2,1,0:T(8,128)S(1)} %maximum_add_fusion.2), channel_id=1, source_target_pairs={{0,64},{8,72},{16,80},{24,88},{32,96},{40,104},{48,112},{56,120},{... | collective-permute-start | bytes 786440 | tf_op jit(solution)/shard_map/ppermute | solution.py:21
  416.0 15.4 %copy-start.8 = (f32[256]{0:T(256)S(1)}, f32[256]{0:T(256)}, u32[]{:S(2)}) copy-start(f32[256]{0:T(256)} %param.13) | copy-start | bytes 3076
  424.2 4.4 collective-permute-start.4
  427.0 4.4 collective-permute-start.5
Sparse Core Ops, SparseCore 0:
  43.6 71.7 all-gather.27
  117.5 68.9 all-gather.25
  188.6 23.0 all-gather.29
  213.7 38.4 all-gather.31
  271.0 34.7 all-gather.33
where the time goes:
time: 446 us; the launch traced here: 439 us
  blocking collectives  235 us (53%)
  waiting for transfers between devices  65.5 us (15%)
  local copies, waits for them, and re-layouts  54 us (12%)
  matrix products  35.8 us (8%)
  starting transfers between devices  29 us (7%)
  between operations  14.2 us (3%)
  other arithmetic  5.17 us (1%)
    all_gather x15, blocking collectives, all_blocks(): pieces = lax.all_gather(pieces, axes[k])  235 us
    all_gather x5, waiting for transfers between devices, all_blocks(): pieces = lax.all_gather(pieces, axes[k])  39.8 us
    ppermute x4, waiting for transfers between devices, partner_2(): return lax.ppermute(value, axis, pairs)  15.6 us
    ppermute x4, starting transfers between devices, partner_2(): return lax.ppermute(value, axis, pairs)  15 us
    dot_general x4, matrix products, band_matrix(): return jnp.einsum('crkj,kja->crka', weights, hitting, precision=HIGH)  11.4 us
    dot_general x12, matrix products, low_dot(): return jnp.dot(left, right, preferred_element_type=jnp.float32)  10.8 us
    all_gather x12, local copies, waits for them, and re-layouts, all_blocks(): pieces = lax.all_gather(pieces, axes[k])  10.1 us
    all_to_all x1, starting transfers between devices, local(): lax.all_to_all(own_channel, 'chan', split_axis=3, concat_axis=2, tiled=True)  9.7 us
  transfers between devices with their start and end apart: 12, of which 7 were waited for; matrix products, arithmetic and copies ran while one was open for 7% of the time, Pallas kernels for 0%

commit v1 on v0

v1 whole, which is shorter than its diff:
```python
import functools

import jax
import jax.numpy as jnp
import ml_dtypes
import numpy as np
from jax import lax
from jax.experimental import pallas as pl
from jax.experimental.pallas import tpu as pltpu
from jax.sharding import Mesh
from jax.sharding import PartitionSpec as P

ANG = 256
BAND = 8
LEVELS = 4
PASSES = 3
PULSES = 32
CHAN = 8
GROUP = 16
ROW = 8
CUT = 9
PAD = 16
HALO = 8
COLS = GROUP * CUT
AXES = ("zh", "x1", "x0", "y", "core", "chan")
SUB = ("zh", "x1", "x0", "y", "core")
ALONG_Z = ("zh", "chan")
PLANE = ("x1", "x0", "y", "core")
MERGE = ("x0", "y", "core")
BF = jnp.bfloat16
F32 = jnp.float32
WHOLE = pl.BlockSpec(memory_space=pltpu.VMEM)
SCALAR = pl.BlockSpec(memory_space=pltpu.SMEM)


def params(mib):
    return pltpu.CompilerParams(vmem_limit_bytes=mib << 20)


def iota(shape, dim):
    return lax.broadcasted_iota(jnp.int32, shape, dim)


def dot(left, right):
    return jnp.dot(left, right, preferred_element_type=F32)


def dot_t(left, right):
    return lax.dot_general(left, right, (((1,), (1,)), ((), ())), preferred_element_type=F32)


def raw_body(raw_ref, out_ref):
    row, col = iota((512, 512), 0), iota((512, 512), 1)
    quarter, part, half, k = col >> 7, (col >> 6) & 1, (col >> 5) & 1, col & 31
    source = part * 256 + half * 128 + quarter * 32 + k
    sign = jnp.where(part == 1, -1.0, 1.0)
    order = jnp.where(row == source, sign, 0.0).astype(BF)
    rows = []
    for u in range(8):
        rows.append(
            jnp.concatenate(
                [
                    raw_ref[part, :, half * 1024 + u * 128 : half * 1024 + (u + 1) * 128]
                    for part in range(2)
                    for half in range(2)
                ],
                axis=1,
            )
        )
    moved = dot(jnp.concatenate(rows, axis=0), order).astype(BF)
    for u in range(8):
        out_ref[:, u * 512 : (u + 1) * 512] = moved[u * 32 : (u + 1) * 32]


def pick_body(filter_ref, out_ref):
    i, k = iota((128, 128), 0), iota((128, 128), 1)
    source = (((i >> 5) & 1) * 8 + ((i >> 2) & 7)) * 8 + (i >> 6) * 4 + (i & 3)
    rows = dot(jnp.where(k == source, 1.0, 0.0).astype(BF), filter_ref[...]).astype(BF)
    bins = iota((COLS, 1024), 1)
    r = iota((COLS, 1024), 0)
    dest = r // CUT
    first = 128 * (dest & 7) - HALO + 8 * CUT * (dest >> 3) + r - dest * CUT
    for g in range(ROW):
        pick = jnp.where(bins == first + CUT * g, 1.0, 0.0).astype(BF)
        block = dot_t(pick, rows).astype(BF)
        for x in range(4):
            out_ref[x, g] = block


def compress_body(filter_ref, own_ref, other_ref, out_ref):
    first, second = [], []
    for s in range(32):
        block = filter_ref[s]
        first.append(block)
        second.append(jnp.concatenate([block[:, 64:], -block[:, :64]], axis=1))
    left = jnp.concatenate(
        [jnp.concatenate(first, axis=1), jnp.concatenate(second, axis=1)], axis=0
    )
    summed = jnp.concatenate([dot_t(left, own_ref[...]), dot_t(left, other_ref[...])], axis=1)
    row, col = iota((2 * COLS, 2 * COLS), 0), iota((2 * COLS, 2 * COLS), 1)
    dest = row // (2 * CUT)
    within = row - dest * (2 * CUT)
    source = dest * CUT + jnp.where(within >= CUT, within - CUT + COLS, within)
    order = jnp.where(col == source, 1.0, 0.0).astype(BF)
    out_ref[...] = dot(order, summed.astype(BF)).astype(BF)


def operator_body(mix_ref, dop_ref, beam_ref, high_ref, low_ref):
    real, imag = [], []
    for c in range(CHAN):
        mr, mi = mix_ref[0, c : c + 1, :], mix_ref[1, c : c + 1, :]
        real.append(mr * dop_ref[0] - mi * dop_ref[1])
        imag.append(mr * dop_ref[1] + mi * dop_ref[0])
    both = jnp.concatenate(real + imag, axis=0)
    top = both.astype(BF)
    rest = (both - top.astype(F32)).astype(BF)
    by_real = dot(top, beam_ref[0]) + dot(rest, beam_ref[0])
    by_imag = dot(top, beam_ref[1]) + dot(rest, beam_ref[1])
    whole = jnp.concatenate(
        [by_real[:256] - by_imag[256:], by_real[256:] + by_imag[:256]], axis=1
    )
    top = whole.astype(BF)
    high_ref[...] = top
    low_ref[...] = (whole - top.astype(F32)).astype(BF)


def band_body(offset_ref, weight_ref, out_ref):
    strip = 32
    offset = jnp.broadcast_to(offset_ref[0], (strip, ANG))
    for start in range(0, ANG, strip):
        step = iota((strip, ANG), 0) + start - offset
        hits = [step == j for j in range(BAND)]
        for c in range(2):
            for part in range(2):
                value = jnp.zeros((strip, ANG), F32)
                for j in range(BAND):
                    value = jnp.where(hits[j], weight_ref[0, c, part, j : j + 1, :], value)
                out_ref[
                    0, c * ANG + start : c * ANG + start + strip, part * ANG : (part + 1) * ANG
                ] = value.astype(BF)


def merge_body(me_ref, comp_ref, high_ref, low_ref, band_ref, out_ref, pulses):
    me = me_ref[0]
    row, col = iota((512, 2 * COLS), 0), iota((512, 2 * COLS), 1)
    j = row & 15
    source = (row >> 5) * (2 * CUT) + ((row >> 4) & 1) * CUT + j
    order = jnp.where((col == source) & (j < CUT), 1.0, 0.0).astype(BF)
    apart = dot(order, comp_ref[...])
    for x in range(2):
        for part in range(2):
            blocks = []
            for c in range(CHAN):
                at = ((x * 8 + c) * 2 + part) * PAD
                blocks.append(apart[at : at + PAD])
            for q in range(8):
                n = x * 8 + (((q & 3) * 2 + (q >> 2)) ^ me)
                pulses[part, n] = jnp.concatenate(
                    [b[:, q * 32 : (q + 1) * 32] for b in blocks], axis=1
                )
    pulse = pulses[...].reshape(2 * GROUP * PAD, 256).astype(BF)
    formed = dot(pulse, high_ref[...]) + dot(pulse, low_ref[...])
    half = GROUP * PAD
    real = formed[:half, :ANG] - formed[half:, ANG:]
    imag = formed[half:, :ANG] + formed[:half, ANG:]
    for level in range(LEVELS):
        inner = 1 << level
        outer = GROUP // (2 * inner)
        real = real.reshape(outer, 2, inner * PAD, ANG)
        imag = imag.reshape(outer, 2, inner * PAD, ANG)
        sides = [
            jnp.concatenate(
                [real[:, c].reshape(half // 2, ANG), imag[:, c].reshape(half // 2, ANG)], axis=0
            )
            for c in range(2)
        ]
        left = jnp.concatenate(sides, axis=1)
        top = left.astype(BF)
        rest = (left - top.astype(F32)).astype(BF)
        reals, imags = [], []
        for h in range(2):
            band = band_ref[2 * level + h]
            out = dot(top, band) + dot(rest, band)
            r = out[: half // 2, :ANG] - out[half // 2 :, ANG:]
            i = out[half // 2 :, :ANG] + out[: half // 2, ANG:]
            reals.append(r.reshape(outer, 1, inner * PAD, ANG))
            imags.append(i.reshape(outer, 1, inner * PAD, ANG))
        real = jnp.concatenate(reals, axis=1)
        imag = jnp.concatenate(imags, axis=1)
    real = real.reshape(GROUP, PAD, ANG)
    imag = imag.reshape(GROUP, PAD, ANG)
    power = real * real + imag * imag
    out_ref[...] = power[:, :CUT, :]


def despeckle_body(chan_ref, power_ref, rate_ref, out_ref, bins):
    for t in range(GROUP):
        bins[t * CUT : (t + 1) * CUT, :] = power_ref[t]
    current = bins[...]
    cell = iota((COLS, ANG), 0) + (chan_ref[0] * 128 - HALO)
    inside = (cell >= 0) & (cell < 1024)
    rate = jnp.broadcast_to(rate_ref[...], (COLS, ANG))
    for _ in range(PASSES):
        before = pltpu.roll(current, 1, 0)
        after = pltpu.roll(current, COLS - 1, 0)
        current = jnp.where(inside, current + rate * (before - 2.0 * current + after), 0.0)
    out_ref[...] = current[HALO : HALO + 128, :].T


def doppler_table():
    index = np.arange(PULSES)
    phase = np.float32(2.0 * np.pi / PULSES) * (
        index[:, None] * index[None, :] % PULSES
    ).astype(np.float32)
    factor = np.float32(1.0 / np.sqrt(PULSES))
    parts = np.stack([np.cos(phase) * factor, -np.sin(phase) * factor])
    return parts.astype(ml_dtypes.bfloat16).astype(np.float32)


def flipped(value, axis, mask):
    pairs = [(source, source ^ mask) for source in range(lax.axis_size(axis))]
    return lax.ppermute(value, axis, pairs)


def exchange(value, axes):
    return lax.all_to_all(value, axes, split_axis=0, concat_axis=0, tiled=True)


def local(
    raw_pulses, range_filter, channel_mix, steer_angles, band_offsets, band_weights, smoothing
):
    raw = pl.pallas_call(
        raw_body,
        out_shape=jax.ShapeDtypeStruct((PULSES, 4096), BF),
        in_specs=[WHOLE],
        out_specs=WHOLE,
        name="raw_order",
    )(raw_pulses.reshape(2, PULSES, 2048))
    own = jnp.concatenate([raw] + [flipped(raw, "y", mask) for mask in (1, 2, 3)], axis=0)
    other = flipped(own, "core", 1)

    rows = range_filter.reshape(8, 1024)
    rows = exchange(jnp.broadcast_to(rows[None], (16, 8, 1024)), ALONG_Z).reshape(128, 1024)
    picked = pl.pallas_call(
        pick_body,
        out_shape=jax.ShapeDtypeStruct((4, ROW, COLS, 128), BF),
        in_specs=[WHOLE],
        out_specs=WHOLE,
        compiler_params=params(24),
        name="pick_bins",
    )(rows)
    filters = exchange(picked.reshape(32, COLS, 128), PLANE)

    offset = jnp.arange(ANG, dtype=jnp.int32).astype(F32) - 0.5 * ANG
    phase = steer_angles[None, :] * offset[:, None]
    factor = 1.0 / np.sqrt(ANG)
    beams = jnp.stack([jnp.cos(phase) * factor, jnp.sin(phase) * factor]).astype(BF)
    mix = channel_mix.transpose(0, 3, 2, 1).reshape(2, CHAN, 256)
    doppler = jnp.asarray(np.tile(doppler_table().transpose(0, 2, 1), (1, 1, CHAN)))
    high, low = pl.pallas_call(
        operator_body,
        out_shape=[jax.ShapeDtypeStruct((256, 2 * ANG), BF)] * 2,
        in_specs=[WHOLE] * 3,
        out_specs=[WHOLE] * 2,
        name="operator",
    )(mix, doppler, beams)
    weights = band_weights.reshape(LEVELS, 2, 2, 2, ANG, BAND).transpose(0, 3, 1, 2, 5, 4)
    band = pl.pallas_call(
        band_body,
        grid=(2 * LEVELS,),
        out_shape=jax.ShapeDtypeStruct((2 * LEVELS, 2 * ANG, 2 * ANG), BF),
        in_specs=[
            pl.BlockSpec((1, 1, ANG), lambda i: (i, 0, 0)),
            pl.BlockSpec((1, 2, 2, BAND, ANG), lambda i: (i, 0, 0, 0, 0)),
        ],
        out_specs=pl.BlockSpec((1, 2 * ANG, 2 * ANG), lambda i: (i, 0, 0)),
        name="band",
    )(
        band_offsets.reshape(2 * LEVELS, 1, ANG),
        weights.reshape(2 * LEVELS, 2, 2, BAND, ANG),
    )

    compressed = pl.pallas_call(
        compress_body,
        out_shape=jax.ShapeDtypeStruct((2 * COLS, 256), BF),
        in_specs=[WHOLE] * 3,
        out_specs=WHOLE,
        compiler_params=params(40),
        name="compress",
    )(filters, own, other)
    compressed = exchange(compressed.reshape(16, 2 * CUT, 256), ("x0", "chan"))
    me = (lax.axis_index("y") * 2 + lax.axis_index("core")).astype(jnp.int32).reshape(1)
    power = pl.pallas_call(
        merge_body,
        out_shape=jax.ShapeDtypeStruct((GROUP, CUT, ANG), F32),
        in_specs=[SCALAR] + [WHOLE] * 4,
        out_specs=WHOLE,
        scratch_shapes=[pltpu.VMEM((2, GROUP, PAD, 256), F32)],
        compiler_params=params(40),
        name="merge",
    )(me, compressed.reshape(2 * COLS, 256), high, low, band)
    power = exchange(power, MERGE)
    chan = lax.axis_index("chan").astype(jnp.int32).reshape(1)
    return pl.pallas_call(
        despeckle_body,
        out_shape=jax.ShapeDtypeStruct((ANG, 128), F32),
        in_specs=[SCALAR] + [WHOLE] * 2,
        out_specs=WHOLE,
        scratch_shapes=[pltpu.VMEM((COLS, ANG), F32)],
        name="despeckle",
    )(chan, power, smoothing.reshape(1, ANG))


def solution(mesh):
    split = Mesh(mesh.devices.reshape(2, 2, 2, 4, 2, mesh.shape["chan"]), AXES)
    placed = (
        P(None, SUB, "chan", None),
        P(None, AXES, None),
        P(),
        P(),
        P(),
        P(),
        P(SUB),
    )
    return jax.shard_map(
        local, mesh=split, in_specs=placed, out_specs=P(SUB, "chan"), check_vma=False
    )
```

time: 446 us -> 111 us (0.25); the launches traced: 439 us -> 110 us
  blocking collectives: 235 us -> 0 us
  local copies, waits for them, and re-layouts: 54 us -> 10 us
  waiting for transfers between devices: 65.5 us -> 25.4 us
  matrix products: 35.8 us -> 0 us
  starting transfers between devices: 29 us -> 51 us
  Pallas kernels: 0 us -> 21.3 us
  between operations: 14.2 us -> 0.17 us
    all_gather x15 -> x0, blocking collectives: 235 us -> none  [all_blocks(): pieces = lax.all_gather(pieces, axes[k])]
    all_gather x5 -> x0, waiting for transfers between devices: 39.8 us -> none  [all_blocks(): pieces = lax.all_gather(pieces, axes[k])]
    dot_general x52 -> x0, matrix products: 35.8 us -> none  [the longest x4 11.4 us: band_matrix(): return jnp.einsum('crkj,kja->crka', weights, hitting, precision=HIGH)]
    all_to_all x1 -> x4, starting transfers between devices: 9.7 us -> 39.5 us  [exchange(): return lax.all_to_all(value, axes, split_axis=0, concat_axis=0, tiled=True)]
    slice x16 -> x0, local copies, waits for them, and re-layouts: 22.2 us -> none  [the longest x2 7.8 us: range_terms(): filter_rows[0]]
    pallas_call x0 -> x7, Pallas kernels: none -> 21.3 us  [the longest x1 6.95 us: local(): pl.pallas_call(band_body, grid=(2 * LEVELS,), out_shape=jax.ShapeDtypeStr...]
    ppermute x6 -> x4, waiting for transfers between devices: 18.4 us -> 2.41 us  [flipped(): return lax.ppermute(value, axis, pairs)]
    all_to_all x1 -> x4, waiting for transfers between devices: 7.18 us -> 23 us  [exchange(): return lax.all_to_all(value, axes, split_axis=0, concat_axis=0, tiled=True)]
  transfers between devices with their start and end apart: 12 -> 8, of which waited for: 7 -> 5; matrix products, arithmetic and copies ran while one was open for 7% -> 5% of each run, Pallas kernels for 0% -> 12%
where the time goes in v1:
time: 111 us; the launch traced here: 110 us
  starting transfers between devices  51 us (46%)
  waiting for transfers between devices  25.4 us (23%)
  Pallas kernels  21.3 us (19%)
  local copies, waits for them, and re-layouts  10 us (9%)
  other arithmetic  1.98 us (2%)
    all_to_all x4, starting transfers between devices, exchange(): return lax.all_to_all(value, axes, split_axis=0, concat_axis=0, tiled=True)  39.5 us
    all_to_all x4, waiting for transfers between devices, exchange(): return lax.all_to_all(value, axes, split_axis=0, concat_axis=0, tiled=True)  23 us
    ppermute x4, starting transfers between devices, flipped(): return lax.ppermute(value, axis, pairs)  11.4 us
    pallas_call x1, Pallas kernels, local(): pl.pallas_call(band_body, grid=(2 * LEVELS,), out_shape=jax.ShapeDtypeStr...  6.95 us
    unnamed x16, local copies, waits for them, and re-layouts  4.8 us
    pallas_call x1, Pallas kernels, local(): pl.pallas_call(merge_body, out_shape=jax.ShapeDtypeStruct((GROUP, CUT, AN...  4.6 us
    ppermute x4, waiting for transfers between devices, flipped(): return lax.ppermute(value, axis, pairs)  2.41 us
    pallas_call x1, Pallas kernels, local(): pl.pallas_call(operator_body, out_shape=[jax.ShapeDtypeStruct((256, 2 * A...  2.27 us
  transfers between devices with their start and end apart: 8, of which 5 were waited for; matrix products, arithmetic and copies ran while one was open for 5% of the time, Pallas kernels for 12%

profile of v1, /device:TPU:1, one launch (start us, length us, event | category | flops | bytes accessed | tf_op | source)
XLA Modules:
  0.0 109.9 jit_solution(17439998565409132016)
XLA Ops:
  0.0 0.7 broadcast_in_dim.4
  0.7 0.7 broadcast_in_dim.10
  1.5 15.7 %all-to-all-start = ((bf16[16,8,1024]{2,1,0:T(8,128)(2,1)}), bf16[16,8,1024]{2,1,0:T(8,128)(2,1)S(1)}, u32[]{:S(2)}, u32[]{:S(2)}) async-start(bf16[16,8,1024]{2,1,0:T(8,128)(2,1)} %broadcast_in_dim.10), calls=%async_computation | async-start | bytes 524288 | tf_op jit(solution)/shard_map/all_to_all | solution.py:226
  17.2 2.0 %raw_order.1 = bf16[32,4096]{1,0:T(8,128)(2,1)} custom-call(bf16[2,32,2048]{2,1,0:T(8,128)(2,1)} %bitcast.15), custom_call_target="tpu_custom_call" | custom-call | tf_op jit(solution)/shard_map/raw_order/pallas_call | solution.py:232
  19.2 4.8 %collective-permute-start.2 = (bf16[32,4096]{1,0:T(8,128)(2,1)}, bf16[32,4096]{1,0:T(8,128)(2,1)S(1)}, u32[]{:S(2)}, u32[]{:S(2)}) collective-permute-start(bf16[32,4096]{1,0:T(8,128)(2,1)} %raw_order.1), channel_id=1, source_target_pairs={{0,48},{16,32},{32,16},{48,0},{1,49},{17,33},{33,17},{49,1},{2,50}... | collective-permute-start | bytes 786440 | tf_op jit(solution)/shard_map/ppermute | solution.py:222
  23.9 2.3 %collective-permute-start.1 = (bf16[32,4096]{1,0:T(8,128)(2,1)}, bf16[32,4096]{1,0:T(8,128)(2,1)S(1)}, u32[]{:S(2)}, u32[]{:S(2)}) collective-permute-start(bf16[32,4096]{1,0:T(8,128)(2,1)} %raw_order.1), channel_id=1, source_target_pairs={{0,32},{16,48},{32,0},{48,16},{1,33},{17,49},{33,1},{49,17},{2,34}... | collective-permute-start | bytes 786440 | tf_op jit(solution)/shard_map/ppermute | solution.py:222
  26.2 2.1 %collective-permute-start = (bf16[32,4096]{1,0:T(8,128)(2,1)}, bf16[32,4096]{1,0:T(8,128)(2,1)S(1)}, u32[]{:S(2)}, u32[]{:S(2)}) collective-permute-start(bf16[32,4096]{1,0:T(8,128)(2,1)} %raw_order.1), channel_id=1, source_target_pairs={{0,16},{16,0},{32,48},{48,32},{1,17},{17,1},{33,49},{49,33},{2,18}... | collective-permute-start | bytes 786440 | tf_op jit(solution)/shard_map/ppermute | solution.py:222
  28.4 2.0 %all-to-all-done = bf16[16,8,1024]{2,1,0:T(8,128)(2,1)S(1)} async-done(((bf16[16,8,1024]{2,1,0:T(8,128)(2,1)}), bf16[16,8,1024]{2,1,0:T(8,128)(2,1)S(1)}, u32[]{:S(2)}, u32[]{:S(2)}) %all-to-all-start) | async-done | bytes 262176 | tf_op jit(solution)/shard_map/all_to_all | solution.py:226
  30.3 2.0 %pick_bins.1 = bf16[4,8,144,128]{3,2,1,0:T(8,128)(2,1)} custom-call(bf16[128,1024]{1,0:T(8,128)(2,1)S(1)} %bitcast.13), custom_call_target="tpu_custom_call" | custom-call | tf_op jit(solution)/shard_map/pick_bins/pallas_call | solution.py:244
  32.3 13.3 %all-to-all-start.1 = ((bf16[32,144,128]{2,1,0:T(8,128)(2,1)}), bf16[32,144,128]{2,1,0:T(8,128)(2,1)S(1)}, u32[]{:S(2)}, u32[]{:S(2)}) async-start(bf16[32,144,128]{2,1,0:T(8,128)(2,1)} %bitcast.3), calls=%async_computation.1 | async-start | bytes 2359296 | tf_op jit(solution)/shard_map/all_to_all | solution.py:226
  45.7 2.3 %collective-permute-start.3 = (bf16[128,4096]{1,0:T(8,128)(2,1)S(1)}, bf16[128,4096]{1,0:T(8,128)(2,1)S(1)}, u32[]{:S(2)}, u32[]{:S(2)}) collective-permute-start(bf16[128,4096]{1,0:T(8,128)(2,1)S(1)} %pad_maximum_fusion.own_ref), channel_id=1, source_target_pairs={{0,8},{8,0},{1,9},{9,1},{2,10},{10,2},{3,11},{11,3},{4,12},{12,4},... | collective-permute-start | bytes 3145736 | tf_op jit(solution)/shard_map/ppermute | solution.py:222
  48.0 2.4 %collective-permute-done.3.other_ref = bf16[128,4096]{1,0:T(8,128)(2,1)S(1)} collective-permute-done((bf16[128,4096]{1,0:T(8,128)(2,1)S(1)}, bf16[128,4096]{1,0:T(8,128)(2,1)S(1)}, u32[]{:S(2)}, u32[]{:S(2)}) %collective-permute-start.3) | collective-permute-done | bytes 1048608 | tf_op jit(solution)/shard_map/ppermute | solution.py:222
  50.4 13.5 %all-to-all-done.1.filter_ref = bf16[32,144,128]{2,1,0:T(8,128)(2,1)S(1)} async-done(((bf16[32,144,128]{2,1,0:T(8,128)(2,1)}), bf16[32,144,128]{2,1,0:T(8,128)(2,1)S(1)}, u32[]{:S(2)}, u32[]{:S(2)}) %all-to-all-start.1) | async-done | bytes 1179680 | tf_op jit(solution)/shard_map/all_to_all | solution.py:226
  63.9 1.7 %compress.1 = bf16[288,256]{1,0:T(8,128)(2,1)S(1)} custom-call(bf16[32,144,128]{2,1,0:T(8,128)(2,1)S(1)} %all-to-all-done.1.filter_ref, bf16[128,4096]{1,0:T(8,128)(2,1)S(1)} %pad_maximum_fusion.own_ref, bf16[128,4096]{1,0:T(8,128)(2,1)S(1)} %collective-permute-done.3.other_ref), custom_call_target="tpu_custom_call" | custom-call | tf_op jit(solution)/shard_map/compress/pallas_call | solution.py:283
  65.7 0.7 reshape.142
  66.4 5.5 %all-to-all-start.2 = ((bf16[16,18,256]{2,1,0:T(8,128)(2,1)}), bf16[16,18,256]{2,1,0:T(8,128)(2,1)S(1)}, u32[]{:S(2)}, u32[]{:S(2)}) async-start(bf16[16,18,256]{2,1,0:T(8,128)(2,1)} %reshape.142), calls=%async_computation.2 | async-start | bytes 393216 | tf_op jit(solution)/shard_map/all_to_all | solution.py:226
  71.9 0.6 reshape.145.offset_ref
  72.6 0.7 reshape.144.mix_ref
  73.2 1.7 %copy.12 = f32[4,2,2,2,256,8]{4,5,2,1,3,0:T(8,128)} copy(f32[4,2,2,2,256,8]{4,5,3,2,1,0:T(8,128)} %bitcast.16) | data formatting | bytes 524288 | tf_op jit(solution)/shard_map/reshape | solution.py:267
  74.9 6.9 %band.1.band_ref = bf16[8,512,512]{2,1,0:T(8,128)(2,1)} custom-call(s32[8,1,256]{2,1,0:T(1,128)} %reshape.145.offset_ref, f32[8,2,2,8,256]{4,3,2,1,0:T(8,128)} %bitcast.14), custom_call_target="tpu_custom_call" | custom-call | tf_op jit(solution)/shard_map/band/pallas_call | solution.py:268
  81.9 1.1 %fusion.1 = (bf16[1,256,256]{2,1,0:T(8,128)(2,1)S(1)}, bf16[1,256,256]{2,1,0:T(8,128)(2,1)S(1)}) fusion(f32[256]{0:T(256)S(1)} %convert_add_fusion, f32[256]{0:T(256)S(1)} %copy-done.7), kind=kLoop, calls=%fused_computation.4 | loop fusion | flops 327680 | bytes 264192 | tf_op jit(solution)/shard_map/convert
  83.1 0.7 pad_maximum_fusion.1.beam_ref
  83.8 2.3 %operator.1 = (bf16[256,512]{1,0:T(8,128)(2,1)}, bf16[256,512]{1,0:T(8,128)(2,1)}) custom-call(f32[2,8,256]{2,1,0:T(8,128)} %reshape.144.mix_ref, f32[2,32,256]{2,1,0:T(8,128)} %constant.23.clone.dop_ref, bf16[2,256,256]{2,1,0:T(8,128)(2,1)} %pad_maximum_fusion.1.beam_ref), custom_call_target="tpu_custom_call" | custom-call | tf_op jit(solution)/shard_map/operator/pallas_call | solution.py:260
  86.1 0.3 all-to-all-done.2
  86.4 2.2 %copy-done = bf16[8,512,512]{2,1,0:T(8,128)(2,1)S(1)} copy-done((bf16[8,512,512]{2,1,0:T(8,128)(2,1)S(1)}, bf16[8,512,512]{2,1,0:T(8,128)(2,1)}, u32[]{:S(2)}) %copy-start) | copy-done | bytes 4194328
  88.6 0.9 copy-done.1
  89.6 0.9 copy-done.2
  90.5 4.6 %merge.1 = f32[16,9,256]{2,1,0:T(8,128)} custom-call(s32[1]{0:T(128)} %bitcast.1.me_ref, bf16[288,256]{1,0:T(8,128)(2,1)S(1)} %reshape.143.comp_ref, bf16[256,512]{1,0:T(8,128)(2,1)S(1)} %copy-done.1, bf16[256,512]{1,0:T(8,128)(2,1)S(1)} %copy-done.2, bf16[8,512,512]{2,1,0:T(8,128)(2,1)S(1)} %copy-done), custom_call_target="tpu_custom_call" | custom-call | tf_op jit(solution)/shard_map/merge/pallas_call | solution.py:293
  95.1 5.0 %all-to-all-start.3 = ((f32[16,9,256]{2,1,0:T(8,128)}), f32[16,9,256]{2,1,0:T(8,128)S(1)}, u32[]{:S(2)}, u32[]{:S(2)}) async-start(f32[16,9,256]{2,1,0:T(8,128)} %merge.1), calls=%async_computation.3 | async-start | bytes 524288 | tf_op jit(solution)/shard_map/all_to_all | solution.py:226
  100.1 7.2 %all-to-all-done.3.power_ref = f32[16,9,256]{2,1,0:T(8,128)S(1)} async-done(((f32[16,9,256]{2,1,0:T(8,128)}), f32[16,9,256]{2,1,0:T(8,128)S(1)}, u32[]{:S(2)}, u32[]{:S(2)}) %all-to-all-start.3) | async-done | bytes 147488 | tf_op jit(solution)/shard_map/all_to_all | solution.py:226
  107.4 0.7 copy-done.3
  108.1 1.9 %despeckle.1 = f32[256,128]{1,0:T(8,128)} custom-call(s32[1]{0:T(128)} %bitcast.chan_ref, f32[16,9,256]{2,1,0:T(8,128)} %copy-done.3, f32[1,256]{1,0:T(1,128)} %bitcast.18), custom_call_target="tpu_custom_call" | custom-call | tf_op jit(solution)/shard_map/despeckle/pallas_call | solution.py:304
  (19 shorter events, 0.2 us)
Async XLA Ops:
  1.5 28.9 %all-to-all-start = ((bf16[16,8,1024]{2,1,0:T(8,128)(2,1)}), bf16[16,8,1024]{2,1,0:T(8,128)(2,1)S(1)}, u32[]{:S(2)}, u32[]{:S(2)}) async-start(bf16[16,8,1024]{2,1,0:T(8,128)(2,1)} %broadcast_in_dim.10), calls=%async_computation | async-start | bytes 524288 | tf_op jit(solution)/shard_map/all_to_all | solution.py:226
  19.2 26.4 %copy-start.4 = (bf16[32,4096]{1,0:T(8,128)(2,1)S(1)}, bf16[32,4096]{1,0:T(8,128)(2,1)}, u32[]{:S(2)}) copy-start(bf16[32,4096]{1,0:T(8,128)(2,1)} %raw_order.1) | copy-start | bytes 786436
  19.2 26.4 %collective-permute-start.2 = (bf16[32,4096]{1,0:T(8,128)(2,1)}, bf16[32,4096]{1,0:T(8,128)(2,1)S(1)}, u32[]{:S(2)}, u32[]{:S(2)}) collective-permute-start(bf16[32,4096]{1,0:T(8,128)(2,1)} %raw_order.1), channel_id=1, source_target_pairs={{0,48},{16,32},{32,16},{48,0},{1,49},{17,33},{33,17},{49,1},{2,50}... | collective-permute-start | bytes 786440 | tf_op jit(solution)/shard_map/ppermute | solution.py:222
  23.9 21.7 %collective-permute-start.1 = (bf16[32,4096]{1,0:T(8,128)(2,1)}, bf16[32,4096]{1,0:T(8,128)(2,1)S(1)}, u32[]{:S(2)}, u32[]{:S(2)}) collective-permute-start(bf16[32,4096]{1,0:T(8,128)(2,1)} %raw_order.1), channel_id=1, source_target_pairs={{0,32},{16,48},{32,0},{48,16},{1,33},{17,49},{33,1},{49,17},{2,34}... | collective-permute-start | bytes 786440 | tf_op jit(solution)/shard_map/ppermute | solution.py:222
  26.2 19.4 %collective-permute-start = (bf16[32,4096]{1,0:T(8,128)(2,1)}, bf16[32,4096]{1,0:T(8,128)(2,1)S(1)}, u32[]{:S(2)}, u32[]{:S(2)}) collective-permute-start(bf16[32,4096]{1,0:T(8,128)(2,1)} %raw_order.1), channel_id=1, source_target_pairs={{0,16},{16,0},{32,48},{48,32},{1,17},{17,1},{33,49},{49,33},{2,18}... | collective-permute-start | bytes 786440 | tf_op jit(solution)/shard_map/ppermute | solution.py:222
  32.3 31.6 %all-to-all-start.1 = ((bf16[32,144,128]{2,1,0:T(8,128)(2,1)}), bf16[32,144,128]{2,1,0:T(8,128)(2,1)S(1)}, u32[]{:S(2)}, u32[]{:S(2)}) async-start(bf16[32,144,128]{2,1,0:T(8,128)(2,1)} %bitcast.3), calls=%async_computation.1 | async-start | bytes 2359296 | tf_op jit(solution)/shard_map/all_to_all | solution.py:226
  45.7 26.2 %copy-start.6 = (s32[4,512]{1,0:T(4,128)S(1)}, s32[4,512]{1,0:T(4,128)}, u32[]{:S(2)}) copy-start(s32[4,512]{1,0:T(4,128)} %param.12) | copy-start | bytes 24580
  45.7 26.8 %copy-start.5 = (f32[2,32,8,8]{1,3,2,0:T(8,128)S(1)}, f32[2,32,8,8]{1,3,2,0:T(8,128)}, u32[]{:S(2)}) copy-start(f32[2,32,8,8]{1,3,2,0:T(8,128)} %param.10) | copy-start | bytes 49156
  45.7 4.7 %collective-permute-start.3 = (bf16[128,4096]{1,0:T(8,128)(2,1)S(1)}, bf16[128,4096]{1,0:T(8,128)(2,1)S(1)}, u32[]{:S(2)}, u32[]{:S(2)}) collective-permute-start(bf16[128,4096]{1,0:T(8,128)(2,1)S(1)} %pad_maximum_fusion.own_ref), channel_id=1, source_target_pairs={{0,8},{8,0},{1,9},{9,1},{2,10},{10,2},{3,11},{11,3},{4,12},{12,4},... | collective-permute-start | bytes 3145736 | tf_op jit(solution)/shard_map/ppermute | solution.py:222
  66.4 20.0 %all-to-all-start.2 = ((bf16[16,18,256]{2,1,0:T(8,128)(2,1)}), bf16[16,18,256]{2,1,0:T(8,128)(2,1)S(1)}, u32[]{:S(2)}, u32[]{:S(2)}) async-start(bf16[16,18,256]{2,1,0:T(8,128)(2,1)} %reshape.142), calls=%async_computation.2 | async-start | bytes 393216 | tf_op jit(solution)/shard_map/all_to_all | solution.py:226
  74.9 7.0 %copy-start.7 = (f32[256]{0:T(256)S(1)}, f32[256]{0:T(256)}, u32[]{:S(2)}) copy-start(f32[256]{0:T(256)} %param.11) | copy-start | bytes 3076
  86.4 2.2 %copy-start = (bf16[8,512,512]{2,1,0:T(8,128)(2,1)S(1)}, bf16[8,512,512]{2,1,0:T(8,128)(2,1)}, u32[]{:S(2)}) copy-start(bf16[8,512,512]{2,1,0:T(8,128)(2,1)} %band.1.band_ref) | copy-start | bytes 12582916
  88.6 0.9 copy-start.1
  89.6 0.9 copy-start.2
  95.1 12.3 %all-to-all-start.3 = ((f32[16,9,256]{2,1,0:T(8,128)}), f32[16,9,256]{2,1,0:T(8,128)S(1)}, u32[]{:S(2)}, u32[]{:S(2)}) async-start(f32[16,9,256]{2,1,0:T(8,128)} %merge.1), calls=%async_computation.3 | async-start | bytes 524288 | tf_op jit(solution)/shard_map/all_to_all | solution.py:226
  107.4 0.7 copy-start.3

commit v2 on v1

--- a/solution.py
+++ b/solution.py
@@ -30,6 +30,7 @@
 BF = jnp.bfloat16
 F32 = jnp.float32
 WHOLE = pl.BlockSpec(memory_space=pltpu.VMEM)
+LEFT = pl.BlockSpec(memory_space=pltpu.HBM)
 SCALAR = pl.BlockSpec(memory_space=pltpu.SMEM)
 
 
@@ -72,6 +73,13 @@
         out_ref[:, u * 512 : (u + 1) * 512] = moved[u * 32 : (u + 1) * 32]
 
 
+def copies_body(filter_ref, out_ref):
+    rows = filter_ref[...].astype(F32)
+    rows = jnp.concatenate([rows[0], rows[1]], axis=0).astype(BF)
+    for z in range(16):
+        out_ref[z] = rows
+
+
 def pick_body(filter_ref, out_ref):
     i, k = iota((128, 128), 0), iota((128, 128), 1)
     source = (((i >> 5) & 1) * 8 + ((i >> 2) & 7)) * 8 + (i >> 6) * 4 + (i & 3)
@@ -97,15 +105,16 @@
         [jnp.concatenate(first, axis=1), jnp.concatenate(second, axis=1)], axis=0
     )
     summed = jnp.concatenate([dot_t(left, own_ref[...]), dot_t(left, other_ref[...])], axis=1)
-    row, col = iota((2 * COLS, 2 * COLS), 0), iota((2 * COLS, 2 * COLS), 1)
-    dest = row // (2 * CUT)
-    within = row - dest * (2 * CUT)
-    source = dest * CUT + jnp.where(within >= CUT, within - CUT + COLS, within)
+    row, col = iota((32 * GROUP, 2 * COLS), 0), iota((32 * GROUP, 2 * COLS), 1)
+    within = row & 31
+    source = (row >> 5) * CUT + jnp.where(within >= CUT, within - CUT + COLS, within)
     order = jnp.where(col == source, 1.0, 0.0).astype(BF)
-    out_ref[...] = dot(order, summed.astype(BF)).astype(BF)
-
-
-def operator_body(mix_ref, dop_ref, beam_ref, high_ref, low_ref):
+    moved = dot(order, summed.astype(BF)).astype(BF)
+    for dest in range(GROUP):
+        out_ref[dest] = moved[dest * 32 : dest * 32 + 2 * CUT]
+
+
+def operator_body(mix_ref, dop_ref, beam_ref, out_ref):
     real, imag = [], []
     for c in range(CHAN):
         mr, mi = mix_ref[0, c : c + 1, :], mix_ref[1, c : c + 1, :]
@@ -120,8 +129,8 @@
         [by_real[:256] - by_imag[256:], by_real[256:] + by_imag[:256]], axis=1
     )
     top = whole.astype(BF)
-    high_ref[...] = top
-    low_ref[...] = (whole - top.astype(F32)).astype(BF)
+    out_ref[0] = top
+    out_ref[1] = (whole - top.astype(F32)).astype(BF)
 
 
 def band_body(offset_ref, weight_ref, out_ref):
@@ -140,7 +149,15 @@
                 ] = value.astype(BF)
 
 
-def merge_body(me_ref, comp_ref, high_ref, low_ref, band_ref, out_ref, pulses):
+def merge_body(me_ref, comp_ref, operator_far, band_far, out_ref, pulses, operator, band, sems):
+    copies = [pltpu.make_async_copy(operator_far, operator, sems.at[0])]
+    for level in range(LEVELS):
+        span = slice(2 * level, 2 * level + 2)
+        copies.append(
+            pltpu.make_async_copy(band_far.at[span], band.at[span], sems.at[1 + level])
+        )
+    for copy in copies:
+        copy.start()
     me = me_ref[0]
     row, col = iota((512, 2 * COLS), 0), iota((512, 2 * COLS), 1)
     j = row & 15
@@ -159,7 +176,8 @@
                     [b[:, q * 32 : (q + 1) * 32] for b in blocks], axis=1
                 )
     pulse = pulses[...].reshape(2 * GROUP * PAD, 256).astype(BF)
-    formed = dot(pulse, high_ref[...]) + dot(pulse, low_ref[...])
+    copies[0].wait()
+    formed = dot(pulse, operator[0]) + dot(pulse, operator[1])
     half = GROUP * PAD
     real = formed[:half, :ANG] - formed[half:, ANG:]
     imag = formed[half:, :ANG] + formed[:half, ANG:]
@@ -178,9 +196,10 @@
         top = left.astype(BF)
         rest = (left - top.astype(F32)).astype(BF)
         reals, imags = [], []
+        copies[1 + level].wait()
         for h in range(2):
-            band = band_ref[2 * level + h]
-            out = dot(top, band) + dot(rest, band)
+            weight = band[2 * level + h]
+            out = dot(top, weight) + dot(rest, weight)
             r = out[: half // 2, :ANG] - out[half // 2 :, ANG:]
             i = out[half // 2 :, :ANG] + out[: half // 2, ANG:]
             reals.append(r.reshape(outer, 1, inner * PAD, ANG))
@@ -234,19 +253,27 @@
         out_shape=jax.ShapeDtypeStruct((PULSES, 4096), BF),
         in_specs=[WHOLE],
         out_specs=WHOLE,
+        compiler_params=params(8),
         name="raw_order",
     )(raw_pulses.reshape(2, PULSES, 2048))
     own = jnp.concatenate([raw] + [flipped(raw, "y", mask) for mask in (1, 2, 3)], axis=0)
     other = flipped(own, "core", 1)
 
-    rows = range_filter.reshape(8, 1024)
-    rows = exchange(jnp.broadcast_to(rows[None], (16, 8, 1024)), ALONG_Z).reshape(128, 1024)
+    rows = pl.pallas_call(
+        copies_body,
+        out_shape=jax.ShapeDtypeStruct((16, 8, 1024), BF),
+        in_specs=[WHOLE],
+        out_specs=WHOLE,
+        compiler_params=params(2),
+        name="copies",
+    )(range_filter)
+    rows = exchange(rows, ALONG_Z).reshape(128, 1024)
     picked = pl.pallas_call(
         pick_body,
         out_shape=jax.ShapeDtypeStruct((4, ROW, COLS, 128), BF),
         in_specs=[WHOLE],
         out_specs=WHOLE,
-        compiler_params=params(24),
+        compiler_params=params(8),
         name="pick_bins",
     )(rows)
     filters = exchange(picked.reshape(32, COLS, 128), PLANE)
@@ -257,11 +284,12 @@
     beams = jnp.stack([jnp.cos(phase) * factor, jnp.sin(phase) * factor]).astype(BF)
     mix = channel_mix.transpose(0, 3, 2, 1).reshape(2, CHAN, 256)
     doppler = jnp.asarray(np.tile(doppler_table().transpose(0, 2, 1), (1, 1, CHAN)))
-    high, low = pl.pallas_call(
+    operator = pl.pallas_call(
         operator_body,
-        out_shape=[jax.ShapeDtypeStruct((256, 2 * ANG), BF)] * 2,
+        out_shape=jax.ShapeDtypeStruct((2, 256, 2 * ANG), BF),
         in_specs=[WHOLE] * 3,
-        out_specs=[WHOLE] * 2,
+        out_specs=WHOLE,
+        compiler_params=params(8),
         name="operator",
     )(mix, doppler, beams)
     weights = band_weights.reshape(LEVELS, 2, 2, 2, ANG, BAND).transpose(0, 3, 1, 2, 5, 4)
@@ -274,31 +302,38 @@
             pl.BlockSpec((1, 2, 2, BAND, ANG), lambda i: (i, 0, 0, 0, 0)),
         ],
         out_specs=pl.BlockSpec((1, 2 * ANG, 2 * ANG), lambda i: (i, 0, 0)),
+        compiler_params=params(4),
         name="band",
     )(
         band_offsets.reshape(2 * LEVELS, 1, ANG),
         weights.reshape(2 * LEVELS, 2, 2, BAND, ANG),
     )
 
+    filters, operator, band = lax.optimization_barrier((filters, operator, band))
     compressed = pl.pallas_call(
         compress_body,
-        out_shape=jax.ShapeDtypeStruct((2 * COLS, 256), BF),
+        out_shape=jax.ShapeDtypeStruct((GROUP, 2 * CUT, 256), BF),
         in_specs=[WHOLE] * 3,
         out_specs=WHOLE,
-        compiler_params=params(40),
+        compiler_params=params(16),
         name="compress",
     )(filters, own, other)
-    compressed = exchange(compressed.reshape(16, 2 * CUT, 256), ("x0", "chan"))
+    compressed = exchange(compressed, ("x0", "chan"))
     me = (lax.axis_index("y") * 2 + lax.axis_index("core")).astype(jnp.int32).reshape(1)
     power = pl.pallas_call(
         merge_body,
         out_shape=jax.ShapeDtypeStruct((GROUP, CUT, ANG), F32),
-        in_specs=[SCALAR] + [WHOLE] * 4,
-        out_specs=WHOLE,
-        scratch_shapes=[pltpu.VMEM((2, GROUP, PAD, 256), F32)],
-        compiler_params=params(40),
+        in_specs=[SCALAR, WHOLE, LEFT, LEFT],
+        out_specs=WHOLE,
+        scratch_shapes=[
+            pltpu.VMEM((2, GROUP, PAD, 256), F32),
+            pltpu.VMEM((2, 256, 2 * ANG), BF),
+            pltpu.VMEM((2 * LEVELS, 2 * ANG, 2 * ANG), BF),
+            pltpu.SemaphoreType.DMA((1 + LEVELS,)),
+        ],
+        compiler_params=params(58),
         name="merge",
-    )(me, compressed.reshape(2 * COLS, 256), high, low, band)
+    )(me, compressed.reshape(2 * COLS, 256), operator, band)
     power = exchange(power, MERGE)
     chan = lax.axis_index("chan").astype(jnp.int32).reshape(1)
     return pl.pallas_call(
@@ -307,6 +342,7 @@
         in_specs=[SCALAR] + [WHOLE] * 2,
         out_specs=WHOLE,
         scratch_shapes=[pltpu.VMEM((COLS, ANG), F32)],
+        compiler_params=params(4),
         name="despeckle",
     )(chan, power, smoothing.reshape(1, ANG))
 

time: 111 us -> 108 us (0.973)
  waiting for transfers between devices: 25.4 us -> 30.6 us
  local copies, waits for them, and re-layouts: 10 us -> 6.21 us
  Pallas kernels: 21.3 us -> 18.1 us
    all_to_all x4, waiting for transfers between devices: 23 us -> 30.5 us  [exchange(): return lax.all_to_all(value, axes, split_axis=0, concat_axis=0, tiled=True)]
    pallas_call x1, Pallas kernels: 6.95 us -> 4.45 us  [local(): pl.pallas_call(band_body, grid=(2 * LEVELS,), out_shape=jax.ShapeDtypeStr...]
    ppermute x4, waiting for transfers between devices: 2.41 us -> 0.01 us  [flipped(): return lax.ppermute(value, axis, pairs)]
    pallas_call x1, Pallas kernels: 4.6 us -> 6.85 us  [local(): pl.pallas_call(merge_body, out_shape=jax.ShapeDtypeStruct((GROUP, CUT, AN...]
    pallas_call x1, Pallas kernels: 1.97 us -> 0.32 us  [local(): pl.pallas_call(raw_body, out_shape=jax.ShapeDtypeStruct((PULSES, 4096), B...]
    broadcast_in_dim x2 -> x0, local copies, waits for them, and re-layouts: 1.45 us -> none  [local(): jnp.broadcast_to(rows[None], (16, 8, 1024))]
    pallas_call x2 -> x3, Pallas kernels: 3.98 us -> 3.54 us  [the longest x1 2.35 us: local(): pl.pallas_call(compress_body, out_shape=jax.ShapeDtypeStruct((GROUP, 2 *...]
    unnamed x16 -> x18, local copies, waits for them, and re-layouts: 4.8 us -> 4.42 us
  transfers between devices with their start and end apart: 8 -> 8, of which waited for: 5 -> 4; matrix products, arithmetic and copies ran while one was open for 5% -> 2% of each run, Pallas kernels for 12% -> 7%
where the time goes in v2:
time: 108 us; the launch traced here: 107 us
  starting transfers between devices  50.9 us (47%)
  waiting for transfers between devices  30.6 us (28%)
  Pallas kernels  18.1 us (17%)
  local copies, waits for them, and re-layouts  6.21 us (6%)
  other arithmetic  1.25 us (1%)
    all_to_all x4, starting transfers between devices, exchange(): return lax.all_to_all(value, axes, split_axis=0, concat_axis=0, tiled=True)  39.7 us
    all_to_all x4, waiting for transfers between devices, exchange(): return lax.all_to_all(value, axes, split_axis=0, concat_axis=0, tiled=True)  30.5 us
    ppermute x4, starting transfers between devices, flipped(): return lax.ppermute(value, axis, pairs)  11.2 us
    pallas_call x1, Pallas kernels, local(): pl.pallas_call(merge_body, out_shape=jax.ShapeDtypeStruct((GROUP, CUT, AN...  6.85 us
    pallas_call x1, Pallas kernels, local(): pl.pallas_call(band_body, grid=(2 * LEVELS,), out_shape=jax.ShapeDtypeStr...  4.45 us
    unnamed x18, local copies, waits for them, and re-layouts  4.42 us
    pallas_call x1, Pallas kernels, local(): pl.pallas_call(compress_body, out_shape=jax.ShapeDtypeStruct((GROUP, 2 *...  2.35 us
  transfers between devices with their start and end apart: 8, of which 4 were waited for; matrix products, arithmetic and copies ran while one was open for 2% of the time, Pallas kernels for 7%

profile of v2, /device:TPU:1, one launch (start us, length us, event | category | flops | bytes accessed | tf_op | source)
XLA Modules:
  0.0 107.2 jit_solution(10633474930862191606)
XLA Ops:
  0.0 0.7 copy-done.4
  0.7 0.7 copies.1
  1.4 15.7 %all-to-all-start = ((bf16[16,8,1024]{2,1,0:T(8,128)(2,1)}), bf16[16,8,1024]{2,1,0:T(8,128)(2,1)S(1)}, u32[]{:S(2)}, u32[]{:S(2)}) async-start(bf16[16,8,1024]{2,1,0:T(8,128)(2,1)} %copies.1), calls=%async_computation | async-start | bytes 524288 | tf_op jit(solution)/shard_map/all_to_all | solution.py:245
  17.2 0.0 copy-start.2
  17.2 0.9 copy-done.2
  18.1 0.3 raw_order.1
  18.5 4.6 %collective-permute-start.2 = (bf16[32,4096]{1,0:T(8,128)(2,1)S(1)}, bf16[32,4096]{1,0:T(8,128)(2,1)S(1)}, u32[]{:S(2)}, u32[]{:S(2)}) collective-permute-start(bf16[32,4096]{1,0:T(8,128)(2,1)S(1)} %raw_order.1), channel_id=1, source_target_pairs={{0,48},{16,32},{32,16},{48,0},{1,49},{17,33},{33,17},{49,1},{2,50}... | collective-permute-start | bytes 786440 | tf_op jit(solution)/shard_map/ppermute | solution.py:241
  23.1 2.3 %collective-permute-start.1 = (bf16[32,4096]{1,0:T(8,128)(2,1)S(1)}, bf16[32,4096]{1,0:T(8,128)(2,1)S(1)}, u32[]{:S(2)}, u32[]{:S(2)}) collective-permute-start(bf16[32,4096]{1,0:T(8,128)(2,1)S(1)} %raw_order.1), channel_id=1, source_target_pairs={{0,32},{16,48},{32,0},{48,16},{1,33},{17,49},{33,1},{49,17},{2,34}... | collective-permute-start | bytes 786440 | tf_op jit(solution)/shard_map/ppermute | solution.py:241
  25.4 2.1 %collective-permute-start = (bf16[32,4096]{1,0:T(8,128)(2,1)S(1)}, bf16[32,4096]{1,0:T(8,128)(2,1)S(1)}, u32[]{:S(2)}, u32[]{:S(2)}) collective-permute-start(bf16[32,4096]{1,0:T(8,128)(2,1)S(1)} %raw_order.1), channel_id=1, source_target_pairs={{0,16},{16,0},{32,48},{48,32},{1,17},{17,1},{33,49},{49,33},{2,18}... | collective-permute-start | bytes 786440 | tf_op jit(solution)/shard_map/ppermute | solution.py:241
  27.5 2.8 %all-to-all-done = bf16[16,8,1024]{2,1,0:T(8,128)(2,1)S(1)} async-done(((bf16[16,8,1024]{2,1,0:T(8,128)(2,1)}), bf16[16,8,1024]{2,1,0:T(8,128)(2,1)S(1)}, u32[]{:S(2)}, u32[]{:S(2)}) %all-to-all-start) | async-done | bytes 262176 | tf_op jit(solution)/shard_map/all_to_all | solution.py:245
  30.3 2.0 %pick_bins.1 = bf16[4,8,144,128]{3,2,1,0:T(8,128)(2,1)} custom-call(bf16[128,1024]{1,0:T(8,128)(2,1)S(1)} %bitcast.14), custom_call_target="tpu_custom_call" | custom-call | tf_op jit(solution)/shard_map/pick_bins/pallas_call | solution.py:271
  32.3 13.4 %all-to-all-start.1 = ((bf16[32,144,128]{2,1,0:T(8,128)(2,1)}), bf16[32,144,128]{2,1,0:T(8,128)(2,1)S(1)}, u32[]{:S(2)}, u32[]{:S(2)}) async-start(bf16[32,144,128]{2,1,0:T(8,128)(2,1)} %bitcast.3), calls=%async_computation.1 | async-start | bytes 2359296 | tf_op jit(solution)/shard_map/all_to_all | solution.py:245
  45.7 0.1 pad_maximum_fusion.own_ref
  45.8 2.1 %collective-permute-start.3 = (bf16[128,4096]{1,0:T(8,128)(2,1)S(1)}, bf16[128,4096]{1,0:T(8,128)(2,1)S(1)}, u32[]{:S(2)}, u32[]{:S(2)}) collective-permute-start(bf16[128,4096]{1,0:T(8,128)(2,1)S(1)} %pad_maximum_fusion.own_ref), channel_id=1, source_target_pairs={{0,8},{8,0},{1,9},{9,1},{2,10},{10,2},{3,11},{11,3},{4,12},{12,4},... | collective-permute-start | bytes 3145736 | tf_op jit(solution)/shard_map/ppermute | solution.py:241
  48.0 0.1 reshape.137.mix_ref
  48.1 1.0 copy.12
  49.1 0.0 copy-start.8
  49.1 0.0 copy-start.3
  49.2 4.4 %band.1.band_far = bf16[8,512,512]{2,1,0:T(8,128)(2,1)S(1)} custom-call(s32[8,1,256]{2,1,0:T(1,128)S(1)} %reshape.138.offset_ref, f32[8,2,2,8,256]{4,3,2,1,0:T(8,128)S(1)} %bitcast.13), custom_call_target="tpu_custom_call" | custom-call | tf_op jit(solution)/shard_map/band/pallas_call | solution.py:296
  53.6 1.9 %copy-done = bf16[8,512,512]{2,1,0:T(8,128)(2,1)} copy-done((bf16[8,512,512]{2,1,0:T(8,128)(2,1)}, bf16[8,512,512]{2,1,0:T(8,128)(2,1)S(1)}, u32[]{:S(2)}) %copy-start) | copy-done | bytes 4194328
  55.6 1.1 %fusion.1 = (bf16[1,256,256]{2,1,0:T(8,128)(2,1)S(1)}, bf16[1,256,256]{2,1,0:T(8,128)(2,1)S(1)}) fusion(f32[256]{0:T(256)S(1)} %convert_add_fusion, f32[256]{0:T(256)S(1)} %copy-done.8), kind=kLoop, calls=%fused_computation.4 | loop fusion | flops 327680 | bytes 264192 | tf_op jit(solution)/shard_map/convert
  56.7 0.5 operator.1.operator_far
  57.2 0.8 copy-done.1
  58.0 6.1 %all-to-all-done.1.filter_ref = bf16[32,144,128]{2,1,0:T(8,128)(2,1)S(1)} async-done(((bf16[32,144,128]{2,1,0:T(8,128)(2,1)}), bf16[32,144,128]{2,1,0:T(8,128)(2,1)S(1)}, u32[]{:S(2)}, u32[]{:S(2)}) %all-to-all-start.1) | async-done | bytes 1179680 | tf_op jit(solution)/shard_map/all_to_all | solution.py:245
  64.1 2.4 %compress.1 = bf16[16,18,256]{2,1,0:T(8,128)(2,1)} custom-call(bf16[32,144,128]{2,1,0:T(8,128)(2,1)S(1)} %all-to-all-done.1.filter_ref, bf16[128,4096]{1,0:T(8,128)(2,1)S(1)} %pad_maximum_fusion.own_ref, bf16[128,4096]{1,0:T(8,128)(2,1)S(1)} %collective-permute-done.3.other_ref), custom_call_target="tpu_custom_call" | custom-call | tf_op jit(solution)/shard_map/compress/pallas_call | solution.py:313
  66.4 5.5 %all-to-all-start.2 = ((bf16[16,18,256]{2,1,0:T(8,128)(2,1)}), bf16[16,18,256]{2,1,0:T(8,128)(2,1)S(1)}, u32[]{:S(2)}, u32[]{:S(2)}) async-start(bf16[16,18,256]{2,1,0:T(8,128)(2,1)} %compress.1), calls=%async_computation.2 | async-start | bytes 393216 | tf_op jit(solution)/shard_map/all_to_all | solution.py:245
  72.0 14.5 %all-to-all-done.2 = bf16[16,18,256]{2,1,0:T(8,128)(2,1)S(1)} async-done(((bf16[16,18,256]{2,1,0:T(8,128)(2,1)}), bf16[16,18,256]{2,1,0:T(8,128)(2,1)S(1)}, u32[]{:S(2)}, u32[]{:S(2)}) %all-to-all-start.2) | async-done | bytes 147488 | tf_op jit(solution)/shard_map/all_to_all | solution.py:245
  86.4 0.7 reshape.142.comp_ref
  87.1 6.9 %merge.1 = f32[16,9,256]{2,1,0:T(8,128)} custom-call(s32[1]{0:T(128)} %bitcast.1.me_ref, bf16[288,256]{1,0:T(8,128)(2,1)} %reshape.142.comp_ref, bf16[2,256,512]{2,1,0:T(8,128)(2,1)} %copy-done.1, bf16[8,512,512]{2,1,0:T(8,128)(2,1)} %copy-done), custom_call_target="tpu_custom_call" | custom-call | tf_op jit(solution)/shard_map/merge/pallas_call | solution.py:323
  94.0 5.0 %all-to-all-start.3 = ((f32[16,9,256]{2,1,0:T(8,128)}), f32[16,9,256]{2,1,0:T(8,128)S(1)}, u32[]{:S(2)}, u32[]{:S(2)}) async-start(f32[16,9,256]{2,1,0:T(8,128)} %merge.1), calls=%async_computation.3 | async-start | bytes 524288 | tf_op jit(solution)/shard_map/all_to_all | solution.py:245
  99.0 7.2 %all-to-all-done.3.power_ref = f32[16,9,256]{2,1,0:T(8,128)S(1)} async-done(((f32[16,9,256]{2,1,0:T(8,128)}), f32[16,9,256]{2,1,0:T(8,128)S(1)}, u32[]{:S(2)}, u32[]{:S(2)}) %all-to-all-start.3) | async-done | bytes 147488 | tf_op jit(solution)/shard_map/all_to_all | solution.py:245
  106.2 0.9 despeckle.1
  (19 shorter events, 0.1 us)
Async XLA Ops:
  0.0 0.7 copy-start.4
  1.4 28.9 %all-to-all-start = ((bf16[16,8,1024]{2,1,0:T(8,128)(2,1)}), bf16[16,8,1024]{2,1,0:T(8,128)(2,1)S(1)}, u32[]{:S(2)}, u32[]{:S(2)}) async-start(bf16[16,8,1024]{2,1,0:T(8,128)(2,1)} %copies.1), calls=%async_computation | async-start | bytes 524288 | tf_op jit(solution)/shard_map/all_to_all | solution.py:245
  17.2 1.0 copy-start.2
  18.5 27.2 %collective-permute-start.2 = (bf16[32,4096]{1,0:T(8,128)(2,1)S(1)}, bf16[32,4096]{1,0:T(8,128)(2,1)S(1)}, u32[]{:S(2)}, u32[]{:S(2)}) collective-permute-start(bf16[32,4096]{1,0:T(8,128)(2,1)S(1)} %raw_order.1), channel_id=1, source_target_pairs={{0,48},{16,32},{32,16},{48,0},{1,49},{17,33},{33,17},{49,1},{2,50}... | collective-permute-start | bytes 786440 | tf_op jit(solution)/shard_map/ppermute | solution.py:241
  23.1 22.6 %collective-permute-start.1 = (bf16[32,4096]{1,0:T(8,128)(2,1)S(1)}, bf16[32,4096]{1,0:T(8,128)(2,1)S(1)}, u32[]{:S(2)}, u32[]{:S(2)}) collective-permute-start(bf16[32,4096]{1,0:T(8,128)(2,1)S(1)} %raw_order.1), channel_id=1, source_target_pairs={{0,32},{16,48},{32,0},{48,16},{1,33},{17,49},{33,1},{49,17},{2,34}... | collective-permute-start | bytes 786440 | tf_op jit(solution)/shard_map/ppermute | solution.py:241
  25.4 20.4 %collective-permute-start = (bf16[32,4096]{1,0:T(8,128)(2,1)S(1)}, bf16[32,4096]{1,0:T(8,128)(2,1)S(1)}, u32[]{:S(2)}, u32[]{:S(2)}) collective-permute-start(bf16[32,4096]{1,0:T(8,128)(2,1)S(1)} %raw_order.1), channel_id=1, source_target_pairs={{0,16},{16,0},{32,48},{48,32},{1,17},{17,1},{33,49},{49,33},{2,18}... | collective-permute-start | bytes 786440 | tf_op jit(solution)/shard_map/ppermute | solution.py:241
  32.3 15.7 %copy-start.6 = (f32[2,32,8,8]{1,3,2,0:T(8,128)S(1)}, f32[2,32,8,8]{1,3,2,0:T(8,128)}, u32[]{:S(2)}) copy-start(f32[2,32,8,8]{1,3,2,0:T(8,128)} %param.10) | copy-start | bytes 49156
  32.3 15.8 %copy-start.7 = (s32[4,512]{1,0:T(4,128)S(1)}, s32[4,512]{1,0:T(4,128)}, u32[]{:S(2)}) copy-start(s32[4,512]{1,0:T(4,128)} %param.12) | copy-start | bytes 24580
  32.3 31.8 %all-to-all-start.1 = ((bf16[32,144,128]{2,1,0:T(8,128)(2,1)}), bf16[32,144,128]{2,1,0:T(8,128)(2,1)S(1)}, u32[]{:S(2)}, u32[]{:S(2)}) async-start(bf16[32,144,128]{2,1,0:T(8,128)(2,1)} %bitcast.3), calls=%async_computation.1 | async-start | bytes 2359296 | tf_op jit(solution)/shard_map/all_to_all | solution.py:245
  45.8 18.2 %collective-permute-start.3 = (bf16[128,4096]{1,0:T(8,128)(2,1)S(1)}, bf16[128,4096]{1,0:T(8,128)(2,1)S(1)}, u32[]{:S(2)}, u32[]{:S(2)}) collective-permute-start(bf16[128,4096]{1,0:T(8,128)(2,1)S(1)} %pad_maximum_fusion.own_ref), channel_id=1, source_target_pairs={{0,8},{8,0},{1,9},{9,1},{2,10},{10,2},{3,11},{11,3},{4,12},{12,4},... | collective-permute-start | bytes 3145736 | tf_op jit(solution)/shard_map/ppermute | solution.py:241
  49.1 6.4 %copy-start.8 = (f32[256]{0:T(256)S(1)}, f32[256]{0:T(256)}, u32[]{:S(2)}) copy-start(f32[256]{0:T(256)} %param.11) | copy-start | bytes 3076
  49.1 7.6 %copy-start.3 = (f32[2,32,256]{2,1,0:T(8,128)S(1)}, f32[2,32,256]{2,1,0:T(8,128)}, u32[]{:S(2)}) copy-start(f32[2,32,256]{2,1,0:T(8,128)} %constant.23.clone.dop_ref) | copy-start | bytes 196612
  53.6 1.9 %copy-start = (bf16[8,512,512]{2,1,0:T(8,128)(2,1)}, bf16[8,512,512]{2,1,0:T(8,128)(2,1)S(1)}, u32[]{:S(2)}) copy-start(bf16[8,512,512]{2,1,0:T(8,128)(2,1)S(1)} %band.1.band_far) | copy-start | bytes 12582916
  57.2 0.8 copy-start.1
  66.4 20.0 %all-to-all-start.2 = ((bf16[16,18,256]{2,1,0:T(8,128)(2,1)}), bf16[16,18,256]{2,1,0:T(8,128)(2,1)S(1)}, u32[]{:S(2)}, u32[]{:S(2)}) async-start(bf16[16,18,256]{2,1,0:T(8,128)(2,1)} %compress.1), calls=%async_computation.2 | async-start | bytes 393216 | tf_op jit(solution)/shard_map/all_to_all | solution.py:245
  87.1 19.1 %copy-start.5 = (f32[256]{0:T(256)S(1)}, f32[256]{0:T(256)}, u32[]{:S(2)}) copy-start(f32[256]{0:T(256)} %param.14) | copy-start | bytes 3076
  94.0 12.3 %all-to-all-start.3 = ((f32[16,9,256]{2,1,0:T(8,128)}), f32[16,9,256]{2,1,0:T(8,128)S(1)}, u32[]{:S(2)}, u32[]{:S(2)}) async-start(f32[16,9,256]{2,1,0:T(8,128)} %merge.1), calls=%async_computation.3 | async-start | bytes 524288 | tf_op jit(solution)/shard_map/all_to_all | solution.py:245

commit v3 on v2

--- a/solution.py
+++ b/solution.py
@@ -20,8 +20,10 @@
 ROW = 8
 CUT = 9
 PAD = 16
+SENT = 24
 HALO = 8
 COLS = GROUP * CUT
+REVERSED = [8 * (m & 1) + 4 * (m >> 1 & 1) + 2 * (m >> 2 & 1) + (m >> 3) for m in range(GROUP)]
 AXES = ("zh", "x1", "x0", "y", "core", "chan")
 SUB = ("zh", "x1", "x0", "y", "core")
 ALONG_Z = ("zh", "chan")
@@ -95,7 +97,9 @@
             out_ref[x, g] = block
 
 
-def compress_body(filter_ref, own_ref, other_ref, out_ref):
+def compress_body(filter_ref, own_ref, other_ref, out_ref, pulses):
+    pulses[:128, :] = own_ref[...]
+    pulses[128:, :] = other_ref[...]
     first, second = [], []
     for s in range(32):
         block = filter_ref[s]
@@ -104,14 +108,14 @@
     left = jnp.concatenate(
         [jnp.concatenate(first, axis=1), jnp.concatenate(second, axis=1)], axis=0
     )
-    summed = jnp.concatenate([dot_t(left, own_ref[...]), dot_t(left, other_ref[...])], axis=1)
+    summed = dot_t(left, pulses[...])
     row, col = iota((32 * GROUP, 2 * COLS), 0), iota((32 * GROUP, 2 * COLS), 1)
     within = row & 31
     source = (row >> 5) * CUT + jnp.where(within >= CUT, within - CUT + COLS, within)
-    order = jnp.where(col == source, 1.0, 0.0).astype(BF)
+    order = jnp.where((col == source) & (within < 2 * CUT), 1.0, 0.0).astype(BF)
     moved = dot(order, summed.astype(BF)).astype(BF)
     for dest in range(GROUP):
-        out_ref[dest] = moved[dest * 32 : dest * 32 + 2 * CUT]
+        out_ref[dest] = moved[dest * 32 : dest * 32 + SENT]
 
 
 def operator_body(mix_ref, dop_ref, beam_ref, out_ref):
@@ -149,19 +153,17 @@
                 ] = value.astype(BF)
 
 
-def merge_body(me_ref, comp_ref, operator_far, band_far, out_ref, pulses, operator, band, sems):
-    copies = [pltpu.make_async_copy(operator_far, operator, sems.at[0])]
+def merge_body(me_ref, comp_ref, operator_ref, band_far, out_ref, pulses, band, sems):
+    copies = []
     for level in range(LEVELS):
         span = slice(2 * level, 2 * level + 2)
-        copies.append(
-            pltpu.make_async_copy(band_far.at[span], band.at[span], sems.at[1 + level])
-        )
+        copies.append(pltpu.make_async_copy(band_far.at[span], band.at[span], sems.at[level]))
     for copy in copies:
         copy.start()
     me = me_ref[0]
-    row, col = iota((512, 2 * COLS), 0), iota((512, 2 * COLS), 1)
+    row, col = iota((512, SENT * GROUP), 0), iota((512, SENT * GROUP), 1)
     j = row & 15
-    source = (row >> 5) * (2 * CUT) + ((row >> 4) & 1) * CUT + j
+    source = (row >> 5) * SENT + ((row >> 4) & 1) * CUT + j
     order = jnp.where((col == source) & (j < CUT), 1.0, 0.0).astype(BF)
     apart = dot(order, comp_ref[...])
     for x in range(2):
@@ -176,45 +178,46 @@
                     [b[:, q * 32 : (q + 1) * 32] for b in blocks], axis=1
                 )
     pulse = pulses[...].reshape(2 * GROUP * PAD, 256).astype(BF)
-    copies[0].wait()
-    formed = dot(pulse, operator[0]) + dot(pulse, operator[1])
+    formed = dot(pulse, operator_ref[0]) + dot(pulse, operator_ref[1])
     half = GROUP * PAD
     real = formed[:half, :ANG] - formed[half:, ANG:]
     imag = formed[half:, :ANG] + formed[:half, ANG:]
+    real, imag = [
+        jnp.concatenate([part[n * PAD : n * PAD + CUT] for n in REVERSED], axis=0)
+        for part in (real, imag)
+    ]
+    half = COLS // 2
     for level in range(LEVELS):
-        inner = 1 << level
-        outer = GROUP // (2 * inner)
-        real = real.reshape(outer, 2, inner * PAD, ANG)
-        imag = imag.reshape(outer, 2, inner * PAD, ANG)
-        sides = [
-            jnp.concatenate(
-                [real[:, c].reshape(half // 2, ANG), imag[:, c].reshape(half // 2, ANG)], axis=0
+        block = COLS >> level
+        sides = []
+        for c in range(2):
+            starts = [k * block + c * (block // 2) for k in range(1 << level)]
+            sides.append(
+                jnp.concatenate(
+                    [part[at : at + block // 2] for part in (real, imag) for at in starts], axis=0
+                )
             )
-            for c in range(2)
-        ]
         left = jnp.concatenate(sides, axis=1)
         top = left.astype(BF)
         rest = (left - top.astype(F32)).astype(BF)
         reals, imags = [], []
-        copies[1 + level].wait()
+        copies[level].wait()
         for h in range(2):
             weight = band[2 * level + h]
             out = dot(top, weight) + dot(rest, weight)
-            r = out[: half // 2, :ANG] - out[half // 2 :, ANG:]
-            i = out[half // 2 :, :ANG] + out[: half // 2, ANG:]
-            reals.append(r.reshape(outer, 1, inner * PAD, ANG))
-            imags.append(i.reshape(outer, 1, inner * PAD, ANG))
-        real = jnp.concatenate(reals, axis=1)
-        imag = jnp.concatenate(imags, axis=1)
-    real = real.reshape(GROUP, PAD, ANG)
-    imag = imag.reshape(GROUP, PAD, ANG)
+            reals.append(out[:half, :ANG] - out[half:, ANG:])
+            imags.append(out[half:, :ANG] + out[:half, ANG:])
+        real = jnp.concatenate(reals, axis=0)
+        imag = jnp.concatenate(imags, axis=0)
     power = real * real + imag * imag
-    out_ref[...] = power[:, :CUT, :]
+    rest = jnp.zeros((PAD - CUT, ANG), F32)
+    for n in range(GROUP):
+        out_ref[n] = jnp.concatenate([power[n * CUT : (n + 1) * CUT], rest], axis=0).astype(BF)
 
 
 def despeckle_body(chan_ref, power_ref, rate_ref, out_ref, bins):
     for t in range(GROUP):
-        bins[t * CUT : (t + 1) * CUT, :] = power_ref[t]
+        bins[t * CUT : (t + 1) * CUT, :] = power_ref[t].astype(F32)[:CUT]
     current = bins[...]
     cell = iota((COLS, ANG), 0) + (chan_ref[0] * 128 - HALO)
     inside = (cell >= 0) & (cell < 1024)
@@ -312,9 +315,10 @@
     filters, operator, band = lax.optimization_barrier((filters, operator, band))
     compressed = pl.pallas_call(
         compress_body,
-        out_shape=jax.ShapeDtypeStruct((GROUP, 2 * CUT, 256), BF),
+        out_shape=jax.ShapeDtypeStruct((GROUP, SENT, 256), BF),
         in_specs=[WHOLE] * 3,
         out_specs=WHOLE,
+        scratch_shapes=[pltpu.VMEM((256, 4096), BF)],
         compiler_params=params(16),
         name="compress",
     )(filters, own, other)
@@ -322,18 +326,17 @@
     me = (lax.axis_index("y") * 2 + lax.axis_index("core")).astype(jnp.int32).reshape(1)
     power = pl.pallas_call(
         merge_body,
-        out_shape=jax.ShapeDtypeStruct((GROUP, CUT, ANG), F32),
-        in_specs=[SCALAR, WHOLE, LEFT, LEFT],
+        out_shape=jax.ShapeDtypeStruct((GROUP, PAD, ANG), BF),
+        in_specs=[SCALAR, WHOLE, WHOLE, LEFT],
         out_specs=WHOLE,
         scratch_shapes=[
             pltpu.VMEM((2, GROUP, PAD, 256), F32),
-            pltpu.VMEM((2, 256, 2 * ANG), BF),
             pltpu.VMEM((2 * LEVELS, 2 * ANG, 2 * ANG), BF),
-            pltpu.SemaphoreType.DMA((1 + LEVELS,)),
+            pltpu.SemaphoreType.DMA((LEVELS,)),
         ],
-        compiler_params=params(58),
+        compiler_params=params(52),
         name="merge",
-    )(me, compressed.reshape(2 * COLS, 256), operator, band)
+    )(me, compressed.reshape(GROUP * SENT, 256), operator, band)
     power = exchange(power, MERGE)
     chan = lax.axis_index("chan").astype(jnp.int32).reshape(1)
     return pl.pallas_call(

time: 108 us -> 104 us (0.963)
  local copies, waits for them, and re-layouts: 6.21 us -> 3.77 us
  Pallas kernels: 18.1 us -> 16.4 us
    pallas_call x2, Pallas kernels: 9.21 us -> 7.5 us  [the longest x1 4.26 us: local(): pl.pallas_call(merge_body, out_shape=jax.ShapeDtypeStruct((GROUP, PAD, AN...]
  transfers between devices with their start and end apart: 8 -> 8, of which waited for: 4 -> 4; matrix products, arithmetic and copies ran while one was open for 2% -> 1% of each run, Pallas kernels for 7% -> 7%
where the time goes in v3:
time: 104 us
  starting transfers between devices  50.8 us (49%)
  waiting for transfers between devices  31.3 us (30%)
  Pallas kernels  16.4 us (16%)
  local copies, waits for them, and re-layouts  3.77 us (4%)
  other arithmetic  1.25 us (1%)
    all_to_all x4, starting transfers between devices, exchange(): return lax.all_to_all(value, axes, split_axis=0, concat_axis=0, tiled=True)  39.6 us
    all_to_all x4, waiting for transfers between devices, exchange(): return lax.all_to_all(value, axes, split_axis=0, concat_axis=0, tiled=True)  31.3 us
    ppermute x4, starting transfers between devices, flipped(): return lax.ppermute(value, axis, pairs)  11.2 us
    pallas_call x1, Pallas kernels, local(): pl.pallas_call(band_body, grid=(2 * LEVELS,), out_shape=jax.ShapeDtypeStr...  4.45 us
    pallas_call x1, Pallas kernels, local(): pl.pallas_call(merge_body, out_shape=jax.ShapeDtypeStruct((GROUP, PAD, AN...  4.26 us
    unnamed x18, local copies, waits for them, and re-layouts  3.63 us
    pallas_call x1, Pallas kernels, local(): pl.pallas_call(compress_body, out_shape=jax.ShapeDtypeStruct((GROUP, SENT...  3.24 us
  transfers between devices with their start and end apart: 8, of which 4 were waited for; matrix products, arithmetic and copies ran while one was open for 1% of the time, Pallas kernels for 7%

profile of v3, /device:TPU:1, one launch (start us, length us, event | category | flops | bytes accessed | tf_op | source)
XLA Modules:
  0.0 103.7 jit_solution(6692214951848358709)
XLA Ops:
  0.0 0.7 copy-done.3
  0.7 0.7 copies.1
  1.4 15.7 %all-to-all-start = ((bf16[16,8,1024]{2,1,0:T(8,128)(2,1)}), bf16[16,8,1024]{2,1,0:T(8,128)(2,1)S(1)}, u32[]{:S(2)}, u32[]{:S(2)}) async-start(bf16[16,8,1024]{2,1,0:T(8,128)(2,1)} %copies.1), calls=%async_computation | async-start | bytes 524288 | tf_op jit(solution)/shard_map/all_to_all | solution.py:248
  17.2 0.0 copy-start.1
  17.2 0.9 copy-done.1
  18.1 0.3 raw_order.1
  18.5 4.6 %collective-permute-start.2 = (bf16[32,4096]{1,0:T(8,128)(2,1)S(1)}, bf16[32,4096]{1,0:T(8,128)(2,1)S(1)}, u32[]{:S(2)}, u32[]{:S(2)}) collective-permute-start(bf16[32,4096]{1,0:T(8,128)(2,1)S(1)} %raw_order.1), channel_id=1, source_target_pairs={{0,48},{16,32},{32,16},{48,0},{1,49},{17,33},{33,17},{49,1},{2,50}... | collective-permute-start | bytes 786440 | tf_op jit(solution)/shard_map/ppermute | solution.py:244
  23.1 2.3 %collective-permute-start.1 = (bf16[32,4096]{1,0:T(8,128)(2,1)S(1)}, bf16[32,4096]{1,0:T(8,128)(2,1)S(1)}, u32[]{:S(2)}, u32[]{:S(2)}) collective-permute-start(bf16[32,4096]{1,0:T(8,128)(2,1)S(1)} %raw_order.1), channel_id=1, source_target_pairs={{0,32},{16,48},{32,0},{48,16},{1,33},{17,49},{33,1},{49,17},{2,34}... | collective-permute-start | bytes 786440 | tf_op jit(solution)/shard_map/ppermute | solution.py:244
  25.4 2.1 %collective-permute-start = (bf16[32,4096]{1,0:T(8,128)(2,1)S(1)}, bf16[32,4096]{1,0:T(8,128)(2,1)S(1)}, u32[]{:S(2)}, u32[]{:S(2)}) collective-permute-start(bf16[32,4096]{1,0:T(8,128)(2,1)S(1)} %raw_order.1), channel_id=1, source_target_pairs={{0,16},{16,0},{32,48},{48,32},{1,17},{17,1},{33,49},{49,33},{2,18}... | collective-permute-start | bytes 786440 | tf_op jit(solution)/shard_map/ppermute | solution.py:244
  27.5 2.8 %all-to-all-done = bf16[16,8,1024]{2,1,0:T(8,128)(2,1)S(1)} async-done(((bf16[16,8,1024]{2,1,0:T(8,128)(2,1)}), bf16[16,8,1024]{2,1,0:T(8,128)(2,1)S(1)}, u32[]{:S(2)}, u32[]{:S(2)}) %all-to-all-start) | async-done | bytes 262176 | tf_op jit(solution)/shard_map/all_to_all | solution.py:248
  30.3 2.0 %pick_bins.1 = bf16[4,8,144,128]{3,2,1,0:T(8,128)(2,1)} custom-call(bf16[128,1024]{1,0:T(8,128)(2,1)S(1)} %bitcast.15), custom_call_target="tpu_custom_call" | custom-call | tf_op jit(solution)/shard_map/pick_bins/pallas_call | solution.py:274
  32.3 13.4 %all-to-all-start.1 = ((bf16[32,144,128]{2,1,0:T(8,128)(2,1)}), bf16[32,144,128]{2,1,0:T(8,128)(2,1)S(1)}, u32[]{:S(2)}, u32[]{:S(2)}) async-start(bf16[32,144,128]{2,1,0:T(8,128)(2,1)} %bitcast.3), calls=%async_computation.1 | async-start | bytes 2359296 | tf_op jit(solution)/shard_map/all_to_all | solution.py:248
  45.7 0.0 copy-start.6
  45.7 0.0 collective-permute-done.1
  45.8 0.0 collective-permute-done
  45.8 0.1 pad_maximum_fusion.own_ref
  45.9 2.1 %collective-permute-start.3 = (bf16[128,4096]{1,0:T(8,128)(2,1)S(1)}, bf16[128,4096]{1,0:T(8,128)(2,1)}, u32[]{:S(2)}, u32[]{:S(2)}) collective-permute-start(bf16[128,4096]{1,0:T(8,128)(2,1)S(1)} %pad_maximum_fusion.own_ref), channel_id=1, source_target_pairs={{0,8},{8,0},{1,9},{9,1},{2,10},{10,2},{3,11},{11,3},{4,12},{12,4},... | collective-permute-start | bytes 3145736 | tf_op jit(solution)/shard_map/ppermute | solution.py:244
  48.0 0.1 reshape.137.mix_ref
  48.2 0.0 copy-start.8
  48.2 0.0 copy-start.2
  48.2 4.4 %band.1.band_far = bf16[8,512,512]{2,1,0:T(8,128)(2,1)S(1)} custom-call(s32[8,1,256]{2,1,0:T(1,128)S(1)} %reshape.138.offset_ref, f32[8,2,2,8,256]{4,3,2,1,0:T(8,128)S(1)} %bitcast.14), custom_call_target="tpu_custom_call" | custom-call | tf_op jit(solution)/shard_map/band/pallas_call | solution.py:299
  52.7 1.9 %copy-done = bf16[8,512,512]{2,1,0:T(8,128)(2,1)} copy-done((bf16[8,512,512]{2,1,0:T(8,128)(2,1)}, bf16[8,512,512]{2,1,0:T(8,128)(2,1)S(1)}, u32[]{:S(2)}) %copy-start) | copy-done | bytes 4194328
  54.6 1.1 %fusion.1 = (bf16[1,256,256]{2,1,0:T(8,128)(2,1)S(1)}, bf16[1,256,256]{2,1,0:T(8,128)(2,1)S(1)}) fusion(f32[256]{0:T(256)S(1)} %convert_add_fusion, f32[256]{0:T(256)S(1)} %copy-done.8), kind=kLoop, calls=%fused_computation.4 | loop fusion | flops 327680 | bytes 264192 | tf_op jit(solution)/shard_map/convert
  55.8 0.5 operator.1.operator_ref
  56.3 7.8 %all-to-all-done.1.filter_ref = bf16[32,144,128]{2,1,0:T(8,128)(2,1)S(1)} async-done(((bf16[32,144,128]{2,1,0:T(8,128)(2,1)}), bf16[32,144,128]{2,1,0:T(8,128)(2,1)S(1)}, u32[]{:S(2)}, u32[]{:S(2)}) %all-to-all-start.1) | async-done | bytes 1179680 | tf_op jit(solution)/shard_map/all_to_all | solution.py:248
  64.1 3.2 %compress.1 = bf16[16,24,256]{2,1,0:T(8,128)(2,1)} custom-call(bf16[32,144,128]{2,1,0:T(8,128)(2,1)S(1)} %all-to-all-done.1.filter_ref, bf16[128,4096]{1,0:T(8,128)(2,1)S(1)} %pad_maximum_fusion.own_ref, bf16[128,4096]{1,0:T(8,128)(2,1)} %collective-permute-done.3.other_ref), custom_call_target="tpu_custom_call" | custom-call | tf_op jit(solution)/shard_map/compress/pallas_call | solution.py:316
  67.3 5.5 %all-to-all-start.2 = ((bf16[16,24,256]{2,1,0:T(8,128)(2,1)}), bf16[16,24,256]{2,1,0:T(8,128)(2,1)S(1)}, u32[]{:S(2)}, u32[]{:S(2)}) async-start(bf16[16,24,256]{2,1,0:T(8,128)(2,1)} %compress.1), calls=%async_computation.2 | async-start | bytes 393216 | tf_op jit(solution)/shard_map/all_to_all | solution.py:248
  72.8 14.5 %all-to-all-done.2 = bf16[16,24,256]{2,1,0:T(8,128)(2,1)S(1)} async-done(((bf16[16,24,256]{2,1,0:T(8,128)(2,1)}), bf16[16,24,256]{2,1,0:T(8,128)(2,1)S(1)}, u32[]{:S(2)}, u32[]{:S(2)}) %all-to-all-start.2) | async-done | bytes 196640 | tf_op jit(solution)/shard_map/all_to_all | solution.py:248
  87.3 4.3 %merge.1 = bf16[16,16,256]{2,1,0:T(8,128)(2,1)} custom-call(s32[1]{0:T(128)} %bitcast.1.me_ref, bf16[384,256]{1,0:T(8,128)(2,1)S(1)} %bitcast.16, bf16[2,256,512]{2,1,0:T(8,128)(2,1)S(1)} %operator.1.operator_ref, bf16[8,512,512]{2,1,0:T(8,128)(2,1)} %copy-done), custom_call_target="tpu_custom_call" | custom-call | tf_op jit(solution)/shard_map/merge/pallas_call | solution.py:327
  91.6 5.0 %all-to-all-start.3 = ((bf16[16,16,256]{2,1,0:T(8,128)(2,1)}), bf16[16,16,256]{2,1,0:T(8,128)(2,1)S(1)}, u32[]{:S(2)}, u32[]{:S(2)}) async-start(bf16[16,16,256]{2,1,0:T(8,128)(2,1)} %merge.1), calls=%async_computation.3 | async-start | bytes 262144 | tf_op jit(solution)/shard_map/all_to_all | solution.py:248
  96.6 6.2 %all-to-all-done.3.power_ref = bf16[16,16,256]{2,1,0:T(8,128)(2,1)S(1)} async-done(((bf16[16,16,256]{2,1,0:T(8,128)(2,1)}), bf16[16,16,256]{2,1,0:T(8,128)(2,1)S(1)}, u32[]{:S(2)}, u32[]{:S(2)}) %all-to-all-start.3) | async-done | bytes 131104 | tf_op jit(solution)/shard_map/all_to_all | solution.py:248
  102.8 0.9 despeckle.1
  (18 shorter events, 0.1 us)
Async XLA Ops:
  0.0 0.7 copy-start.3
  1.4 28.9 %all-to-all-start = ((bf16[16,8,1024]{2,1,0:T(8,128)(2,1)}), bf16[16,8,1024]{2,1,0:T(8,128)(2,1)S(1)}, u32[]{:S(2)}, u32[]{:S(2)}) async-start(bf16[16,8,1024]{2,1,0:T(8,128)(2,1)} %copies.1), calls=%async_computation | async-start | bytes 524288 | tf_op jit(solution)/shard_map/all_to_all | solution.py:248
  17.2 1.0 copy-start.1
  18.5 27.3 %collective-permute-start.2 = (bf16[32,4096]{1,0:T(8,128)(2,1)S(1)}, bf16[32,4096]{1,0:T(8,128)(2,1)S(1)}, u32[]{:S(2)}, u32[]{:S(2)}) collective-permute-start(bf16[32,4096]{1,0:T(8,128)(2,1)S(1)} %raw_order.1), channel_id=1, source_target_pairs={{0,48},{16,32},{32,16},{48,0},{1,49},{17,33},{33,17},{49,1},{2,50}... | collective-permute-start | bytes 786440 | tf_op jit(solution)/shard_map/ppermute | solution.py:244
  23.1 22.6 %collective-permute-start.1 = (bf16[32,4096]{1,0:T(8,128)(2,1)S(1)}, bf16[32,4096]{1,0:T(8,128)(2,1)S(1)}, u32[]{:S(2)}, u32[]{:S(2)}) collective-permute-start(bf16[32,4096]{1,0:T(8,128)(2,1)S(1)} %raw_order.1), channel_id=1, source_target_pairs={{0,32},{16,48},{32,0},{48,16},{1,33},{17,49},{33,1},{49,17},{2,34}... | collective-permute-start | bytes 786440 | tf_op jit(solution)/shard_map/ppermute | solution.py:244
  25.4 20.4 %collective-permute-start = (bf16[32,4096]{1,0:T(8,128)(2,1)S(1)}, bf16[32,4096]{1,0:T(8,128)(2,1)S(1)}, u32[]{:S(2)}, u32[]{:S(2)}) collective-permute-start(bf16[32,4096]{1,0:T(8,128)(2,1)S(1)} %raw_order.1), channel_id=1, source_target_pairs={{0,16},{16,0},{32,48},{48,32},{1,17},{17,1},{33,49},{49,33},{2,18}... | collective-permute-start | bytes 786440 | tf_op jit(solution)/shard_map/ppermute | solution.py:244
  32.3 15.8 %copy-start.7 = (s32[4,512]{1,0:T(4,128)S(1)}, s32[4,512]{1,0:T(4,128)}, u32[]{:S(2)}) copy-start(s32[4,512]{1,0:T(4,128)} %param.12) | copy-start | bytes 24580
  32.3 15.9 %copy-start.5 = (f32[4,2,2,512,8]{3,4,2,1,0:T(8,128)S(1)}, f32[4,2,2,512,8]{3,4,2,1,0:T(8,128)}, u32[]{:S(2)}) copy-start(f32[4,2,2,512,8]{3,4,2,1,0:T(8,128)} %param.13) | copy-start | bytes 786436
  32.3 31.8 %all-to-all-start.1 = ((bf16[32,144,128]{2,1,0:T(8,128)(2,1)}), bf16[32,144,128]{2,1,0:T(8,128)(2,1)S(1)}, u32[]{:S(2)}, u32[]{:S(2)}) async-start(bf16[32,144,128]{2,1,0:T(8,128)(2,1)} %bitcast.3), calls=%async_computation.1 | async-start | bytes 2359296 | tf_op jit(solution)/shard_map/all_to_all | solution.py:248
  45.7 2.3 %copy-start.6 = (f32[2,32,8,8]{1,3,2,0:T(8,128)S(1)}, f32[2,32,8,8]{1,3,2,0:T(8,128)}, u32[]{:S(2)}) copy-start(f32[2,32,8,8]{1,3,2,0:T(8,128)} %param.10) | copy-start | bytes 49156
  45.9 18.2 %collective-permute-start.3 = (bf16[128,4096]{1,0:T(8,128)(2,1)S(1)}, bf16[128,4096]{1,0:T(8,128)(2,1)}, u32[]{:S(2)}, u32[]{:S(2)}) collective-permute-start(bf16[128,4096]{1,0:T(8,128)(2,1)S(1)} %pad_maximum_fusion.own_ref), channel_id=1, source_target_pairs={{0,8},{8,0},{1,9},{9,1},{2,10},{10,2},{3,11},{11,3},{4,12},{12,4},... | collective-permute-start | bytes 3145736 | tf_op jit(solution)/shard_map/ppermute | solution.py:244
  48.2 6.4 %copy-start.8 = (f32[256]{0:T(256)S(1)}, f32[256]{0:T(256)}, u32[]{:S(2)}) copy-start(f32[256]{0:T(256)} %param.11) | copy-start | bytes 3076
  48.2 7.6 %copy-start.2 = (f32[2,32,256]{2,1,0:T(8,128)S(1)}, f32[2,32,256]{2,1,0:T(8,128)}, u32[]{:S(2)}) copy-start(f32[2,32,256]{2,1,0:T(8,128)} %constant.23.clone.dop_ref) | copy-start | bytes 196612
  52.7 1.9 %copy-start = (bf16[8,512,512]{2,1,0:T(8,128)(2,1)}, bf16[8,512,512]{2,1,0:T(8,128)(2,1)S(1)}, u32[]{:S(2)}) copy-start(bf16[8,512,512]{2,1,0:T(8,128)(2,1)S(1)} %band.1.band_far) | copy-start | bytes 12582916
  67.3 20.0 %all-to-all-start.2 = ((bf16[16,24,256]{2,1,0:T(8,128)(2,1)}), bf16[16,24,256]{2,1,0:T(8,128)(2,1)S(1)}, u32[]{:S(2)}, u32[]{:S(2)}) async-start(bf16[16,24,256]{2,1,0:T(8,128)(2,1)} %compress.1), calls=%async_computation.2 | async-start | bytes 393216 | tf_op jit(solution)/shard_map/all_to_all | solution.py:248
  87.3 15.5 %copy-start.4 = (f32[256]{0:T(256)S(1)}, f32[256]{0:T(256)}, u32[]{:S(2)}) copy-start(f32[256]{0:T(256)} %param.14) | copy-start | bytes 3076
  91.6 11.2 %all-to-all-start.3 = ((bf16[16,16,256]{2,1,0:T(8,128)(2,1)}), bf16[16,16,256]{2,1,0:T(8,128)(2,1)S(1)}, u32[]{:S(2)}, u32[]{:S(2)}) async-start(bf16[16,16,256]{2,1,0:T(8,128)(2,1)} %merge.1), calls=%async_computation.3 | async-start | bytes 262144 | tf_op jit(solution)/shard_map/all_to_all | solution.py:248

commit v4 on v3

--- a/solution.py
+++ b/solution.py
@@ -75,31 +75,37 @@
         out_ref[:, u * 512 : (u + 1) * 512] = moved[u * 32 : (u + 1) * 32]
 
 
-def copies_body(filter_ref, out_ref):
-    rows = filter_ref[...].astype(F32)
-    rows = jnp.concatenate([rows[0], rows[1]], axis=0).astype(BF)
+def copies_body(filter_far, out_far, sems):
+    copies = [pltpu.make_async_copy(filter_far, out_far.at[z], sems.at[z]) for z in range(16)]
+    for copy in copies:
+        copy.start()
+    for copy in copies:
+        copy.wait()
+
+
+def pick_body(filter_ref, out_far, ordered, picked, sems):
     for z in range(16):
-        out_ref[z] = rows
-
-
-def pick_body(filter_ref, out_ref):
-    i, k = iota((128, 128), 0), iota((128, 128), 1)
-    source = (((i >> 5) & 1) * 8 + ((i >> 2) & 7)) * 8 + (i >> 6) * 4 + (i & 3)
-    rows = dot(jnp.where(k == source, 1.0, 0.0).astype(BF), filter_ref[...]).astype(BF)
+        for part in range(2):
+            at = part * 64 + z * 4
+            ordered[at : at + 4, :] = filter_ref[z, part].astype(F32)
+    rows = ordered[...].astype(BF)
     bins = iota((COLS, 1024), 1)
     r = iota((COLS, 1024), 0)
     dest = r // CUT
     first = 128 * (dest & 7) - HALO + 8 * CUT * (dest >> 3) + r - dest * CUT
+    copies = []
     for g in range(ROW):
         pick = jnp.where(bins == first + CUT * g, 1.0, 0.0).astype(BF)
-        block = dot_t(pick, rows).astype(BF)
+        picked[g] = dot_t(pick, rows).astype(BF)
         for x in range(4):
-            out_ref[x, g] = block
-
-
-def compress_body(filter_ref, own_ref, other_ref, out_ref, pulses):
-    pulses[:128, :] = own_ref[...]
-    pulses[128:, :] = other_ref[...]
+            copy = pltpu.make_async_copy(picked.at[g], out_far.at[x, g], sems.at[x, g])
+            copy.start()
+            copies.append(copy)
+    for copy in copies:
+        copy.wait()
+
+
+def compress_body(filter_ref, own_ref, other_ref, out_ref):
     first, second = [], []
     for s in range(32):
         block = filter_ref[s]
@@ -108,7 +114,7 @@
     left = jnp.concatenate(
         [jnp.concatenate(first, axis=1), jnp.concatenate(second, axis=1)], axis=0
     )
-    summed = dot_t(left, pulses[...])
+    summed = jnp.concatenate([dot_t(left, own_ref[...]), dot_t(left, other_ref[...])], axis=1)
     row, col = iota((32 * GROUP, 2 * COLS), 0), iota((32 * GROUP, 2 * COLS), 1)
     within = row & 31
     source = (row >> 5) * CUT + jnp.where(within >= CUT, within - CUT + COLS, within)
@@ -264,37 +270,28 @@
 
     rows = pl.pallas_call(
         copies_body,
-        out_shape=jax.ShapeDtypeStruct((16, 8, 1024), BF),
-        in_specs=[WHOLE],
-        out_specs=WHOLE,
-        compiler_params=params(2),
+        out_shape=jax.ShapeDtypeStruct((16, 2, 4, 1024), BF),
+        in_specs=[LEFT],
+        out_specs=LEFT,
+        scratch_shapes=[pltpu.SemaphoreType.DMA((16,))],
         name="copies",
     )(range_filter)
-    rows = exchange(rows, ALONG_Z).reshape(128, 1024)
+    rows = exchange(rows, ALONG_Z)
     picked = pl.pallas_call(
         pick_body,
         out_shape=jax.ShapeDtypeStruct((4, ROW, COLS, 128), BF),
         in_specs=[WHOLE],
-        out_specs=WHOLE,
+        out_specs=LEFT,
+        scratch_shapes=[
+            pltpu.VMEM((128, 1024), F32),
+            pltpu.VMEM((ROW, COLS, 128), BF),
+            pltpu.SemaphoreType.DMA((4, ROW)),
+        ],
         compiler_params=params(8),
         name="pick_bins",
     )(rows)
     filters = exchange(picked.reshape(32, COLS, 128), PLANE)
 
-    offset = jnp.arange(ANG, dtype=jnp.int32).astype(F32) - 0.5 * ANG
-    phase = steer_angles[None, :] * offset[:, None]
-    factor = 1.0 / np.sqrt(ANG)
-    beams = jnp.stack([jnp.cos(phase) * factor, jnp.sin(phase) * factor]).astype(BF)
-    mix = channel_mix.transpose(0, 3, 2, 1).reshape(2, CHAN, 256)
-    doppler = jnp.asarray(np.tile(doppler_table().transpose(0, 2, 1), (1, 1, CHAN)))
-    operator = pl.pallas_call(
-        operator_body,
-        out_shape=jax.ShapeDtypeStruct((2, 256, 2 * ANG), BF),
-        in_specs=[WHOLE] * 3,
-        out_specs=WHOLE,
-        compiler_params=params(8),
-        name="operator",
-    )(mix, doppler, beams)
     weights = band_weights.reshape(LEVELS, 2, 2, 2, ANG, BAND).transpose(0, 3, 1, 2, 5, 4)
     band = pl.pallas_call(
         band_body,
@@ -312,16 +309,33 @@
         weights.reshape(2 * LEVELS, 2, 2, BAND, ANG),
     )
 
-    filters, operator, band = lax.optimization_barrier((filters, operator, band))
+    filters, band = lax.optimization_barrier((filters, band))
     compressed = pl.pallas_call(
         compress_body,
         out_shape=jax.ShapeDtypeStruct((GROUP, SENT, 256), BF),
         in_specs=[WHOLE] * 3,
         out_specs=WHOLE,
-        scratch_shapes=[pltpu.VMEM((256, 4096), BF)],
         compiler_params=params(16),
         name="compress",
     )(filters, own, other)
+
+    compressed, steer_angles, channel_mix = lax.optimization_barrier(
+        (compressed, steer_angles, channel_mix)
+    )
+    offset = jnp.arange(ANG, dtype=jnp.int32).astype(F32) - 0.5 * ANG
+    phase = steer_angles[None, :] * offset[:, None]
+    factor = 1.0 / np.sqrt(ANG)
+    beams = jnp.stack([jnp.cos(phase) * factor, jnp.sin(phase) * factor]).astype(BF)
+    mix = channel_mix.transpose(0, 3, 2, 1).reshape(2, CHAN, 256)
+    doppler = jnp.asarray(np.tile(doppler_table().transpose(0, 2, 1), (1, 1, CHAN)))
+    operator = pl.pallas_call(
+        operator_body,
+        out_shape=jax.ShapeDtypeStruct((2, 256, 2 * ANG), BF),
+        in_specs=[WHOLE] * 3,
+        out_specs=WHOLE,
+        compiler_params=params(8),
+        name="operator",
+    )(mix, doppler, beams)
     compressed = exchange(compressed, ("x0", "chan"))
     me = (lax.axis_index("y") * 2 + lax.axis_index("core")).astype(jnp.int32).reshape(1)
     power = pl.pallas_call(

time: 104 us -> 111 us (1.067)
  Pallas kernels: 16.4 us -> 23.8 us
    pallas_call x1, Pallas kernels: 0.72 us -> 9.18 us  [local(): pl.pallas_call(copies_body, out_shape=jax.ShapeDtypeStruct((16, 2, 4, 102...]
    unnamed x18 -> x16, local copies, waits for them, and re-layouts: 3.63 us -> 2.91 us
  transfers between devices with their start and end apart: 8 -> 8, of which waited for: 4 -> 4; matrix products, arithmetic and copies ran while one was open for 1% -> 1% of each run, Pallas kernels for 7% -> 6%
where the time goes in v4:
time: 111 us
  starting transfers between devices  50.9 us (46%)
  waiting for transfers between devices  31.3 us (28%)
  Pallas kernels  23.8 us (21%)
  local copies, waits for them, and re-layouts  3.05 us (3%)
  other arithmetic  1.27 us (1%)
    all_to_all x4, starting transfers between devices, exchange(): return lax.all_to_all(value, axes, split_axis=0, concat_axis=0, tiled=True)  39.7 us
    all_to_all x4, waiting for transfers between devices, exchange(): return lax.all_to_all(value, axes, split_axis=0, concat_axis=0, tiled=True)  31.3 us
    ppermute x4, starting transfers between devices, flipped(): return lax.ppermute(value, axis, pairs)  11.2 us
    pallas_call x1, Pallas kernels, local(): pl.pallas_call(copies_body, out_shape=jax.ShapeDtypeStruct((16, 2, 4, 102...  9.18 us
    pallas_call x1, Pallas kernels, local(): pl.pallas_call(band_body, grid=(2 * LEVELS,), out_shape=jax.ShapeDtypeStr...  4.45 us
    pallas_call x1, Pallas kernels, local(): pl.pallas_call(merge_body, out_shape=jax.ShapeDtypeStruct((GROUP, PAD, AN...  4.26 us
    unnamed x16, local copies, waits for them, and re-layouts  2.91 us
    pallas_call x1, Pallas kernels, local(): pl.pallas_call(compress_body, out_shape=jax.ShapeDtypeStruct((GROUP, SENT...  2.35 us
  transfers between devices with their start and end apart: 8, of which 4 were waited for; matrix products, arithmetic and copies ran while one was open for 1% of the time, Pallas kernels for 6%

profile of v4, /device:TPU:1, one launch (start us, length us, event | category | flops | bytes accessed | tf_op | source)
XLA Modules:
  0.0 110.5 jit_solution(10449136014470425385)
XLA Ops:
  0.0 9.2 %copies.1 = bf16[16,2,4,1024]{3,2,1,0:T(4,128)(2,1)} custom-call(bf16[2,4,1024]{2,1,0:T(4,128)(2,1)} %filter_far.1), custom_call_target="tpu_custom_call" | custom-call | tf_op jit(solution)/shard_map/copies/pallas_call | solution.py:271
  9.2 15.8 %all-to-all-start = ((bf16[16,2,4,1024]{3,2,1,0:T(4,128)(2,1)}), bf16[16,2,4,1024]{3,2,1,0:T(4,128)(2,1)S(1)}, u32[]{:S(2)}, u32[]{:S(2)}) async-start(bf16[16,2,4,1024]{3,2,1,0:T(4,128)(2,1)} %copies.1), calls=%async_computation | async-start | bytes 524288 | tf_op jit(solution)/shard_map/all_to_all | solution.py:254
  25.0 0.0 copy-start.1
  25.0 0.9 copy-done.1
  25.9 0.3 raw_order.1
  26.2 4.6 %collective-permute-start.2 = (bf16[32,4096]{1,0:T(8,128)(2,1)S(1)}, bf16[32,4096]{1,0:T(8,128)(2,1)S(1)}, u32[]{:S(2)}, u32[]{:S(2)}) collective-permute-start(bf16[32,4096]{1,0:T(8,128)(2,1)S(1)} %raw_order.1), channel_id=1, source_target_pairs={{0,48},{16,32},{32,16},{48,0},{1,49},{17,33},{33,17},{49,1},{2,50}... | collective-permute-start | bytes 786440 | tf_op jit(solution)/shard_map/ppermute | solution.py:250
  30.9 2.3 %collective-permute-start.1 = (bf16[32,4096]{1,0:T(8,128)(2,1)S(1)}, bf16[32,4096]{1,0:T(8,128)(2,1)S(1)}, u32[]{:S(2)}, u32[]{:S(2)}) collective-permute-start(bf16[32,4096]{1,0:T(8,128)(2,1)S(1)} %raw_order.1), channel_id=1, source_target_pairs={{0,32},{16,48},{32,0},{48,16},{1,33},{17,49},{33,1},{49,17},{2,34}... | collective-permute-start | bytes 786440 | tf_op jit(solution)/shard_map/ppermute | solution.py:250
  33.1 2.2 %collective-permute-start = (bf16[32,4096]{1,0:T(8,128)(2,1)S(1)}, bf16[32,4096]{1,0:T(8,128)(2,1)S(1)}, u32[]{:S(2)}, u32[]{:S(2)}) collective-permute-start(bf16[32,4096]{1,0:T(8,128)(2,1)S(1)} %raw_order.1), channel_id=1, source_target_pairs={{0,16},{16,0},{32,48},{48,32},{1,17},{17,1},{33,49},{49,33},{2,18}... | collective-permute-start | bytes 786440 | tf_op jit(solution)/shard_map/ppermute | solution.py:250
  35.3 2.8 %all-to-all-done.filter_ref = bf16[16,2,4,1024]{3,2,1,0:T(4,128)(2,1)S(1)} async-done(((bf16[16,2,4,1024]{3,2,1,0:T(4,128)(2,1)}), bf16[16,2,4,1024]{3,2,1,0:T(4,128)(2,1)S(1)}, u32[]{:S(2)}, u32[]{:S(2)}) %all-to-all-start) | async-done | bytes 262176 | tf_op jit(solution)/shard_map/all_to_all | solution.py:254
  38.1 1.8 %pick_bins.1 = bf16[4,8,144,128]{3,2,1,0:T(8,128)(2,1)} custom-call(bf16[16,2,4,1024]{3,2,1,0:T(4,128)(2,1)S(1)} %all-to-all-done.filter_ref), custom_call_target="tpu_custom_call" | custom-call | tf_op jit(solution)/shard_map/pick_bins/pallas_call | solution.py:280
  39.9 0.0 copy-start.6
  39.9 0.0 copy-start.4
  40.0 13.4 %all-to-all-start.1 = ((bf16[32,144,128]{2,1,0:T(8,128)(2,1)}), bf16[32,144,128]{2,1,0:T(8,128)(2,1)S(1)}, u32[]{:S(2)}, u32[]{:S(2)}) async-start(bf16[32,144,128]{2,1,0:T(8,128)(2,1)} %bitcast.2), calls=%async_computation.1 | async-start | bytes 2359296 | tf_op jit(solution)/shard_map/all_to_all | solution.py:254
  53.4 0.0 collective-permute-done.2
  53.4 0.0 collective-permute-done.1
  53.4 0.0 collective-permute-done
  53.4 0.1 pad_maximum_fusion.own_ref
  53.5 2.1 %collective-permute-start.3 = (bf16[128,4096]{1,0:T(8,128)(2,1)S(1)}, bf16[128,4096]{1,0:T(8,128)(2,1)S(1)}, u32[]{:S(2)}, u32[]{:S(2)}) collective-permute-start(bf16[128,4096]{1,0:T(8,128)(2,1)S(1)} %pad_maximum_fusion.own_ref), channel_id=1, source_target_pairs={{0,8},{8,0},{1,9},{9,1},{2,10},{10,2},{3,11},{11,3},{4,12},{12,4},... | collective-permute-start | bytes 3145736 | tf_op jit(solution)/shard_map/ppermute | solution.py:250
  55.7 4.4 %band.1.band_far = bf16[8,512,512]{2,1,0:T(8,128)(2,1)S(1)} custom-call(s32[8,1,256]{2,1,0:T(1,128)S(1)} %reshape.133.offset_ref, f32[8,2,2,8,256]{4,3,2,1,0:T(8,128)S(1)} %bitcast.13), custom_call_target="tpu_custom_call" | custom-call | tf_op jit(solution)/shard_map/band/pallas_call | solution.py:296
  60.2 1.9 %copy-done = bf16[8,512,512]{2,1,0:T(8,128)(2,1)} copy-done((bf16[8,512,512]{2,1,0:T(8,128)(2,1)}, bf16[8,512,512]{2,1,0:T(8,128)(2,1)S(1)}, u32[]{:S(2)}) %copy-start) | copy-done | bytes 4194328
  62.1 9.6 %all-to-all-done.1.filter_ref = bf16[32,144,128]{2,1,0:T(8,128)(2,1)S(1)} async-done(((bf16[32,144,128]{2,1,0:T(8,128)(2,1)}), bf16[32,144,128]{2,1,0:T(8,128)(2,1)S(1)}, u32[]{:S(2)}, u32[]{:S(2)}) %all-to-all-start.1) | async-done | bytes 1179680 | tf_op jit(solution)/shard_map/all_to_all | solution.py:254
  71.7 0.0 collective-permute-done.3.other_ref
  71.7 2.3 %compress.1 = bf16[16,24,256]{2,1,0:T(8,128)(2,1)} custom-call(bf16[32,144,128]{2,1,0:T(8,128)(2,1)S(1)} %all-to-all-done.1.filter_ref, bf16[128,4096]{1,0:T(8,128)(2,1)S(1)} %pad_maximum_fusion.own_ref, bf16[128,4096]{1,0:T(8,128)(2,1)S(1)} %collective-permute-done.3.other_ref), custom_call_target="tpu_custom_call" | custom-call | tf_op jit(solution)/shard_map/compress/pallas_call | solution.py:313
  74.1 5.5 %all-to-all-start.2 = ((bf16[16,24,256]{2,1,0:T(8,128)(2,1)}), bf16[16,24,256]{2,1,0:T(8,128)(2,1)S(1)}, u32[]{:S(2)}, u32[]{:S(2)}) async-start(bf16[16,24,256]{2,1,0:T(8,128)(2,1)} %compress.1), calls=%async_computation.2 | async-start | bytes 393216 | tf_op jit(solution)/shard_map/all_to_all | solution.py:254
  79.7 0.1 reshape.138.mix_ref
  79.7 1.1 %fusion.1 = (bf16[1,256,256]{2,1,0:T(8,128)(2,1)S(1)}, bf16[1,256,256]{2,1,0:T(8,128)(2,1)S(1)}) fusion(f32[256]{0:T(256)S(1)} %convert_add_fusion, f32[256]{0:T(256)S(1)} %copy-done.7), kind=kLoop, calls=%fused_computation.4 | loop fusion | flops 327680 | bytes 264192 | tf_op jit(solution)/shard_map/convert
  80.9 0.5 operator.1.operator_ref
  81.4 12.7 %all-to-all-done.2 = bf16[16,24,256]{2,1,0:T(8,128)(2,1)S(1)} async-done(((bf16[16,24,256]{2,1,0:T(8,128)(2,1)}), bf16[16,24,256]{2,1,0:T(8,128)(2,1)S(1)}, u32[]{:S(2)}, u32[]{:S(2)}) %all-to-all-start.2) | async-done | bytes 196640 | tf_op jit(solution)/shard_map/all_to_all | solution.py:254
  94.1 4.3 %merge.1 = bf16[16,16,256]{2,1,0:T(8,128)(2,1)} custom-call(s32[1]{0:T(128)} %bitcast.1.me_ref, bf16[384,256]{1,0:T(8,128)(2,1)S(1)} %bitcast.14, bf16[2,256,512]{2,1,0:T(8,128)(2,1)S(1)} %operator.1.operator_ref, bf16[8,512,512]{2,1,0:T(8,128)(2,1)} %copy-done), custom_call_target="tpu_custom_call" | custom-call | tf_op jit(solution)/shard_map/merge/pallas_call | solution.py:341
  98.3 5.0 %all-to-all-start.3 = ((bf16[16,16,256]{2,1,0:T(8,128)(2,1)}), bf16[16,16,256]{2,1,0:T(8,128)(2,1)S(1)}, u32[]{:S(2)}, u32[]{:S(2)}) async-start(bf16[16,16,256]{2,1,0:T(8,128)(2,1)} %merge.1), calls=%async_computation.3 | async-start | bytes 262144 | tf_op jit(solution)/shard_map/all_to_all | solution.py:254
  103.3 6.2 %all-to-all-done.3.power_ref = bf16[16,16,256]{2,1,0:T(8,128)(2,1)S(1)} async-done(((bf16[16,16,256]{2,1,0:T(8,128)(2,1)}), bf16[16,16,256]{2,1,0:T(8,128)(2,1)S(1)}, u32[]{:S(2)}, u32[]{:S(2)}) %all-to-all-start.3) | async-done | bytes 131104 | tf_op jit(solution)/shard_map/all_to_all | solution.py:254
  109.6 0.9 despeckle.1
  (16 shorter events, 0.1 us)
Async XLA Ops:
  9.2 28.9 %all-to-all-start = ((bf16[16,2,4,1024]{3,2,1,0:T(4,128)(2,1)}), bf16[16,2,4,1024]{3,2,1,0:T(4,128)(2,1)S(1)}, u32[]{:S(2)}, u32[]{:S(2)}) async-start(bf16[16,2,4,1024]{3,2,1,0:T(4,128)(2,1)} %copies.1), calls=%async_computation | async-start | bytes 524288 | tf_op jit(solution)/shard_map/all_to_all | solution.py:254
  25.0 1.0 copy-start.1
  26.2 27.1 %collective-permute-start.2 = (bf16[32,4096]{1,0:T(8,128)(2,1)S(1)}, bf16[32,4096]{1,0:T(8,128)(2,1)S(1)}, u32[]{:S(2)}, u32[]{:S(2)}) collective-permute-start(bf16[32,4096]{1,0:T(8,128)(2,1)S(1)} %raw_order.1), channel_id=1, source_target_pairs={{0,48},{16,32},{32,16},{48,0},{1,49},{17,33},{33,17},{49,1},{2,50}... | collective-permute-start | bytes 786440 | tf_op jit(solution)/shard_map/ppermute | solution.py:250
  30.9 22.5 %collective-permute-start.1 = (bf16[32,4096]{1,0:T(8,128)(2,1)S(1)}, bf16[32,4096]{1,0:T(8,128)(2,1)S(1)}, u32[]{:S(2)}, u32[]{:S(2)}) collective-permute-start(bf16[32,4096]{1,0:T(8,128)(2,1)S(1)} %raw_order.1), channel_id=1, source_target_pairs={{0,32},{16,48},{32,0},{48,16},{1,33},{17,49},{33,1},{49,17},{2,34}... | collective-permute-start | bytes 786440 | tf_op jit(solution)/shard_map/ppermute | solution.py:250
  33.1 20.2 %collective-permute-start = (bf16[32,4096]{1,0:T(8,128)(2,1)S(1)}, bf16[32,4096]{1,0:T(8,128)(2,1)S(1)}, u32[]{:S(2)}, u32[]{:S(2)}) collective-permute-start(bf16[32,4096]{1,0:T(8,128)(2,1)S(1)} %raw_order.1), channel_id=1, source_target_pairs={{0,16},{16,0},{32,48},{48,32},{1,17},{17,1},{33,49},{49,33},{2,18}... | collective-permute-start | bytes 786440 | tf_op jit(solution)/shard_map/ppermute | solution.py:250
  39.9 15.7 %copy-start.6 = (s32[4,512]{1,0:T(4,128)S(1)}, s32[4,512]{1,0:T(4,128)}, u32[]{:S(2)}) copy-start(s32[4,512]{1,0:T(4,128)} %param.12) | copy-start | bytes 24580
  39.9 15.7 %copy-start.4 = (f32[4,2,2,512,8]{3,4,2,1,0:T(8,128)S(1)}, f32[4,2,2,512,8]{3,4,2,1,0:T(8,128)}, u32[]{:S(2)}) copy-start(f32[4,2,2,512,8]{3,4,2,1,0:T(8,128)} %param.13) | copy-start | bytes 786436
  40.0 31.8 %all-to-all-start.1 = ((bf16[32,144,128]{2,1,0:T(8,128)(2,1)}), bf16[32,144,128]{2,1,0:T(8,128)(2,1)S(1)}, u32[]{:S(2)}, u32[]{:S(2)}) async-start(bf16[32,144,128]{2,1,0:T(8,128)(2,1)} %bitcast.2), calls=%async_computation.1 | async-start | bytes 2359296 | tf_op jit(solution)/shard_map/all_to_all | solution.py:254
  53.5 18.2 %collective-permute-start.3 = (bf16[128,4096]{1,0:T(8,128)(2,1)S(1)}, bf16[128,4096]{1,0:T(8,128)(2,1)S(1)}, u32[]{:S(2)}, u32[]{:S(2)}) collective-permute-start(bf16[128,4096]{1,0:T(8,128)(2,1)S(1)} %pad_maximum_fusion.own_ref), channel_id=1, source_target_pairs={{0,8},{8,0},{1,9},{9,1},{2,10},{10,2},{3,11},{11,3},{4,12},{12,4},... | collective-permute-start | bytes 3145736 | tf_op jit(solution)/shard_map/ppermute | solution.py:250
  60.2 1.9 %copy-start = (bf16[8,512,512]{2,1,0:T(8,128)(2,1)}, bf16[8,512,512]{2,1,0:T(8,128)(2,1)S(1)}, u32[]{:S(2)}) copy-start(bf16[8,512,512]{2,1,0:T(8,128)(2,1)S(1)} %band.1.band_far) | copy-start | bytes 12582916
  62.1 17.5 %copy-start.5 = (f32[2,32,8,8]{1,3,2,0:T(8,128)S(1)}, f32[2,32,8,8]{1,3,2,0:T(8,128)}, u32[]{:S(2)}) copy-start(f32[2,32,8,8]{1,3,2,0:T(8,128)} %param.10) | copy-start | bytes 49156
  62.1 17.6 %copy-start.7 = (f32[256]{0:T(256)S(1)}, f32[256]{0:T(256)}, u32[]{:S(2)}) copy-start(f32[256]{0:T(256)} %param.11) | copy-start | bytes 3076
  62.1 18.8 %copy-start.2 = (f32[2,32,256]{2,1,0:T(8,128)S(1)}, f32[2,32,256]{2,1,0:T(8,128)}, u32[]{:S(2)}) copy-start(f32[2,32,256]{2,1,0:T(8,128)} %constant.23.clone.dop_ref) | copy-start | bytes 196612
  74.1 20.0 %all-to-all-start.2 = ((bf16[16,24,256]{2,1,0:T(8,128)(2,1)}), bf16[16,24,256]{2,1,0:T(8,128)(2,1)S(1)}, u32[]{:S(2)}, u32[]{:S(2)}) async-start(bf16[16,24,256]{2,1,0:T(8,128)(2,1)} %compress.1), calls=%async_computation.2 | async-start | bytes 393216 | tf_op jit(solution)/shard_map/all_to_all | solution.py:254
  94.1 15.5 %copy-start.3 = (f32[256]{0:T(256)S(1)}, f32[256]{0:T(256)}, u32[]{:S(2)}) copy-start(f32[256]{0:T(256)} %param.14) | copy-start | bytes 3076
  98.3 11.2 %all-to-all-start.3 = ((bf16[16,16,256]{2,1,0:T(8,128)(2,1)}), bf16[16,16,256]{2,1,0:T(8,128)(2,1)S(1)}, u32[]{:S(2)}, u32[]{:S(2)}) async-start(bf16[16,16,256]{2,1,0:T(8,128)(2,1)} %merge.1), calls=%async_computation.3 | async-start | bytes 262144 | tf_op jit(solution)/shard_map/all_to_all | solution.py:254

commit v5 on v4

--- a/solution.py
+++ b/solution.py
@@ -75,14 +75,6 @@
         out_ref[:, u * 512 : (u + 1) * 512] = moved[u * 32 : (u + 1) * 32]
 
 
-def copies_body(filter_far, out_far, sems):
-    copies = [pltpu.make_async_copy(filter_far, out_far.at[z], sems.at[z]) for z in range(16)]
-    for copy in copies:
-        copy.start()
-    for copy in copies:
-        copy.wait()
-
-
 def pick_body(filter_ref, out_far, ordered, picked, sems):
     for z in range(16):
         for part in range(2):
@@ -105,7 +97,9 @@
         copy.wait()
 
 
-def compress_body(filter_ref, own_ref, other_ref, out_ref):
+def compress_body(filter_ref, own_ref, other_ref, out_ref, pulses):
+    pulses[:128, :] = own_ref[...]
+    pulses[128:, :] = other_ref[...]
     first, second = [], []
     for s in range(32):
         block = filter_ref[s]
@@ -114,7 +108,7 @@
     left = jnp.concatenate(
         [jnp.concatenate(first, axis=1), jnp.concatenate(second, axis=1)], axis=0
     )
-    summed = jnp.concatenate([dot_t(left, own_ref[...]), dot_t(left, other_ref[...])], axis=1)
+    summed = dot_t(left, pulses[...])
     row, col = iota((32 * GROUP, 2 * COLS), 0), iota((32 * GROUP, 2 * COLS), 1)
     within = row & 31
     source = (row >> 5) * CUT + jnp.where(within >= CUT, within - CUT + COLS, within)
@@ -167,20 +161,16 @@
     for copy in copies:
         copy.start()
     me = me_ref[0]
-    row, col = iota((512, SENT * GROUP), 0), iota((512, SENT * GROUP), 1)
-    j = row & 15
-    source = (row >> 5) * SENT + ((row >> 4) & 1) * CUT + j
-    order = jnp.where((col == source) & (j < CUT), 1.0, 0.0).astype(BF)
-    apart = dot(order, comp_ref[...])
+    apart = comp_ref[...].astype(F32)
     for x in range(2):
         for part in range(2):
             blocks = []
             for c in range(CHAN):
-                at = ((x * 8 + c) * 2 + part) * PAD
-                blocks.append(apart[at : at + PAD])
+                at = (x * 8 + c) * SENT + part * CUT
+                blocks.append(apart[at : at + CUT])
             for q in range(8):
                 n = x * 8 + (((q & 3) * 2 + (q >> 2)) ^ me)
-                pulses[part, n] = jnp.concatenate(
+                pulses[part, n, :CUT, :] = jnp.concatenate(
                     [b[:, q * 32 : (q + 1) * 32] for b in blocks], axis=1
                 )
     pulse = pulses[...].reshape(2 * GROUP * PAD, 256).astype(BF)
@@ -268,14 +258,7 @@
     own = jnp.concatenate([raw] + [flipped(raw, "y", mask) for mask in (1, 2, 3)], axis=0)
     other = flipped(own, "core", 1)
 
-    rows = pl.pallas_call(
-        copies_body,
-        out_shape=jax.ShapeDtypeStruct((16, 2, 4, 1024), BF),
-        in_specs=[LEFT],
-        out_specs=LEFT,
-        scratch_shapes=[pltpu.SemaphoreType.DMA((16,))],
-        name="copies",
-    )(range_filter)
+    rows = jnp.broadcast_to(range_filter[None], (16, *range_filter.shape))
     rows = exchange(rows, ALONG_Z)
     picked = pl.pallas_call(
         pick_body,
@@ -315,6 +298,7 @@
         out_shape=jax.ShapeDtypeStruct((GROUP, SENT, 256), BF),
         in_specs=[WHOLE] * 3,
         out_specs=WHOLE,
+        scratch_shapes=[pltpu.VMEM((256, 4096), BF)],
         compiler_params=params(16),
         name="compress",
     )(filters, own, other)

time: 111 us -> 103 us (0.928)
  Pallas kernels: 23.8 us -> 14.3 us
  local copies, waits for them, and re-layouts: 3.05 us -> 4.57 us
    pallas_call x1 -> x0, Pallas kernels: 9.18 us -> none  [local(): pl.pallas_call(copies_body, out_shape=jax.ShapeDtypeStruct((16, 2, 4, 102...]
    broadcast_in_dim x0 -> x1, local copies, waits for them, and re-layouts: none -> 1.52 us  [local(): rows = jnp.broadcast_to(range_filter[None], (16, *range_filter.shape))]
  transfers between devices with their start and end apart: 8 -> 8, of which waited for: 4 -> 4; matrix products, arithmetic and copies ran while one was open for 1% -> 1% of each run, Pallas kernels for 6% -> 7%
where the time goes in v5:
time: 103 us
  starting transfers between devices  50.8 us (49%)
  waiting for transfers between devices  31.3 us (30%)
  Pallas kernels  14.3 us (14%)
  local copies, waits for them, and re-layouts  4.57 us (4%)
  other arithmetic  1.27 us (1%)
    all_to_all x4, starting transfers between devices, exchange(): return lax.all_to_all(value, axes, split_axis=0, concat_axis=0, tiled=True)  39.7 us
    all_to_all x4, waiting for transfers between devices, exchange(): return lax.all_to_all(value, axes, split_axis=0, concat_axis=0, tiled=True)  31.3 us
    ppermute x4, starting transfers between devices, flipped(): return lax.ppermute(value, axis, pairs)  11.2 us
    pallas_call x1, Pallas kernels, local(): pl.pallas_call(band_body, grid=(2 * LEVELS,), out_shape=jax.ShapeDtypeStr...  4.45 us
    pallas_call x1, Pallas kernels, local(): pl.pallas_call(merge_body, out_shape=jax.ShapeDtypeStruct((GROUP, PAD, AN...  4.32 us
    unnamed x16, local copies, waits for them, and re-layouts  2.91 us
  transfers between devices with their start and end apart: 8, of which 4 were waited for; matrix products, arithmetic and copies ran while one was open for 1% of the time, Pallas kernels for 7%

profile of v5, /device:TPU:1, one launch (start us, length us, event | category | flops | bytes accessed | tf_op | source)
XLA Modules:
  0.0 102.5 jit_solution(7678453070092921365)
XLA Ops:
  0.0 1.5 %broadcast_in_dim.2 = bf16[16,2,4,1024]{3,2,1,0:T(4,128)(2,1)} broadcast(bf16[2,4,1024]{2,1,0:T(4,128)(2,1)} %param.9), dimensions={1,2,3} | broadcast | bytes 278528 | tf_op jit(solution)/shard_map/broadcast_in_dim | solution.py:261
  1.5 15.7 %all-to-all-start = ((bf16[16,2,4,1024]{3,2,1,0:T(4,128)(2,1)}), bf16[16,2,4,1024]{3,2,1,0:T(4,128)(2,1)S(1)}, u32[]{:S(2)}, u32[]{:S(2)}) async-start(bf16[16,2,4,1024]{3,2,1,0:T(4,128)(2,1)} %broadcast_in_dim.2), calls=%async_computation | async-start | bytes 524288 | tf_op jit(solution)/shard_map/all_to_all | solution.py:244
  17.3 0.0 copy-start.1
  17.3 0.9 copy-done.1
  18.2 0.3 raw_order.1
  18.6 4.6 %collective-permute-start.2 = (bf16[32,4096]{1,0:T(8,128)(2,1)S(1)}, bf16[32,4096]{1,0:T(8,128)(2,1)S(1)}, u32[]{:S(2)}, u32[]{:S(2)}) collective-permute-start(bf16[32,4096]{1,0:T(8,128)(2,1)S(1)} %raw_order.1), channel_id=1, source_target_pairs={{0,48},{16,32},{32,16},{48,0},{1,49},{17,33},{33,17},{49,1},{2,50}... | collective-permute-start | bytes 786440 | tf_op jit(solution)/shard_map/ppermute | solution.py:240
  23.2 2.3 %collective-permute-start.1 = (bf16[32,4096]{1,0:T(8,128)(2,1)S(1)}, bf16[32,4096]{1,0:T(8,128)(2,1)S(1)}, u32[]{:S(2)}, u32[]{:S(2)}) collective-permute-start(bf16[32,4096]{1,0:T(8,128)(2,1)S(1)} %raw_order.1), channel_id=1, source_target_pairs={{0,32},{16,48},{32,0},{48,16},{1,33},{17,49},{33,1},{49,17},{2,34}... | collective-permute-start | bytes 786440 | tf_op jit(solution)/shard_map/ppermute | solution.py:240
  25.5 2.1 %collective-permute-start = (bf16[32,4096]{1,0:T(8,128)(2,1)S(1)}, bf16[32,4096]{1,0:T(8,128)(2,1)S(1)}, u32[]{:S(2)}, u32[]{:S(2)}) collective-permute-start(bf16[32,4096]{1,0:T(8,128)(2,1)S(1)} %raw_order.1), channel_id=1, source_target_pairs={{0,16},{16,0},{32,48},{48,32},{1,17},{17,1},{33,49},{49,33},{2,18}... | collective-permute-start | bytes 786440 | tf_op jit(solution)/shard_map/ppermute | solution.py:240
  27.6 2.8 %all-to-all-done.filter_ref = bf16[16,2,4,1024]{3,2,1,0:T(4,128)(2,1)S(1)} async-done(((bf16[16,2,4,1024]{3,2,1,0:T(4,128)(2,1)}), bf16[16,2,4,1024]{3,2,1,0:T(4,128)(2,1)S(1)}, u32[]{:S(2)}, u32[]{:S(2)}) %all-to-all-start) | async-done | bytes 262176 | tf_op jit(solution)/shard_map/all_to_all | solution.py:244
  30.4 1.8 %pick_bins.1 = bf16[4,8,144,128]{3,2,1,0:T(8,128)(2,1)} custom-call(bf16[16,2,4,1024]{3,2,1,0:T(4,128)(2,1)S(1)} %all-to-all-done.filter_ref), custom_call_target="tpu_custom_call" | custom-call | tf_op jit(solution)/shard_map/pick_bins/pallas_call | solution.py:263
  32.2 0.0 copy-start.6
  32.3 0.0 copy-start.4
  32.3 13.4 %all-to-all-start.1 = ((bf16[32,144,128]{2,1,0:T(8,128)(2,1)}), bf16[32,144,128]{2,1,0:T(8,128)(2,1)S(1)}, u32[]{:S(2)}, u32[]{:S(2)}) async-start(bf16[32,144,128]{2,1,0:T(8,128)(2,1)} %bitcast.2), calls=%async_computation.1 | async-start | bytes 2359296 | tf_op jit(solution)/shard_map/all_to_all | solution.py:244
  45.7 0.0 collective-permute-done.2
  45.7 0.0 collective-permute-done.1
  45.7 0.0 collective-permute-done
  45.7 0.1 pad_maximum_fusion.own_ref
  45.8 2.1 %collective-permute-start.3 = (bf16[128,4096]{1,0:T(8,128)(2,1)S(1)}, bf16[128,4096]{1,0:T(8,128)(2,1)S(1)}, u32[]{:S(2)}, u32[]{:S(2)}) collective-permute-start(bf16[128,4096]{1,0:T(8,128)(2,1)S(1)} %pad_maximum_fusion.own_ref), channel_id=1, source_target_pairs={{0,8},{8,0},{1,9},{9,1},{2,10},{10,2},{3,11},{11,3},{4,12},{12,4},... | collective-permute-start | bytes 3145736 | tf_op jit(solution)/shard_map/ppermute | solution.py:240
  48.0 4.4 %band.1.band_far = bf16[8,512,512]{2,1,0:T(8,128)(2,1)S(1)} custom-call(s32[8,1,256]{2,1,0:T(1,128)S(1)} %reshape.134.offset_ref, f32[8,2,2,8,256]{4,3,2,1,0:T(8,128)S(1)} %bitcast.13), custom_call_target="tpu_custom_call" | custom-call | tf_op jit(solution)/shard_map/band/pallas_call | solution.py:279
  52.5 1.9 %copy-done = bf16[8,512,512]{2,1,0:T(8,128)(2,1)} copy-done((bf16[8,512,512]{2,1,0:T(8,128)(2,1)}, bf16[8,512,512]{2,1,0:T(8,128)(2,1)S(1)}, u32[]{:S(2)}) %copy-start) | copy-done | bytes 4194328
  54.4 9.6 %all-to-all-done.1.filter_ref = bf16[32,144,128]{2,1,0:T(8,128)(2,1)S(1)} async-done(((bf16[32,144,128]{2,1,0:T(8,128)(2,1)}), bf16[32,144,128]{2,1,0:T(8,128)(2,1)S(1)}, u32[]{:S(2)}, u32[]{:S(2)}) %all-to-all-start.1) | async-done | bytes 1179680 | tf_op jit(solution)/shard_map/all_to_all | solution.py:244
  64.0 0.0 collective-permute-done.3.other_ref
  64.0 2.0 %compress.1 = bf16[16,24,256]{2,1,0:T(8,128)(2,1)} custom-call(bf16[32,144,128]{2,1,0:T(8,128)(2,1)S(1)} %all-to-all-done.1.filter_ref, bf16[128,4096]{1,0:T(8,128)(2,1)S(1)} %pad_maximum_fusion.own_ref, bf16[128,4096]{1,0:T(8,128)(2,1)S(1)} %collective-permute-done.3.other_ref), custom_call_target="tpu_custom_call" | custom-call | tf_op jit(solution)/shard_map/compress/pallas_call | solution.py:296
  66.1 5.5 %all-to-all-start.2 = ((bf16[16,24,256]{2,1,0:T(8,128)(2,1)}), bf16[16,24,256]{2,1,0:T(8,128)(2,1)S(1)}, u32[]{:S(2)}, u32[]{:S(2)}) async-start(bf16[16,24,256]{2,1,0:T(8,128)(2,1)} %compress.1), calls=%async_computation.2 | async-start | bytes 393216 | tf_op jit(solution)/shard_map/all_to_all | solution.py:244
  71.6 0.1 reshape.139.mix_ref
  71.7 1.1 %fusion.1 = (bf16[1,256,256]{2,1,0:T(8,128)(2,1)S(1)}, bf16[1,256,256]{2,1,0:T(8,128)(2,1)S(1)}) fusion(f32[256]{0:T(256)S(1)} %convert_add_fusion, f32[256]{0:T(256)S(1)} %copy-done.7), kind=kLoop, calls=%fused_computation.4 | loop fusion | flops 327680 | bytes 264192 | tf_op jit(solution)/shard_map/convert
  72.9 0.5 operator.1.operator_ref
  73.4 12.7 %all-to-all-done.2 = bf16[16,24,256]{2,1,0:T(8,128)(2,1)S(1)} async-done(((bf16[16,24,256]{2,1,0:T(8,128)(2,1)}), bf16[16,24,256]{2,1,0:T(8,128)(2,1)S(1)}, u32[]{:S(2)}, u32[]{:S(2)}) %all-to-all-start.2) | async-done | bytes 196640 | tf_op jit(solution)/shard_map/all_to_all | solution.py:244
  86.0 4.3 %merge.1 = bf16[16,16,256]{2,1,0:T(8,128)(2,1)} custom-call(s32[1]{0:T(128)} %bitcast.1.me_ref, bf16[384,256]{1,0:T(8,128)(2,1)S(1)} %bitcast.14, bf16[2,256,512]{2,1,0:T(8,128)(2,1)S(1)} %operator.1.operator_ref, bf16[8,512,512]{2,1,0:T(8,128)(2,1)} %copy-done), custom_call_target="tpu_custom_call" | custom-call | tf_op jit(solution)/shard_map/merge/pallas_call | solution.py:325
  90.4 5.0 %all-to-all-start.3 = ((bf16[16,16,256]{2,1,0:T(8,128)(2,1)}), bf16[16,16,256]{2,1,0:T(8,128)(2,1)S(1)}, u32[]{:S(2)}, u32[]{:S(2)}) async-start(bf16[16,16,256]{2,1,0:T(8,128)(2,1)} %merge.1), calls=%async_computation.3 | async-start | bytes 262144 | tf_op jit(solution)/shard_map/all_to_all | solution.py:244
  95.4 6.2 %all-to-all-done.3.power_ref = bf16[16,16,256]{2,1,0:T(8,128)(2,1)S(1)} async-done(((bf16[16,16,256]{2,1,0:T(8,128)(2,1)}), bf16[16,16,256]{2,1,0:T(8,128)(2,1)S(1)}, u32[]{:S(2)}, u32[]{:S(2)}) %all-to-all-start.3) | async-done | bytes 131104 | tf_op jit(solution)/shard_map/all_to_all | solution.py:244
  101.6 0.9 despeckle.1
  (16 shorter events, 0.1 us)
Async XLA Ops:
  1.5 28.9 %all-to-all-start = ((bf16[16,2,4,1024]{3,2,1,0:T(4,128)(2,1)}), bf16[16,2,4,1024]{3,2,1,0:T(4,128)(2,1)S(1)}, u32[]{:S(2)}, u32[]{:S(2)}) async-start(bf16[16,2,4,1024]{3,2,1,0:T(4,128)(2,1)} %broadcast_in_dim.2), calls=%async_computation | async-start | bytes 524288 | tf_op jit(solution)/shard_map/all_to_all | solution.py:244
  17.3 1.0 copy-start.1
  18.6 27.1 %collective-permute-start.2 = (bf16[32,4096]{1,0:T(8,128)(2,1)S(1)}, bf16[32,4096]{1,0:T(8,128)(2,1)S(1)}, u32[]{:S(2)}, u32[]{:S(2)}) collective-permute-start(bf16[32,4096]{1,0:T(8,128)(2,1)S(1)} %raw_order.1), channel_id=1, source_target_pairs={{0,48},{16,32},{32,16},{48,0},{1,49},{17,33},{33,17},{49,1},{2,50}... | collective-permute-start | bytes 786440 | tf_op jit(solution)/shard_map/ppermute | solution.py:240
  23.2 22.5 %collective-permute-start.1 = (bf16[32,4096]{1,0:T(8,128)(2,1)S(1)}, bf16[32,4096]{1,0:T(8,128)(2,1)S(1)}, u32[]{:S(2)}, u32[]{:S(2)}) collective-permute-start(bf16[32,4096]{1,0:T(8,128)(2,1)S(1)} %raw_order.1), channel_id=1, source_target_pairs={{0,32},{16,48},{32,0},{48,16},{1,33},{17,49},{33,1},{49,17},{2,34}... | collective-permute-start | bytes 786440 | tf_op jit(solution)/shard_map/ppermute | solution.py:240
  25.5 20.2 %collective-permute-start = (bf16[32,4096]{1,0:T(8,128)(2,1)S(1)}, bf16[32,4096]{1,0:T(8,128)(2,1)S(1)}, u32[]{:S(2)}, u32[]{:S(2)}) collective-permute-start(bf16[32,4096]{1,0:T(8,128)(2,1)S(1)} %raw_order.1), channel_id=1, source_target_pairs={{0,16},{16,0},{32,48},{48,32},{1,17},{17,1},{33,49},{49,33},{2,18}... | collective-permute-start | bytes 786440 | tf_op jit(solution)/shard_map/ppermute | solution.py:240
  32.2 15.7 %copy-start.6 = (s32[4,512]{1,0:T(4,128)S(1)}, s32[4,512]{1,0:T(4,128)}, u32[]{:S(2)}) copy-start(s32[4,512]{1,0:T(4,128)} %param.12) | copy-start | bytes 24580
  32.3 15.7 %copy-start.4 = (f32[4,2,2,512,8]{3,4,2,1,0:T(8,128)S(1)}, f32[4,2,2,512,8]{3,4,2,1,0:T(8,128)}, u32[]{:S(2)}) copy-start(f32[4,2,2,512,8]{3,4,2,1,0:T(8,128)} %param.13) | copy-start | bytes 786436
  32.3 31.8 %all-to-all-start.1 = ((bf16[32,144,128]{2,1,0:T(8,128)(2,1)}), bf16[32,144,128]{2,1,0:T(8,128)(2,1)S(1)}, u32[]{:S(2)}, u32[]{:S(2)}) async-start(bf16[32,144,128]{2,1,0:T(8,128)(2,1)} %bitcast.2), calls=%async_computation.1 | async-start | bytes 2359296 | tf_op jit(solution)/shard_map/all_to_all | solution.py:244
  45.8 18.2 %collective-permute-start.3 = (bf16[128,4096]{1,0:T(8,128)(2,1)S(1)}, bf16[128,4096]{1,0:T(8,128)(2,1)S(1)}, u32[]{:S(2)}, u32[]{:S(2)}) collective-permute-start(bf16[128,4096]{1,0:T(8,128)(2,1)S(1)} %pad_maximum_fusion.own_ref), channel_id=1, source_target_pairs={{0,8},{8,0},{1,9},{9,1},{2,10},{10,2},{3,11},{11,3},{4,12},{12,4},... | collective-permute-start | bytes 3145736 | tf_op jit(solution)/shard_map/ppermute | solution.py:240
  52.5 1.9 %copy-start = (bf16[8,512,512]{2,1,0:T(8,128)(2,1)}, bf16[8,512,512]{2,1,0:T(8,128)(2,1)S(1)}, u32[]{:S(2)}) copy-start(bf16[8,512,512]{2,1,0:T(8,128)(2,1)S(1)} %band.1.band_far) | copy-start | bytes 12582916
  54.4 17.1 %copy-start.5 = (f32[2,32,8,8]{1,3,2,0:T(8,128)S(1)}, f32[2,32,8,8]{1,3,2,0:T(8,128)}, u32[]{:S(2)}) copy-start(f32[2,32,8,8]{1,3,2,0:T(8,128)} %param.10) | copy-start | bytes 49156
  54.4 17.3 %copy-start.7 = (f32[256]{0:T(256)S(1)}, f32[256]{0:T(256)}, u32[]{:S(2)}) copy-start(f32[256]{0:T(256)} %param.11) | copy-start | bytes 3076
  54.4 18.5 %copy-start.2 = (f32[2,32,256]{2,1,0:T(8,128)S(1)}, f32[2,32,256]{2,1,0:T(8,128)}, u32[]{:S(2)}) copy-start(f32[2,32,256]{2,1,0:T(8,128)} %constant.23.clone.dop_ref) | copy-start | bytes 196612
  66.1 20.0 %all-to-all-start.2 = ((bf16[16,24,256]{2,1,0:T(8,128)(2,1)}), bf16[16,24,256]{2,1,0:T(8,128)(2,1)S(1)}, u32[]{:S(2)}, u32[]{:S(2)}) async-start(bf16[16,24,256]{2,1,0:T(8,128)(2,1)} %compress.1), calls=%async_computation.2 | async-start | bytes 393216 | tf_op jit(solution)/shard_map/all_to_all | solution.py:244
  86.0 15.5 %copy-start.3 = (f32[256]{0:T(256)S(1)}, f32[256]{0:T(256)}, u32[]{:S(2)}) copy-start(f32[256]{0:T(256)} %param.14) | copy-start | bytes 3076
  90.4 11.2 %all-to-all-start.3 = ((bf16[16,16,256]{2,1,0:T(8,128)(2,1)}), bf16[16,16,256]{2,1,0:T(8,128)(2,1)S(1)}, u32[]{:S(2)}, u32[]{:S(2)}) async-start(bf16[16,16,256]{2,1,0:T(8,128)(2,1)} %merge.1), calls=%async_computation.3 | async-start | bytes 262144 | tf_op jit(solution)/shard_map/all_to_all | solution.py:244

commit v6 on v5

--- a/solution.py
+++ b/solution.py
@@ -20,9 +20,11 @@
 ROW = 8
 CUT = 9
 PAD = 16
-SENT = 24
-HALO = 8
+SENT = 40
+HALO = 4
 COLS = GROUP * CUT
+LOWER = 8 * CUT
+PICKED = LOWER + 64
 REVERSED = [8 * (m & 1) + 4 * (m >> 1 & 1) + 2 * (m >> 2 & 1) + (m >> 3) for m in range(GROUP)]
 AXES = ("zh", "x1", "x0", "y", "core", "chan")
 SUB = ("zh", "x1", "x0", "y", "core")
@@ -81,13 +83,14 @@
             at = part * 64 + z * 4
             ordered[at : at + 4, :] = filter_ref[z, part].astype(F32)
     rows = ordered[...].astype(BF)
-    bins = iota((COLS, 1024), 1)
-    r = iota((COLS, 1024), 0)
+    r, k = iota((LOWER, 1024), 0), iota((64, 1024), 0)
     dest = r // CUT
-    first = 128 * (dest & 7) - HALO + 8 * CUT * (dest >> 3) + r - dest * CUT
+    lower = iota((LOWER, 1024), 1) - (128 * dest - HALO + r - dest * CUT)
+    upper = iota((64, 1024), 1) - (128 * (k >> 3) - HALO + LOWER + (k & 7))
     copies = []
     for g in range(ROW):
-        pick = jnp.where(bins == first + CUT * g, 1.0, 0.0).astype(BF)
+        hits = [jnp.where(lower == CUT * g, 1.0, 0.0), jnp.where(upper == 8 * g, 1.0, 0.0)]
+        pick = jnp.concatenate(hits, axis=0).astype(BF)
         picked[g] = dot_t(pick, rows).astype(BF)
         for x in range(4):
             copy = pltpu.make_async_copy(picked.at[g], out_far.at[x, g], sems.at[x, g])
@@ -109,13 +112,20 @@
         [jnp.concatenate(first, axis=1), jnp.concatenate(second, axis=1)], axis=0
     )
     summed = dot_t(left, pulses[...])
-    row, col = iota((32 * GROUP, 2 * COLS), 0), iota((32 * GROUP, 2 * COLS), 1)
+    row, col = iota((32 * GROUP, 2 * PICKED), 0), iota((32 * GROUP, 2 * PICKED), 1)
     within = row & 31
-    source = (row >> 5) * CUT + jnp.where(within >= CUT, within - CUT + COLS, within)
-    order = jnp.where((col == source) & (within < 2 * CUT), 1.0, 0.0).astype(BF)
-    moved = dot(order, summed.astype(BF)).astype(BF)
+    j = jnp.where(within >= CUT, within - CUT, within)
+    c = (row >> 5) & 7
+    upper = row >= 8 * 32
+    source = jnp.where(upper, LOWER + 8 * c, CUT * c) + j
+    source = jnp.where(within >= CUT, source + PICKED, source)
+    held = (within < 2 * CUT) & ((j < 8) | ~upper)
+    order = jnp.where((col == source) & held, 1.0, 0.0).astype(BF)
+    moved = dot(order, summed.astype(BF))
+    rest = jnp.zeros((SENT - 4 * CUT, 128), F32)
     for dest in range(GROUP):
-        out_ref[dest] = moved[dest * 32 : dest * 32 + SENT]
+        block = moved[dest * 32 : dest * 32 + 2 * CUT]
+        out_ref[dest] = jnp.concatenate([block[:, :128], block[:, 128:], rest], axis=0).astype(BF)
 
 
 def operator_body(mix_ref, dop_ref, beam_ref, out_ref):
@@ -164,15 +174,13 @@
     apart = comp_ref[...].astype(F32)
     for x in range(2):
         for part in range(2):
-            blocks = []
-            for c in range(CHAN):
-                at = (x * 8 + c) * SENT + part * CUT
-                blocks.append(apart[at : at + CUT])
             for q in range(8):
                 n = x * 8 + (((q & 3) * 2 + (q >> 2)) ^ me)
-                pulses[part, n, :CUT, :] = jnp.concatenate(
-                    [b[:, q * 32 : (q + 1) * 32] for b in blocks], axis=1
-                )
+                blocks = []
+                for c in range(CHAN):
+                    at = (x * 8 + c) * SENT + (q >> 2) * 2 * CUT + part * CUT
+                    blocks.append(apart[at : at + CUT, (q & 3) * 32 : (q & 3) * 32 + 32])
+                pulses[part, n, :CUT, :] = jnp.concatenate(blocks, axis=1)
     pulse = pulses[...].reshape(2 * GROUP * PAD, 256).astype(BF)
     formed = dot(pulse, operator_ref[0]) + dot(pulse, operator_ref[1])
     half = GROUP * PAD
@@ -213,14 +221,15 @@
 
 def despeckle_body(chan_ref, power_ref, rate_ref, out_ref, bins):
     for t in range(GROUP):
-        bins[t * CUT : (t + 1) * CUT, :] = power_ref[t].astype(F32)[:CUT]
+        at, count = (t * CUT, CUT) if t < 8 else (LOWER + (t - 8) * 8, 8)
+        bins[at : at + count, :] = power_ref[t].astype(F32)[:count]
     current = bins[...]
-    cell = iota((COLS, ANG), 0) + (chan_ref[0] * 128 - HALO)
+    cell = iota((PICKED, ANG), 0) + (chan_ref[0] * 128 - HALO)
     inside = (cell >= 0) & (cell < 1024)
-    rate = jnp.broadcast_to(rate_ref[...], (COLS, ANG))
+    rate = jnp.broadcast_to(rate_ref[...], (PICKED, ANG))
     for _ in range(PASSES):
         before = pltpu.roll(current, 1, 0)
-        after = pltpu.roll(current, COLS - 1, 0)
+        after = pltpu.roll(current, PICKED - 1, 0)
         current = jnp.where(inside, current + rate * (before - 2.0 * current + after), 0.0)
     out_ref[...] = current[HALO : HALO + 128, :].T
 
@@ -262,18 +271,18 @@
     rows = exchange(rows, ALONG_Z)
     picked = pl.pallas_call(
         pick_body,
-        out_shape=jax.ShapeDtypeStruct((4, ROW, COLS, 128), BF),
+        out_shape=jax.ShapeDtypeStruct((4, ROW, PICKED, 128), BF),
         in_specs=[WHOLE],
         out_specs=LEFT,
         scratch_shapes=[
             pltpu.VMEM((128, 1024), F32),
-            pltpu.VMEM((ROW, COLS, 128), BF),
+            pltpu.VMEM((ROW, PICKED, 128), BF),
             pltpu.SemaphoreType.DMA((4, ROW)),
         ],
         compiler_params=params(8),
         name="pick_bins",
     )(rows)
-    filters = exchange(picked.reshape(32, COLS, 128), PLANE)
+    filters = exchange(picked.reshape(32, PICKED, 128), PLANE)
 
     weights = band_weights.reshape(LEVELS, 2, 2, 2, ANG, BAND).transpose(0, 3, 1, 2, 5, 4)
     band = pl.pallas_call(
@@ -295,7 +304,7 @@
     filters, band = lax.optimization_barrier((filters, band))
     compressed = pl.pallas_call(
         compress_body,
-        out_shape=jax.ShapeDtypeStruct((GROUP, SENT, 256), BF),
+        out_shape=jax.ShapeDtypeStruct((GROUP, SENT, 128), BF),
         in_specs=[WHOLE] * 3,
         out_specs=WHOLE,
         scratch_shapes=[pltpu.VMEM((256, 4096), BF)],
@@ -334,7 +343,7 @@
         ],
         compiler_params=params(52),
         name="merge",
-    )(me, compressed.reshape(GROUP * SENT, 256), operator, band)
+    )(me, compressed.reshape(GROUP * SENT, 128), operator, band)
     power = exchange(power, MERGE)
     chan = lax.axis_index("chan").astype(jnp.int32).reshape(1)
     return pl.pallas_call(
@@ -342,7 +351,7 @@
         out_shape=jax.ShapeDtypeStruct((ANG, 128), F32),
         in_specs=[SCALAR] + [WHOLE] * 2,
         out_specs=WHOLE,
-        scratch_shapes=[pltpu.VMEM((COLS, ANG), F32)],
+        scratch_shapes=[pltpu.VMEM((PICKED, ANG), F32)],
         compiler_params=params(4),
         name="despeckle",
     )(chan, power, smoothing.reshape(1, ANG))

time: 103 us -> 101 us (0.981)
  waiting for transfers between devices: 31.3 us -> 29.6 us
    all_to_all x4, waiting for transfers between devices: 31.3 us -> 29.6 us  [exchange(): return lax.all_to_all(value, axes, split_axis=0, concat_axis=0, tiled=True)]
where the time goes in v6:
time: 101 us
  starting transfers between devices  50.7 us (50%)
  waiting for transfers between devices  29.6 us (29%)
  Pallas kernels  14.2 us (14%)
  local copies, waits for them, and re-layouts  4.57 us (5%)
  other arithmetic  1.27 us (1%)
    all_to_all x4, starting transfers between devices, exchange(): return lax.all_to_all(value, axes, split_axis=0, concat_axis=0, tiled=True)  39.6 us
    all_to_all x4, waiting for transfers between devices, exchange(): return lax.all_to_all(value, axes, split_axis=0, concat_axis=0, tiled=True)  29.6 us
    ppermute x4, starting transfers between devices, flipped(): return lax.ppermute(value, axis, pairs)  11.2 us
    pallas_call x1, Pallas kernels, local(): pl.pallas_call(band_body, grid=(2 * LEVELS,), out_shape=jax.ShapeDtypeStr...  4.45 us
    pallas_call x1, Pallas kernels, local(): pl.pallas_call(merge_body, out_shape=jax.ShapeDtypeStruct((GROUP, PAD, AN...  4.24 us
    unnamed x16, local copies, waits for them, and re-layouts  2.91 us
  transfers between devices with their start and end apart: 8, of which 4 were waited for; matrix products, arithmetic and copies ran while one was open for 1% of the time, Pallas kernels for 7%

profile of v6, /device:TPU:1, one launch (start us, length us, event | category | flops | bytes accessed | tf_op | source)
XLA Modules:
  0.0 100.6 jit_solution(10410998418128449987)
XLA Ops:
  0.0 1.5 %broadcast_in_dim.2 = bf16[16,2,4,1024]{3,2,1,0:T(4,128)(2,1)} broadcast(bf16[2,4,1024]{2,1,0:T(4,128)(2,1)} %param.9), dimensions={1,2,3} | broadcast | bytes 278528 | tf_op jit(solution)/shard_map/broadcast_in_dim | solution.py:270
  1.5 15.7 %all-to-all-start = ((bf16[16,2,4,1024]{3,2,1,0:T(4,128)(2,1)}), bf16[16,2,4,1024]{3,2,1,0:T(4,128)(2,1)S(1)}, u32[]{:S(2)}, u32[]{:S(2)}) async-start(bf16[16,2,4,1024]{3,2,1,0:T(4,128)(2,1)} %broadcast_in_dim.2), calls=%async_computation | async-start | bytes 524288 | tf_op jit(solution)/shard_map/all_to_all | solution.py:253
  17.3 0.0 copy-start.1
  17.3 0.9 copy-done.1
  18.2 0.3 raw_order.1
  18.6 4.6 %collective-permute-start.2 = (bf16[32,4096]{1,0:T(8,128)(2,1)S(1)}, bf16[32,4096]{1,0:T(8,128)(2,1)S(1)}, u32[]{:S(2)}, u32[]{:S(2)}) collective-permute-start(bf16[32,4096]{1,0:T(8,128)(2,1)S(1)} %raw_order.1), channel_id=1, source_target_pairs={{0,48},{16,32},{32,16},{48,0},{1,49},{17,33},{33,17},{49,1},{2,50}... | collective-permute-start | bytes 786440 | tf_op jit(solution)/shard_map/ppermute | solution.py:249
  23.2 2.3 %collective-permute-start.1 = (bf16[32,4096]{1,0:T(8,128)(2,1)S(1)}, bf16[32,4096]{1,0:T(8,128)(2,1)S(1)}, u32[]{:S(2)}, u32[]{:S(2)}) collective-permute-start(bf16[32,4096]{1,0:T(8,128)(2,1)S(1)} %raw_order.1), channel_id=1, source_target_pairs={{0,32},{16,48},{32,0},{48,16},{1,33},{17,49},{33,1},{49,17},{2,34}... | collective-permute-start | bytes 786440 | tf_op jit(solution)/shard_map/ppermute | solution.py:249
  25.5 2.1 %collective-permute-start = (bf16[32,4096]{1,0:T(8,128)(2,1)S(1)}, bf16[32,4096]{1,0:T(8,128)(2,1)S(1)}, u32[]{:S(2)}, u32[]{:S(2)}) collective-permute-start(bf16[32,4096]{1,0:T(8,128)(2,1)S(1)} %raw_order.1), channel_id=1, source_target_pairs={{0,16},{16,0},{32,48},{48,32},{1,17},{17,1},{33,49},{49,33},{2,18}... | collective-permute-start | bytes 786440 | tf_op jit(solution)/shard_map/ppermute | solution.py:249
  27.6 2.8 %all-to-all-done.filter_ref = bf16[16,2,4,1024]{3,2,1,0:T(4,128)(2,1)S(1)} async-done(((bf16[16,2,4,1024]{3,2,1,0:T(4,128)(2,1)}), bf16[16,2,4,1024]{3,2,1,0:T(4,128)(2,1)S(1)}, u32[]{:S(2)}, u32[]{:S(2)}) %all-to-all-start) | async-done | bytes 262176 | tf_op jit(solution)/shard_map/all_to_all | solution.py:253
  30.4 1.8 %pick_bins.1 = bf16[4,8,136,128]{3,2,1,0:T(8,128)(2,1)} custom-call(bf16[16,2,4,1024]{3,2,1,0:T(4,128)(2,1)S(1)} %all-to-all-done.filter_ref), custom_call_target="tpu_custom_call" | custom-call | tf_op jit(solution)/shard_map/pick_bins/pallas_call | solution.py:272
  32.2 0.0 copy-start.6
  32.3 0.0 copy-start.4
  32.3 13.4 %all-to-all-start.1 = ((bf16[32,136,128]{2,1,0:T(8,128)(2,1)}), bf16[32,136,128]{2,1,0:T(8,128)(2,1)S(1)}, u32[]{:S(2)}, u32[]{:S(2)}) async-start(bf16[32,136,128]{2,1,0:T(8,128)(2,1)} %bitcast.2), calls=%async_computation.1 | async-start | bytes 2228224 | tf_op jit(solution)/shard_map/all_to_all | solution.py:253
  45.7 0.0 collective-permute-done.2
  45.7 0.0 collective-permute-done.1
  45.7 0.0 collective-permute-done
  45.7 0.1 pad_maximum_fusion.own_ref
  45.8 2.1 %collective-permute-start.3 = (bf16[128,4096]{1,0:T(8,128)(2,1)S(1)}, bf16[128,4096]{1,0:T(8,128)(2,1)S(1)}, u32[]{:S(2)}, u32[]{:S(2)}) collective-permute-start(bf16[128,4096]{1,0:T(8,128)(2,1)S(1)} %pad_maximum_fusion.own_ref), channel_id=1, source_target_pairs={{0,8},{8,0},{1,9},{9,1},{2,10},{10,2},{3,11},{11,3},{4,12},{12,4},... | collective-permute-start | bytes 3145736 | tf_op jit(solution)/shard_map/ppermute | solution.py:249
  48.0 4.4 %band.1.band_far = bf16[8,512,512]{2,1,0:T(8,128)(2,1)S(1)} custom-call(s32[8,1,256]{2,1,0:T(1,128)S(1)} %reshape.134.offset_ref, f32[8,2,2,8,256]{4,3,2,1,0:T(8,128)S(1)} %bitcast.13), custom_call_target="tpu_custom_call" | custom-call | tf_op jit(solution)/shard_map/band/pallas_call | solution.py:288
  52.5 1.9 %copy-done = bf16[8,512,512]{2,1,0:T(8,128)(2,1)} copy-done((bf16[8,512,512]{2,1,0:T(8,128)(2,1)}, bf16[8,512,512]{2,1,0:T(8,128)(2,1)S(1)}, u32[]{:S(2)}) %copy-start) | copy-done | bytes 4194328
  54.4 8.9 %all-to-all-done.1.filter_ref = bf16[32,136,128]{2,1,0:T(8,128)(2,1)S(1)} async-done(((bf16[32,136,128]{2,1,0:T(8,128)(2,1)}), bf16[32,136,128]{2,1,0:T(8,128)(2,1)S(1)}, u32[]{:S(2)}, u32[]{:S(2)}) %all-to-all-start.1) | async-done | bytes 1114144 | tf_op jit(solution)/shard_map/all_to_all | solution.py:253
  63.3 0.0 collective-permute-done.3.other_ref
  63.3 2.0 %compress.1 = bf16[16,40,128]{2,1,0:T(8,128)(2,1)} custom-call(bf16[32,136,128]{2,1,0:T(8,128)(2,1)S(1)} %all-to-all-done.1.filter_ref, bf16[128,4096]{1,0:T(8,128)(2,1)S(1)} %pad_maximum_fusion.own_ref, bf16[128,4096]{1,0:T(8,128)(2,1)S(1)} %collective-permute-done.3.other_ref), custom_call_target="tpu_custom_call" | custom-call | tf_op jit(solution)/shard_map/compress/pallas_call | solution.py:305
  65.3 5.5 %all-to-all-start.2 = ((bf16[16,40,128]{2,1,0:T(8,128)(2,1)}), bf16[16,40,128]{2,1,0:T(8,128)(2,1)S(1)}, u32[]{:S(2)}, u32[]{:S(2)}) async-start(bf16[16,40,128]{2,1,0:T(8,128)(2,1)} %compress.1), calls=%async_computation.2 | async-start | bytes 327680 | tf_op jit(solution)/shard_map/all_to_all | solution.py:253
  70.9 0.1 reshape.139.mix_ref
  71.0 1.1 %fusion.1 = (bf16[1,256,256]{2,1,0:T(8,128)(2,1)S(1)}, bf16[1,256,256]{2,1,0:T(8,128)(2,1)S(1)}) fusion(f32[256]{0:T(256)S(1)} %convert_add_fusion, f32[256]{0:T(256)S(1)} %copy-done.7), kind=kLoop, calls=%fused_computation.4 | loop fusion | flops 327680 | bytes 264192 | tf_op jit(solution)/shard_map/convert
  72.2 0.5 operator.1.operator_ref
  72.6 11.7 %all-to-all-done.2 = bf16[16,40,128]{2,1,0:T(8,128)(2,1)S(1)} async-done(((bf16[16,40,128]{2,1,0:T(8,128)(2,1)}), bf16[16,40,128]{2,1,0:T(8,128)(2,1)S(1)}, u32[]{:S(2)}, u32[]{:S(2)}) %all-to-all-start.2) | async-done | bytes 163872 | tf_op jit(solution)/shard_map/all_to_all | solution.py:253
  84.3 4.2 %merge.1 = bf16[16,16,256]{2,1,0:T(8,128)(2,1)} custom-call(s32[1]{0:T(128)} %bitcast.1.me_ref, bf16[640,128]{1,0:T(8,128)(2,1)S(1)} %bitcast.14, bf16[2,256,512]{2,1,0:T(8,128)(2,1)S(1)} %operator.1.operator_ref, bf16[8,512,512]{2,1,0:T(8,128)(2,1)} %copy-done), custom_call_target="tpu_custom_call" | custom-call | tf_op jit(solution)/shard_map/merge/pallas_call | solution.py:334
  88.6 4.9 %all-to-all-start.3 = ((bf16[16,16,256]{2,1,0:T(8,128)(2,1)}), bf16[16,16,256]{2,1,0:T(8,128)(2,1)S(1)}, u32[]{:S(2)}, u32[]{:S(2)}) async-start(bf16[16,16,256]{2,1,0:T(8,128)(2,1)} %merge.1), calls=%async_computation.3 | async-start | bytes 262144 | tf_op jit(solution)/shard_map/all_to_all | solution.py:253
  93.5 6.2 %all-to-all-done.3.power_ref = bf16[16,16,256]{2,1,0:T(8,128)(2,1)S(1)} async-done(((bf16[16,16,256]{2,1,0:T(8,128)(2,1)}), bf16[16,16,256]{2,1,0:T(8,128)(2,1)S(1)}, u32[]{:S(2)}, u32[]{:S(2)}) %all-to-all-start.3) | async-done | bytes 131104 | tf_op jit(solution)/shard_map/all_to_all | solution.py:253
  99.7 0.9 despeckle.1
  (16 shorter events, 0.1 us)
Async XLA Ops:
  1.5 28.9 %all-to-all-start = ((bf16[16,2,4,1024]{3,2,1,0:T(4,128)(2,1)}), bf16[16,2,4,1024]{3,2,1,0:T(4,128)(2,1)S(1)}, u32[]{:S(2)}, u32[]{:S(2)}) async-start(bf16[16,2,4,1024]{3,2,1,0:T(4,128)(2,1)} %broadcast_in_dim.2), calls=%async_computation | async-start | bytes 524288 | tf_op jit(solution)/shard_map/all_to_all | solution.py:253
  17.3 1.0 copy-start.1
  18.6 27.1 %collective-permute-start.2 = (bf16[32,4096]{1,0:T(8,128)(2,1)S(1)}, bf16[32,4096]{1,0:T(8,128)(2,1)S(1)}, u32[]{:S(2)}, u32[]{:S(2)}) collective-permute-start(bf16[32,4096]{1,0:T(8,128)(2,1)S(1)} %raw_order.1), channel_id=1, source_target_pairs={{0,48},{16,32},{32,16},{48,0},{1,49},{17,33},{33,17},{49,1},{2,50}... | collective-permute-start | bytes 786440 | tf_op jit(solution)/shard_map/ppermute | solution.py:249
  23.2 22.5 %collective-permute-start.1 = (bf16[32,4096]{1,0:T(8,128)(2,1)S(1)}, bf16[32,4096]{1,0:T(8,128)(2,1)S(1)}, u32[]{:S(2)}, u32[]{:S(2)}) collective-permute-start(bf16[32,4096]{1,0:T(8,128)(2,1)S(1)} %raw_order.1), channel_id=1, source_target_pairs={{0,32},{16,48},{32,0},{48,16},{1,33},{17,49},{33,1},{49,17},{2,34}... | collective-permute-start | bytes 786440 | tf_op jit(solution)/shard_map/ppermute | solution.py:249
  25.5 20.2 %collective-permute-start = (bf16[32,4096]{1,0:T(8,128)(2,1)S(1)}, bf16[32,4096]{1,0:T(8,128)(2,1)S(1)}, u32[]{:S(2)}, u32[]{:S(2)}) collective-permute-start(bf16[32,4096]{1,0:T(8,128)(2,1)S(1)} %raw_order.1), channel_id=1, source_target_pairs={{0,16},{16,0},{32,48},{48,32},{1,17},{17,1},{33,49},{49,33},{2,18}... | collective-permute-start | bytes 786440 | tf_op jit(solution)/shard_map/ppermute | solution.py:249
  32.2 15.7 %copy-start.6 = (s32[4,512]{1,0:T(4,128)S(1)}, s32[4,512]{1,0:T(4,128)}, u32[]{:S(2)}) copy-start(s32[4,512]{1,0:T(4,128)} %param.12) | copy-start | bytes 24580
  32.3 15.7 %copy-start.4 = (f32[4,2,2,512,8]{3,4,2,1,0:T(8,128)S(1)}, f32[4,2,2,512,8]{3,4,2,1,0:T(8,128)}, u32[]{:S(2)}) copy-start(f32[4,2,2,512,8]{3,4,2,1,0:T(8,128)} %param.13) | copy-start | bytes 786436
  32.3 31.1 %all-to-all-start.1 = ((bf16[32,136,128]{2,1,0:T(8,128)(2,1)}), bf16[32,136,128]{2,1,0:T(8,128)(2,1)S(1)}, u32[]{:S(2)}, u32[]{:S(2)}) async-start(bf16[32,136,128]{2,1,0:T(8,128)(2,1)} %bitcast.2), calls=%async_computation.1 | async-start | bytes 2228224 | tf_op jit(solution)/shard_map/all_to_all | solution.py:253
  45.8 17.5 %collective-permute-start.3 = (bf16[128,4096]{1,0:T(8,128)(2,1)S(1)}, bf16[128,4096]{1,0:T(8,128)(2,1)S(1)}, u32[]{:S(2)}, u32[]{:S(2)}) collective-permute-start(bf16[128,4096]{1,0:T(8,128)(2,1)S(1)} %pad_maximum_fusion.own_ref), channel_id=1, source_target_pairs={{0,8},{8,0},{1,9},{9,1},{2,10},{10,2},{3,11},{11,3},{4,12},{12,4},... | collective-permute-start | bytes 3145736 | tf_op jit(solution)/shard_map/ppermute | solution.py:249
  52.5 1.9 %copy-start = (bf16[8,512,512]{2,1,0:T(8,128)(2,1)}, bf16[8,512,512]{2,1,0:T(8,128)(2,1)S(1)}, u32[]{:S(2)}) copy-start(bf16[8,512,512]{2,1,0:T(8,128)(2,1)S(1)} %band.1.band_far) | copy-start | bytes 12582916
  54.4 16.4 %copy-start.5 = (f32[2,32,8,8]{1,3,2,0:T(8,128)S(1)}, f32[2,32,8,8]{1,3,2,0:T(8,128)}, u32[]{:S(2)}) copy-start(f32[2,32,8,8]{1,3,2,0:T(8,128)} %param.10) | copy-start | bytes 49156
  54.4 16.5 %copy-start.7 = (f32[256]{0:T(256)S(1)}, f32[256]{0:T(256)}, u32[]{:S(2)}) copy-start(f32[256]{0:T(256)} %param.11) | copy-start | bytes 3076
  54.4 17.7 %copy-start.2 = (f32[2,32,256]{2,1,0:T(8,128)S(1)}, f32[2,32,256]{2,1,0:T(8,128)}, u32[]{:S(2)}) copy-start(f32[2,32,256]{2,1,0:T(8,128)} %constant.23.clone.dop_ref) | copy-start | bytes 196612
  65.3 19.0 %all-to-all-start.2 = ((bf16[16,40,128]{2,1,0:T(8,128)(2,1)}), bf16[16,40,128]{2,1,0:T(8,128)(2,1)S(1)}, u32[]{:S(2)}, u32[]{:S(2)}) async-start(bf16[16,40,128]{2,1,0:T(8,128)(2,1)} %compress.1), calls=%async_computation.2 | async-start | bytes 327680 | tf_op jit(solution)/shard_map/all_to_all | solution.py:253
  84.3 15.4 %copy-start.3 = (f32[256]{0:T(256)S(1)}, f32[256]{0:T(256)}, u32[]{:S(2)}) copy-start(f32[256]{0:T(256)} %param.14) | copy-start | bytes 3076
  88.6 11.1 %all-to-all-start.3 = ((bf16[16,16,256]{2,1,0:T(8,128)(2,1)}), bf16[16,16,256]{2,1,0:T(8,128)(2,1)S(1)}, u32[]{:S(2)}, u32[]{:S(2)}) async-start(bf16[16,16,256]{2,1,0:T(8,128)(2,1)} %merge.1), calls=%async_computation.3 | async-start | bytes 262144 | tf_op jit(solution)/shard_map/all_to_all | solution.py:253

commit v7 on v6

--- a/solution.py
+++ b/solution.py
@@ -77,6 +77,17 @@
         out_ref[:, u * 512 : (u + 1) * 512] = moved[u * 32 : (u + 1) * 32]
 
 
+def copies_body(filter_far, out_far, rows, sem, sems):
+    first = pltpu.make_async_copy(filter_far, rows, sem)
+    first.start()
+    first.wait()
+    copies = [pltpu.make_async_copy(rows, out_far.at[z], sems.at[z]) for z in range(16)]
+    for copy in copies:
+        copy.start()
+    for copy in copies:
+        copy.wait()
+
+
 def pick_body(filter_ref, out_far, ordered, picked, sems):
     for z in range(16):
         for part in range(2):
@@ -181,15 +192,12 @@
                     at = (x * 8 + c) * SENT + (q >> 2) * 2 * CUT + part * CUT
                     blocks.append(apart[at : at + CUT, (q & 3) * 32 : (q & 3) * 32 + 32])
                 pulses[part, n, :CUT, :] = jnp.concatenate(blocks, axis=1)
-    pulse = pulses[...].reshape(2 * GROUP * PAD, 256).astype(BF)
+    pulse = jnp.concatenate(
+        [pulses[part, n, :CUT, :] for part in range(2) for n in REVERSED], axis=0
+    ).astype(BF)
     formed = dot(pulse, operator_ref[0]) + dot(pulse, operator_ref[1])
-    half = GROUP * PAD
-    real = formed[:half, :ANG] - formed[half:, ANG:]
-    imag = formed[half:, :ANG] + formed[:half, ANG:]
-    real, imag = [
-        jnp.concatenate([part[n * PAD : n * PAD + CUT] for n in REVERSED], axis=0)
-        for part in (real, imag)
-    ]
+    real = formed[:COLS, :ANG] - formed[COLS:, ANG:]
+    imag = formed[COLS:, :ANG] + formed[:COLS, ANG:]
     half = COLS // 2
     for level in range(LEVELS):
         block = COLS >> level
@@ -267,7 +275,19 @@
     own = jnp.concatenate([raw] + [flipped(raw, "y", mask) for mask in (1, 2, 3)], axis=0)
     other = flipped(own, "core", 1)
 
-    rows = jnp.broadcast_to(range_filter[None], (16, *range_filter.shape))
+    rows = pl.pallas_call(
+        copies_body,
+        out_shape=jax.ShapeDtypeStruct((16, 2, 4, 1024), BF),
+        in_specs=[LEFT],
+        out_specs=LEFT,
+        scratch_shapes=[
+            pltpu.VMEM((2, 4, 1024), BF),
+            pltpu.SemaphoreType.DMA,
+            pltpu.SemaphoreType.DMA((16,)),
+        ],
+        compiler_params=params(60),
+        name="copies",
+    )(range_filter)
     rows = exchange(rows, ALONG_Z)
     picked = pl.pallas_call(
         pick_body,

time: 101 us -> 101 us (level)
  Pallas kernels: 14.2 us -> 15.5 us
    pallas_call x0 -> x1, Pallas kernels: none -> 1.56 us  [local(): pl.pallas_call(copies_body, out_shape=jax.ShapeDtypeStruct((16, 2, 4, 102...]
    broadcast_in_dim x1 -> x0, local copies, waits for them, and re-layouts: 1.52 us -> none  [local(): rows = jnp.broadcast_to(range_filter[None], (16, *range_filter.shape))]
    unnamed x16 -> x14, local copies, waits for them, and re-layouts: 2.91 us -> 2.91 us
  transfers between devices with their start and end apart: 8 -> 8, of which waited for: 4 -> 4; matrix products, arithmetic and copies ran while one was open for 1% -> 2% of each run, Pallas kernels for 7% -> 7%
where the time goes in v7:
time: 101 us; the launch traced here: 100 us
  starting transfers between devices  50.6 us (50%)
  waiting for transfers between devices  28.6 us (28%)
  Pallas kernels  15.5 us (15%)
  local copies, waits for them, and re-layouts  4 us (4%)
  other arithmetic  1.27 us (1%)
    all_to_all x4, starting transfers between devices, exchange(): return lax.all_to_all(value, axes, split_axis=0, concat_axis=0, tiled=True)  39.5 us
    all_to_all x4, waiting for transfers between devices, exchange(): return lax.all_to_all(value, axes, split_axis=0, concat_axis=0, tiled=True)  28.6 us
    ppermute x4, starting transfers between devices, flipped(): return lax.ppermute(value, axis, pairs)  11.2 us
    pallas_call x1, Pallas kernels, local(): pl.pallas_call(band_body, grid=(2 * LEVELS,), out_shape=jax.ShapeDtypeStr...  4.45 us
    pallas_call x1, Pallas kernels, local(): pl.pallas_call(merge_body, out_shape=jax.ShapeDtypeStruct((GROUP, PAD, AN...  4.05 us
    unnamed x14, local copies, waits for them, and re-layouts  2.91 us
  transfers between devices with their start and end apart: 8, of which 4 were waited for; matrix products, arithmetic and copies ran while one was open for 2% of the time, Pallas kernels for 7%

profile of v7, /device:TPU:1, one launch (start us, length us, event | category | flops | bytes accessed | tf_op | source)
XLA Modules:
  0.0 100.3 jit_solution(11616457479989590080)
XLA Ops:
  0.0 1.6 %copies.1 = bf16[16,2,4,1024]{3,2,1,0:T(4,128)(2,1)} custom-call(bf16[2,4,1024]{2,1,0:T(4,128)(2,1)} %filter_far.1), custom_call_target="tpu_custom_call" | custom-call | tf_op jit(solution)/shard_map/copies/pallas_call | solution.py:278
  1.6 15.8 %all-to-all-start = ((bf16[16,2,4,1024]{3,2,1,0:T(4,128)(2,1)}), bf16[16,2,4,1024]{3,2,1,0:T(4,128)(2,1)S(1)}, u32[]{:S(2)}, u32[]{:S(2)}) async-start(bf16[16,2,4,1024]{3,2,1,0:T(4,128)(2,1)} %copies.1), calls=%async_computation | async-start | bytes 524288 | tf_op jit(solution)/shard_map/all_to_all | solution.py:261
  17.3 0.0 copy-start.1
  17.3 0.9 copy-done.1
  18.3 0.3 raw_order.1
  18.6 4.6 %collective-permute-start.2 = (bf16[32,4096]{1,0:T(8,128)(2,1)S(1)}, bf16[32,4096]{1,0:T(8,128)(2,1)S(1)}, u32[]{:S(2)}, u32[]{:S(2)}) collective-permute-start(bf16[32,4096]{1,0:T(8,128)(2,1)S(1)} %raw_order.1), channel_id=1, source_target_pairs={{0,48},{16,32},{32,16},{48,0},{1,49},{17,33},{33,17},{49,1},{2,50}... | collective-permute-start | bytes 786440 | tf_op jit(solution)/shard_map/ppermute | solution.py:257
  23.3 2.3 %collective-permute-start.1 = (bf16[32,4096]{1,0:T(8,128)(2,1)S(1)}, bf16[32,4096]{1,0:T(8,128)(2,1)S(1)}, u32[]{:S(2)}, u32[]{:S(2)}) collective-permute-start(bf16[32,4096]{1,0:T(8,128)(2,1)S(1)} %raw_order.1), channel_id=1, source_target_pairs={{0,32},{16,48},{32,0},{48,16},{1,33},{17,49},{33,1},{49,17},{2,34}... | collective-permute-start | bytes 786440 | tf_op jit(solution)/shard_map/ppermute | solution.py:257
  25.5 2.1 %collective-permute-start = (bf16[32,4096]{1,0:T(8,128)(2,1)S(1)}, bf16[32,4096]{1,0:T(8,128)(2,1)S(1)}, u32[]{:S(2)}, u32[]{:S(2)}) collective-permute-start(bf16[32,4096]{1,0:T(8,128)(2,1)S(1)} %raw_order.1), channel_id=1, source_target_pairs={{0,16},{16,0},{32,48},{48,32},{1,17},{17,1},{33,49},{49,33},{2,18}... | collective-permute-start | bytes 786440 | tf_op jit(solution)/shard_map/ppermute | solution.py:257
  27.7 2.8 %all-to-all-done.filter_ref = bf16[16,2,4,1024]{3,2,1,0:T(4,128)(2,1)S(1)} async-done(((bf16[16,2,4,1024]{3,2,1,0:T(4,128)(2,1)}), bf16[16,2,4,1024]{3,2,1,0:T(4,128)(2,1)S(1)}, u32[]{:S(2)}, u32[]{:S(2)}) %all-to-all-start) | async-done | bytes 262176 | tf_op jit(solution)/shard_map/all_to_all | solution.py:261
  30.5 1.8 %pick_bins.1 = bf16[4,8,136,128]{3,2,1,0:T(8,128)(2,1)} custom-call(bf16[16,2,4,1024]{3,2,1,0:T(4,128)(2,1)S(1)} %all-to-all-done.filter_ref), custom_call_target="tpu_custom_call" | custom-call | tf_op jit(solution)/shard_map/pick_bins/pallas_call | solution.py:292
  32.3 0.0 copy-start.5
  32.3 13.3 %all-to-all-start.1 = ((bf16[32,136,128]{2,1,0:T(8,128)(2,1)}), bf16[32,136,128]{2,1,0:T(8,128)(2,1)S(1)}, u32[]{:S(2)}, u32[]{:S(2)}) async-start(bf16[32,136,128]{2,1,0:T(8,128)(2,1)} %bitcast.2), calls=%async_computation.1 | async-start | bytes 2228224 | tf_op jit(solution)/shard_map/all_to_all | solution.py:261
  45.6 0.0 collective-permute-done.2
  45.6 0.0 collective-permute-done.1
  45.6 0.0 collective-permute-done
  45.6 0.1 pad_maximum_fusion.own_ref
  45.7 2.1 %collective-permute-start.3 = (bf16[128,4096]{1,0:T(8,128)(2,1)S(1)}, bf16[128,4096]{1,0:T(8,128)(2,1)S(1)}, u32[]{:S(2)}, u32[]{:S(2)}) collective-permute-start(bf16[128,4096]{1,0:T(8,128)(2,1)S(1)} %pad_maximum_fusion.own_ref), channel_id=1, source_target_pairs={{0,8},{8,0},{1,9},{9,1},{2,10},{10,2},{3,11},{11,3},{4,12},{12,4},... | collective-permute-start | bytes 3145736 | tf_op jit(solution)/shard_map/ppermute | solution.py:257
  47.9 1.0 copy.9
  48.9 4.4 %band.1.band_far = bf16[8,512,512]{2,1,0:T(8,128)(2,1)S(1)} custom-call(s32[8,1,256]{2,1,0:T(1,128)S(1)} %reshape.133.offset_ref, f32[8,2,2,8,256]{4,3,2,1,0:T(8,128)S(1)} %bitcast.13), custom_call_target="tpu_custom_call" | custom-call | tf_op jit(solution)/shard_map/band/pallas_call | solution.py:308
  53.3 1.9 %copy-done = bf16[8,512,512]{2,1,0:T(8,128)(2,1)} copy-done((bf16[8,512,512]{2,1,0:T(8,128)(2,1)}, bf16[8,512,512]{2,1,0:T(8,128)(2,1)S(1)}, u32[]{:S(2)}) %copy-start) | copy-done | bytes 4194328
  55.3 7.9 %all-to-all-done.1.filter_ref = bf16[32,136,128]{2,1,0:T(8,128)(2,1)S(1)} async-done(((bf16[32,136,128]{2,1,0:T(8,128)(2,1)}), bf16[32,136,128]{2,1,0:T(8,128)(2,1)S(1)}, u32[]{:S(2)}, u32[]{:S(2)}) %all-to-all-start.1) | async-done | bytes 1114144 | tf_op jit(solution)/shard_map/all_to_all | solution.py:261
  63.2 0.0 collective-permute-done.3.other_ref
  63.2 2.0 %compress.1 = bf16[16,40,128]{2,1,0:T(8,128)(2,1)} custom-call(bf16[32,136,128]{2,1,0:T(8,128)(2,1)S(1)} %all-to-all-done.1.filter_ref, bf16[128,4096]{1,0:T(8,128)(2,1)S(1)} %pad_maximum_fusion.own_ref, bf16[128,4096]{1,0:T(8,128)(2,1)S(1)} %collective-permute-done.3.other_ref), custom_call_target="tpu_custom_call" | custom-call | tf_op jit(solution)/shard_map/compress/pallas_call | solution.py:325
  65.2 5.5 %all-to-all-start.2 = ((bf16[16,40,128]{2,1,0:T(8,128)(2,1)}), bf16[16,40,128]{2,1,0:T(8,128)(2,1)S(1)}, u32[]{:S(2)}, u32[]{:S(2)}) async-start(bf16[16,40,128]{2,1,0:T(8,128)(2,1)} %compress.1), calls=%async_computation.2 | async-start | bytes 327680 | tf_op jit(solution)/shard_map/all_to_all | solution.py:261
  70.7 0.1 reshape.138.mix_ref
  70.8 1.1 %fusion.1 = (bf16[1,256,256]{2,1,0:T(8,128)(2,1)S(1)}, bf16[1,256,256]{2,1,0:T(8,128)(2,1)S(1)}) fusion(f32[256]{0:T(256)S(1)} %convert_add_fusion, f32[256]{0:T(256)S(1)} %copy-done.6), kind=kLoop, calls=%fused_computation.4 | loop fusion | flops 327680 | bytes 264192 | tf_op jit(solution)/shard_map/convert
  72.0 0.5 operator.1.operator_ref
  72.5 11.7 %all-to-all-done.2 = bf16[16,40,128]{2,1,0:T(8,128)(2,1)S(1)} async-done(((bf16[16,40,128]{2,1,0:T(8,128)(2,1)}), bf16[16,40,128]{2,1,0:T(8,128)(2,1)S(1)}, u32[]{:S(2)}, u32[]{:S(2)}) %all-to-all-start.2) | async-done | bytes 163872 | tf_op jit(solution)/shard_map/all_to_all | solution.py:261
  84.2 4.0 %merge.1 = bf16[16,16,256]{2,1,0:T(8,128)(2,1)} custom-call(s32[1]{0:T(128)} %bitcast.1.me_ref, bf16[640,128]{1,0:T(8,128)(2,1)S(1)} %bitcast.14, bf16[2,256,512]{2,1,0:T(8,128)(2,1)S(1)} %operator.1.operator_ref, bf16[8,512,512]{2,1,0:T(8,128)(2,1)} %copy-done), custom_call_target="tpu_custom_call" | custom-call | tf_op jit(solution)/shard_map/merge/pallas_call | solution.py:354
  88.2 4.9 %all-to-all-start.3 = ((bf16[16,16,256]{2,1,0:T(8,128)(2,1)}), bf16[16,16,256]{2,1,0:T(8,128)(2,1)S(1)}, u32[]{:S(2)}, u32[]{:S(2)}) async-start(bf16[16,16,256]{2,1,0:T(8,128)(2,1)} %merge.1), calls=%async_computation.3 | async-start | bytes 262144 | tf_op jit(solution)/shard_map/all_to_all | solution.py:261
  93.2 6.2 %all-to-all-done.3.power_ref = bf16[16,16,256]{2,1,0:T(8,128)(2,1)S(1)} async-done(((bf16[16,16,256]{2,1,0:T(8,128)(2,1)}), bf16[16,16,256]{2,1,0:T(8,128)(2,1)S(1)}, u32[]{:S(2)}, u32[]{:S(2)}) %all-to-all-start.3) | async-done | bytes 131104 | tf_op jit(solution)/shard_map/all_to_all | solution.py:261
  99.4 0.9 despeckle.1
  (14 shorter events, 0.1 us)
Async XLA Ops:
  1.6 28.9 %all-to-all-start = ((bf16[16,2,4,1024]{3,2,1,0:T(4,128)(2,1)}), bf16[16,2,4,1024]{3,2,1,0:T(4,128)(2,1)S(1)}, u32[]{:S(2)}, u32[]{:S(2)}) async-start(bf16[16,2,4,1024]{3,2,1,0:T(4,128)(2,1)} %copies.1), calls=%async_computation | async-start | bytes 524288 | tf_op jit(solution)/shard_map/all_to_all | solution.py:261
  17.3 1.0 copy-start.1
  18.6 27.0 %collective-permute-start.2 = (bf16[32,4096]{1,0:T(8,128)(2,1)S(1)}, bf16[32,4096]{1,0:T(8,128)(2,1)S(1)}, u32[]{:S(2)}, u32[]{:S(2)}) collective-permute-start(bf16[32,4096]{1,0:T(8,128)(2,1)S(1)} %raw_order.1), channel_id=1, source_target_pairs={{0,48},{16,32},{32,16},{48,0},{1,49},{17,33},{33,17},{49,1},{2,50}... | collective-permute-start | bytes 786440 | tf_op jit(solution)/shard_map/ppermute | solution.py:257
  23.3 22.3 %collective-permute-start.1 = (bf16[32,4096]{1,0:T(8,128)(2,1)S(1)}, bf16[32,4096]{1,0:T(8,128)(2,1)S(1)}, u32[]{:S(2)}, u32[]{:S(2)}) collective-permute-start(bf16[32,4096]{1,0:T(8,128)(2,1)S(1)} %raw_order.1), channel_id=1, source_target_pairs={{0,32},{16,48},{32,0},{48,16},{1,33},{17,49},{33,1},{49,17},{2,34}... | collective-permute-start | bytes 786440 | tf_op jit(solution)/shard_map/ppermute | solution.py:257
  25.5 20.1 %collective-permute-start = (bf16[32,4096]{1,0:T(8,128)(2,1)S(1)}, bf16[32,4096]{1,0:T(8,128)(2,1)S(1)}, u32[]{:S(2)}, u32[]{:S(2)}) collective-permute-start(bf16[32,4096]{1,0:T(8,128)(2,1)S(1)} %raw_order.1), channel_id=1, source_target_pairs={{0,16},{16,0},{32,48},{48,32},{1,17},{17,1},{33,49},{49,33},{2,18}... | collective-permute-start | bytes 786440 | tf_op jit(solution)/shard_map/ppermute | solution.py:257
  32.3 15.6 %copy-start.5 = (s32[4,512]{1,0:T(4,128)S(1)}, s32[4,512]{1,0:T(4,128)}, u32[]{:S(2)}) copy-start(s32[4,512]{1,0:T(4,128)} %param.12) | copy-start | bytes 24580
  32.3 30.9 %all-to-all-start.1 = ((bf16[32,136,128]{2,1,0:T(8,128)(2,1)}), bf16[32,136,128]{2,1,0:T(8,128)(2,1)S(1)}, u32[]{:S(2)}, u32[]{:S(2)}) async-start(bf16[32,136,128]{2,1,0:T(8,128)(2,1)} %bitcast.2), calls=%async_computation.1 | async-start | bytes 2228224 | tf_op jit(solution)/shard_map/all_to_all | solution.py:261
  45.7 17.5 %collective-permute-start.3 = (bf16[128,4096]{1,0:T(8,128)(2,1)S(1)}, bf16[128,4096]{1,0:T(8,128)(2,1)S(1)}, u32[]{:S(2)}, u32[]{:S(2)}) collective-permute-start(bf16[128,4096]{1,0:T(8,128)(2,1)S(1)} %pad_maximum_fusion.own_ref), channel_id=1, source_target_pairs={{0,8},{8,0},{1,9},{9,1},{2,10},{10,2},{3,11},{11,3},{4,12},{12,4},... | collective-permute-start | bytes 3145736 | tf_op jit(solution)/shard_map/ppermute | solution.py:257
  53.3 2.0 %copy-start = (bf16[8,512,512]{2,1,0:T(8,128)(2,1)}, bf16[8,512,512]{2,1,0:T(8,128)(2,1)S(1)}, u32[]{:S(2)}) copy-start(bf16[8,512,512]{2,1,0:T(8,128)(2,1)S(1)} %band.1.band_far) | copy-start | bytes 12582916
  55.3 15.4 %copy-start.4 = (f32[2,32,8,8]{1,3,2,0:T(8,128)S(1)}, f32[2,32,8,8]{1,3,2,0:T(8,128)}, u32[]{:S(2)}) copy-start(f32[2,32,8,8]{1,3,2,0:T(8,128)} %param.10) | copy-start | bytes 49156
  55.3 15.6 %copy-start.6 = (f32[256]{0:T(256)S(1)}, f32[256]{0:T(256)}, u32[]{:S(2)}) copy-start(f32[256]{0:T(256)} %param.11) | copy-start | bytes 3076
  55.3 16.8 %copy-start.2 = (f32[2,32,256]{2,1,0:T(8,128)S(1)}, f32[2,32,256]{2,1,0:T(8,128)}, u32[]{:S(2)}) copy-start(f32[2,32,256]{2,1,0:T(8,128)} %constant.23.clone.dop_ref) | copy-start | bytes 196612
  65.2 19.0 %all-to-all-start.2 = ((bf16[16,40,128]{2,1,0:T(8,128)(2,1)}), bf16[16,40,128]{2,1,0:T(8,128)(2,1)S(1)}, u32[]{:S(2)}, u32[]{:S(2)}) async-start(bf16[16,40,128]{2,1,0:T(8,128)(2,1)} %compress.1), calls=%async_computation.2 | async-start | bytes 327680 | tf_op jit(solution)/shard_map/all_to_all | solution.py:261
  84.2 15.2 %copy-start.3 = (f32[256]{0:T(256)S(1)}, f32[256]{0:T(256)}, u32[]{:S(2)}) copy-start(f32[256]{0:T(256)} %param.14) | copy-start | bytes 3076
  88.2 11.1 %all-to-all-start.3 = ((bf16[16,16,256]{2,1,0:T(8,128)(2,1)}), bf16[16,16,256]{2,1,0:T(8,128)(2,1)S(1)}, u32[]{:S(2)}, u32[]{:S(2)}) async-start(bf16[16,16,256]{2,1,0:T(8,128)(2,1)} %merge.1), calls=%async_computation.3 | async-start | bytes 262144 | tf_op jit(solution)/shard_map/all_to_all | solution.py:261

commit v8 on v7

--- a/solution.py
+++ b/solution.py
@@ -169,9 +169,11 @@
                 value = jnp.zeros((strip, ANG), F32)
                 for j in range(BAND):
                     value = jnp.where(hits[j], weight_ref[0, c, part, j : j + 1, :], value)
-                out_ref[
-                    0, c * ANG + start : c * ANG + start + strip, part * ANG : (part + 1) * ANG
-                ] = value.astype(BF)
+                rows = slice(c * ANG + start, c * ANG + start + strip)
+                lanes = slice(part * ANG, (part + 1) * ANG)
+                top = value.astype(BF)
+                out_ref[0, 0, rows, lanes] = top
+                out_ref[0, 1, rows, lanes] = (value - top.astype(F32)).astype(BF)
 
 
 def merge_body(me_ref, comp_ref, operator_ref, band_far, out_ref, pulses, band, sems):
@@ -215,8 +217,8 @@
         reals, imags = [], []
         copies[level].wait()
         for h in range(2):
-            weight = band[2 * level + h]
-            out = dot(top, weight) + dot(rest, weight)
+            weight = band[2 * level + h, 0]
+            out = dot(top, weight) + dot(rest, weight) + dot(top, band[2 * level + h, 1])
             reals.append(out[:half, :ANG] - out[half:, ANG:])
             imags.append(out[half:, :ANG] + out[:half, ANG:])
         real = jnp.concatenate(reals, axis=0)
@@ -308,13 +310,13 @@
     band = pl.pallas_call(
         band_body,
         grid=(2 * LEVELS,),
-        out_shape=jax.ShapeDtypeStruct((2 * LEVELS, 2 * ANG, 2 * ANG), BF),
+        out_shape=jax.ShapeDtypeStruct((2 * LEVELS, 2, 2 * ANG, 2 * ANG), BF),
         in_specs=[
             pl.BlockSpec((1, 1, ANG), lambda i: (i, 0, 0)),
             pl.BlockSpec((1, 2, 2, BAND, ANG), lambda i: (i, 0, 0, 0, 0)),
         ],
-        out_specs=pl.BlockSpec((1, 2 * ANG, 2 * ANG), lambda i: (i, 0, 0)),
-        compiler_params=params(4),
+        out_specs=pl.BlockSpec((1, 2, 2 * ANG, 2 * ANG), lambda i: (i, 0, 0, 0)),
+        compiler_params=params(6),
         name="band",
     )(
         band_offsets.reshape(2 * LEVELS, 1, ANG),
@@ -358,7 +360,7 @@
         out_specs=WHOLE,
         scratch_shapes=[
             pltpu.VMEM((2, GROUP, PAD, 256), F32),
-            pltpu.VMEM((2 * LEVELS, 2 * ANG, 2 * ANG), BF),
+            pltpu.VMEM((2 * LEVELS, 2, 2 * ANG, 2 * ANG), BF),
             pltpu.SemaphoreType.DMA((LEVELS,)),
         ],
         compiler_params=params(52),

time: 101 us -> 102 us (level)
  waiting for transfers between devices: 28.6 us -> 26.6 us
  Pallas kernels: 15.5 us -> 17.2 us
  local copies, waits for them, and re-layouts: 4 us -> 5.29 us
    all_to_all x4, waiting for transfers between devices: 28.6 us -> 26.5 us  [exchange(): return lax.all_to_all(value, axes, split_axis=0, concat_axis=0, tiled=True)]
    unnamed x14, local copies, waits for them, and re-layouts: 2.91 us -> 4.2 us
  transfers between devices with their start and end apart: 8 -> 8, of which waited for: 4 -> 4; matrix products, arithmetic and copies ran while one was open for 2% -> 2% of each run, Pallas kernels for 7% -> 8%
where the time goes in v8:
time: 102 us; the launch traced here: 101 us
  starting transfers between devices  50.6 us (50%)
  waiting for transfers between devices  26.6 us (26%)
  Pallas kernels  17.2 us (17%)
  local copies, waits for them, and re-layouts  5.29 us (5%)
  other arithmetic  1.27 us (1%)
    all_to_all x4, starting transfers between devices, exchange(): return lax.all_to_all(value, axes, split_axis=0, concat_axis=0, tiled=True)  39.4 us
    all_to_all x4, waiting for transfers between devices, exchange(): return lax.all_to_all(value, axes, split_axis=0, concat_axis=0, tiled=True)  26.5 us
    ppermute x4, starting transfers between devices, flipped(): return lax.ppermute(value, axis, pairs)  11.2 us
    pallas_call x1, Pallas kernels, local(): pl.pallas_call(band_body, grid=(2 * LEVELS,), out_shape=jax.ShapeDtypeStr...  5.24 us
    pallas_call x1, Pallas kernels, local(): pl.pallas_call(merge_body, out_shape=jax.ShapeDtypeStruct((GROUP, PAD, AN...  4.93 us
    unnamed x14, local copies, waits for them, and re-layouts  4.2 us
  transfers between devices with their start and end apart: 8, of which 4 were waited for; matrix products, arithmetic and copies ran while one was open for 2% of the time, Pallas kernels for 8%

profile of v8, /device:TPU:1, one launch (start us, length us, event | category | flops | bytes accessed | tf_op | source)
XLA Modules:
  0.0 101.2 jit_solution(16263768176522644931)
XLA Ops:
  0.0 1.6 %copies.1 = bf16[16,2,4,1024]{3,2,1,0:T(4,128)(2,1)} custom-call(bf16[2,4,1024]{2,1,0:T(4,128)(2,1)} %filter_far.1), custom_call_target="tpu_custom_call" | custom-call | tf_op jit(solution)/shard_map/copies/pallas_call | solution.py:280
  1.6 15.8 %all-to-all-start = ((bf16[16,2,4,1024]{3,2,1,0:T(4,128)(2,1)}), bf16[16,2,4,1024]{3,2,1,0:T(4,128)(2,1)S(1)}, u32[]{:S(2)}, u32[]{:S(2)}) async-start(bf16[16,2,4,1024]{3,2,1,0:T(4,128)(2,1)} %copies.1), calls=%async_computation | async-start | bytes 524288 | tf_op jit(solution)/shard_map/all_to_all | solution.py:263
  17.3 0.0 copy-start.1
  17.3 0.9 copy-done.1
  18.3 0.3 raw_order.1
  18.6 4.6 %collective-permute-start.2 = (bf16[32,4096]{1,0:T(8,128)(2,1)S(1)}, bf16[32,4096]{1,0:T(8,128)(2,1)S(1)}, u32[]{:S(2)}, u32[]{:S(2)}) collective-permute-start(bf16[32,4096]{1,0:T(8,128)(2,1)S(1)} %raw_order.1), channel_id=1, source_target_pairs={{0,48},{16,32},{32,16},{48,0},{1,49},{17,33},{33,17},{49,1},{2,50}... | collective-permute-start | bytes 786440 | tf_op jit(solution)/shard_map/ppermute | solution.py:259
  23.3 2.3 %collective-permute-start.1 = (bf16[32,4096]{1,0:T(8,128)(2,1)S(1)}, bf16[32,4096]{1,0:T(8,128)(2,1)S(1)}, u32[]{:S(2)}, u32[]{:S(2)}) collective-permute-start(bf16[32,4096]{1,0:T(8,128)(2,1)S(1)} %raw_order.1), channel_id=1, source_target_pairs={{0,32},{16,48},{32,0},{48,16},{1,33},{17,49},{33,1},{49,17},{2,34}... | collective-permute-start | bytes 786440 | tf_op jit(solution)/shard_map/ppermute | solution.py:259
  25.5 2.1 %collective-permute-start = (bf16[32,4096]{1,0:T(8,128)(2,1)S(1)}, bf16[32,4096]{1,0:T(8,128)(2,1)S(1)}, u32[]{:S(2)}, u32[]{:S(2)}) collective-permute-start(bf16[32,4096]{1,0:T(8,128)(2,1)S(1)} %raw_order.1), channel_id=1, source_target_pairs={{0,16},{16,0},{32,48},{48,32},{1,17},{17,1},{33,49},{49,33},{2,18}... | collective-permute-start | bytes 786440 | tf_op jit(solution)/shard_map/ppermute | solution.py:259
  27.7 2.8 %all-to-all-done.filter_ref = bf16[16,2,4,1024]{3,2,1,0:T(4,128)(2,1)S(1)} async-done(((bf16[16,2,4,1024]{3,2,1,0:T(4,128)(2,1)}), bf16[16,2,4,1024]{3,2,1,0:T(4,128)(2,1)S(1)}, u32[]{:S(2)}, u32[]{:S(2)}) %all-to-all-start) | async-done | bytes 262176 | tf_op jit(solution)/shard_map/all_to_all | solution.py:263
  30.5 1.8 %pick_bins.1 = bf16[4,8,136,128]{3,2,1,0:T(8,128)(2,1)} custom-call(bf16[16,2,4,1024]{3,2,1,0:T(4,128)(2,1)S(1)} %all-to-all-done.filter_ref), custom_call_target="tpu_custom_call" | custom-call | tf_op jit(solution)/shard_map/pick_bins/pallas_call | solution.py:294
  32.3 0.0 copy-start.5
  32.3 13.3 %all-to-all-start.1 = ((bf16[32,136,128]{2,1,0:T(8,128)(2,1)}), bf16[32,136,128]{2,1,0:T(8,128)(2,1)S(1)}, u32[]{:S(2)}, u32[]{:S(2)}) async-start(bf16[32,136,128]{2,1,0:T(8,128)(2,1)} %bitcast.2), calls=%async_computation.1 | async-start | bytes 2228224 | tf_op jit(solution)/shard_map/all_to_all | solution.py:263
  45.6 0.0 collective-permute-done.2
  45.6 0.0 collective-permute-done.1
  45.6 0.0 collective-permute-done
  45.6 0.1 pad_maximum_fusion.own_ref
  45.7 2.1 %collective-permute-start.3 = (bf16[128,4096]{1,0:T(8,128)(2,1)S(1)}, bf16[128,4096]{1,0:T(8,128)(2,1)S(1)}, u32[]{:S(2)}, u32[]{:S(2)}) collective-permute-start(bf16[128,4096]{1,0:T(8,128)(2,1)S(1)} %pad_maximum_fusion.own_ref), channel_id=1, source_target_pairs={{0,8},{8,0},{1,9},{9,1},{2,10},{10,2},{3,11},{11,3},{4,12},{12,4},... | collective-permute-start | bytes 3145736 | tf_op jit(solution)/shard_map/ppermute | solution.py:259
  47.9 1.0 copy.9
  48.9 5.2 %band.1.band_far = bf16[8,2,512,512]{3,2,1,0:T(8,128)(2,1)S(1)} custom-call(s32[8,1,256]{2,1,0:T(1,128)S(1)} %reshape.133.offset_ref, f32[8,2,2,8,256]{4,3,2,1,0:T(8,128)S(1)} %bitcast.13), custom_call_target="tpu_custom_call" | custom-call | tf_op jit(solution)/shard_map/band/pallas_call | solution.py:310
  54.2 3.2 %copy-done = bf16[8,2,512,512]{3,2,1,0:T(8,128)(2,1)} copy-done((bf16[8,2,512,512]{3,2,1,0:T(8,128)(2,1)}, bf16[8,2,512,512]{3,2,1,0:T(8,128)(2,1)S(1)}, u32[]{:S(2)}) %copy-start) | copy-done | bytes 8388632
  57.4 5.9 %all-to-all-done.1.filter_ref = bf16[32,136,128]{2,1,0:T(8,128)(2,1)S(1)} async-done(((bf16[32,136,128]{2,1,0:T(8,128)(2,1)}), bf16[32,136,128]{2,1,0:T(8,128)(2,1)S(1)}, u32[]{:S(2)}, u32[]{:S(2)}) %all-to-all-start.1) | async-done | bytes 1114144 | tf_op jit(solution)/shard_map/all_to_all | solution.py:263
  63.3 0.0 collective-permute-done.3.other_ref
  63.3 2.0 %compress.1 = bf16[16,40,128]{2,1,0:T(8,128)(2,1)} custom-call(bf16[32,136,128]{2,1,0:T(8,128)(2,1)S(1)} %all-to-all-done.1.filter_ref, bf16[128,4096]{1,0:T(8,128)(2,1)S(1)} %pad_maximum_fusion.own_ref, bf16[128,4096]{1,0:T(8,128)(2,1)S(1)} %collective-permute-done.3.other_ref), custom_call_target="tpu_custom_call" | custom-call | tf_op jit(solution)/shard_map/compress/pallas_call | solution.py:327
  65.2 5.5 %all-to-all-start.2 = ((bf16[16,40,128]{2,1,0:T(8,128)(2,1)}), bf16[16,40,128]{2,1,0:T(8,128)(2,1)S(1)}, u32[]{:S(2)}, u32[]{:S(2)}) async-start(bf16[16,40,128]{2,1,0:T(8,128)(2,1)} %compress.1), calls=%async_computation.2 | async-start | bytes 327680 | tf_op jit(solution)/shard_map/all_to_all | solution.py:263
  70.8 0.1 reshape.138.mix_ref
  70.9 1.1 %fusion.1 = (bf16[1,256,256]{2,1,0:T(8,128)(2,1)S(1)}, bf16[1,256,256]{2,1,0:T(8,128)(2,1)S(1)}) fusion(f32[256]{0:T(256)S(1)} %convert_add_fusion, f32[256]{0:T(256)S(1)} %copy-done.6), kind=kLoop, calls=%fused_computation.4 | loop fusion | flops 327680 | bytes 264192 | tf_op jit(solution)/shard_map/convert
  72.1 0.5 operator.1.operator_ref
  72.6 11.7 %all-to-all-done.2 = bf16[16,40,128]{2,1,0:T(8,128)(2,1)S(1)} async-done(((bf16[16,40,128]{2,1,0:T(8,128)(2,1)}), bf16[16,40,128]{2,1,0:T(8,128)(2,1)S(1)}, u32[]{:S(2)}, u32[]{:S(2)}) %all-to-all-start.2) | async-done | bytes 163872 | tf_op jit(solution)/shard_map/all_to_all | solution.py:263
  84.2 4.9 %merge.1 = bf16[16,16,256]{2,1,0:T(8,128)(2,1)} custom-call(s32[1]{0:T(128)} %bitcast.1.me_ref, bf16[640,128]{1,0:T(8,128)(2,1)S(1)} %bitcast.14, bf16[2,256,512]{2,1,0:T(8,128)(2,1)S(1)} %operator.1.operator_ref, bf16[8,2,512,512]{3,2,1,0:T(8,128)(2,1)} %copy-done), custom_call_target="tpu_custom_call" | custom-call | tf_op jit(solution)/shard_map/merge/pallas_call | solution.py:356
  89.2 4.9 %all-to-all-start.3 = ((bf16[16,16,256]{2,1,0:T(8,128)(2,1)}), bf16[16,16,256]{2,1,0:T(8,128)(2,1)S(1)}, u32[]{:S(2)}, u32[]{:S(2)}) async-start(bf16[16,16,256]{2,1,0:T(8,128)(2,1)} %merge.1), calls=%async_computation.3 | async-start | bytes 262144 | tf_op jit(solution)/shard_map/all_to_all | solution.py:263
  94.1 6.2 %all-to-all-done.3.power_ref = bf16[16,16,256]{2,1,0:T(8,128)(2,1)S(1)} async-done(((bf16[16,16,256]{2,1,0:T(8,128)(2,1)}), bf16[16,16,256]{2,1,0:T(8,128)(2,1)S(1)}, u32[]{:S(2)}, u32[]{:S(2)}) %all-to-all-start.3) | async-done | bytes 131104 | tf_op jit(solution)/shard_map/all_to_all | solution.py:263
  100.3 0.9 despeckle.1
  (14 shorter events, 0.1 us)
Async XLA Ops:
  1.6 28.9 %all-to-all-start = ((bf16[16,2,4,1024]{3,2,1,0:T(4,128)(2,1)}), bf16[16,2,4,1024]{3,2,1,0:T(4,128)(2,1)S(1)}, u32[]{:S(2)}, u32[]{:S(2)}) async-start(bf16[16,2,4,1024]{3,2,1,0:T(4,128)(2,1)} %copies.1), calls=%async_computation | async-start | bytes 524288 | tf_op jit(solution)/shard_map/all_to_all | solution.py:263
  17.3 1.0 copy-start.1
  18.6 27.0 %collective-permute-start.2 = (bf16[32,4096]{1,0:T(8,128)(2,1)S(1)}, bf16[32,4096]{1,0:T(8,128)(2,1)S(1)}, u32[]{:S(2)}, u32[]{:S(2)}) collective-permute-start(bf16[32,4096]{1,0:T(8,128)(2,1)S(1)} %raw_order.1), channel_id=1, source_target_pairs={{0,48},{16,32},{32,16},{48,0},{1,49},{17,33},{33,17},{49,1},{2,50}... | collective-permute-start | bytes 786440 | tf_op jit(solution)/shard_map/ppermute | solution.py:259
  23.3 22.4 %collective-permute-start.1 = (bf16[32,4096]{1,0:T(8,128)(2,1)S(1)}, bf16[32,4096]{1,0:T(8,128)(2,1)S(1)}, u32[]{:S(2)}, u32[]{:S(2)}) collective-permute-start(bf16[32,4096]{1,0:T(8,128)(2,1)S(1)} %raw_order.1), channel_id=1, source_target_pairs={{0,32},{16,48},{32,0},{48,16},{1,33},{17,49},{33,1},{49,17},{2,34}... | collective-permute-start | bytes 786440 | tf_op jit(solution)/shard_map/ppermute | solution.py:259
  25.5 20.1 %collective-permute-start = (bf16[32,4096]{1,0:T(8,128)(2,1)S(1)}, bf16[32,4096]{1,0:T(8,128)(2,1)S(1)}, u32[]{:S(2)}, u32[]{:S(2)}) collective-permute-start(bf16[32,4096]{1,0:T(8,128)(2,1)S(1)} %raw_order.1), channel_id=1, source_target_pairs={{0,16},{16,0},{32,48},{48,32},{1,17},{17,1},{33,49},{49,33},{2,18}... | collective-permute-start | bytes 786440 | tf_op jit(solution)/shard_map/ppermute | solution.py:259
  32.3 15.6 %copy-start.5 = (s32[4,512]{1,0:T(4,128)S(1)}, s32[4,512]{1,0:T(4,128)}, u32[]{:S(2)}) copy-start(s32[4,512]{1,0:T(4,128)} %param.12) | copy-start | bytes 24580
  32.3 30.9 %all-to-all-start.1 = ((bf16[32,136,128]{2,1,0:T(8,128)(2,1)}), bf16[32,136,128]{2,1,0:T(8,128)(2,1)S(1)}, u32[]{:S(2)}, u32[]{:S(2)}) async-start(bf16[32,136,128]{2,1,0:T(8,128)(2,1)} %bitcast.2), calls=%async_computation.1 | async-start | bytes 2228224 | tf_op jit(solution)/shard_map/all_to_all | solution.py:263
  45.7 17.5 %collective-permute-start.3 = (bf16[128,4096]{1,0:T(8,128)(2,1)S(1)}, bf16[128,4096]{1,0:T(8,128)(2,1)S(1)}, u32[]{:S(2)}, u32[]{:S(2)}) collective-permute-start(bf16[128,4096]{1,0:T(8,128)(2,1)S(1)} %pad_maximum_fusion.own_ref), channel_id=1, source_target_pairs={{0,8},{8,0},{1,9},{9,1},{2,10},{10,2},{3,11},{11,3},{4,12},{12,4},... | collective-permute-start | bytes 3145736 | tf_op jit(solution)/shard_map/ppermute | solution.py:259
  54.2 3.2 %copy-start = (bf16[8,2,512,512]{3,2,1,0:T(8,128)(2,1)}, bf16[8,2,512,512]{3,2,1,0:T(8,128)(2,1)S(1)}, u32[]{:S(2)}) copy-start(bf16[8,2,512,512]{3,2,1,0:T(8,128)(2,1)S(1)} %band.1.band_far) | copy-start | bytes 25165828
  57.4 13.4 %copy-start.4 = (f32[2,32,8,8]{1,3,2,0:T(8,128)S(1)}, f32[2,32,8,8]{1,3,2,0:T(8,128)}, u32[]{:S(2)}) copy-start(f32[2,32,8,8]{1,3,2,0:T(8,128)} %param.10) | copy-start | bytes 49156
  57.4 13.5 %copy-start.6 = (f32[256]{0:T(256)S(1)}, f32[256]{0:T(256)}, u32[]{:S(2)}) copy-start(f32[256]{0:T(256)} %param.11) | copy-start | bytes 3076
  57.4 14.7 %copy-start.2 = (f32[2,32,256]{2,1,0:T(8,128)S(1)}, f32[2,32,256]{2,1,0:T(8,128)}, u32[]{:S(2)}) copy-start(f32[2,32,256]{2,1,0:T(8,128)} %constant.23.clone.dop_ref) | copy-start | bytes 196612
  65.2 19.0 %all-to-all-start.2 = ((bf16[16,40,128]{2,1,0:T(8,128)(2,1)}), bf16[16,40,128]{2,1,0:T(8,128)(2,1)S(1)}, u32[]{:S(2)}, u32[]{:S(2)}) async-start(bf16[16,40,128]{2,1,0:T(8,128)(2,1)} %compress.1), calls=%async_computation.2 | async-start | bytes 327680 | tf_op jit(solution)/shard_map/all_to_all | solution.py:263
  84.2 16.1 %copy-start.3 = (f32[256]{0:T(256)S(1)}, f32[256]{0:T(256)}, u32[]{:S(2)}) copy-start(f32[256]{0:T(256)} %param.14) | copy-start | bytes 3076
  89.2 11.1 %all-to-all-start.3 = ((bf16[16,16,256]{2,1,0:T(8,128)(2,1)}), bf16[16,16,256]{2,1,0:T(8,128)(2,1)S(1)}, u32[]{:S(2)}, u32[]{:S(2)}) async-start(bf16[16,16,256]{2,1,0:T(8,128)(2,1)} %merge.1), calls=%async_computation.3 | async-start | bytes 262144 | tf_op jit(solution)/shard_map/all_to_all | solution.py:263

commit v9 on v8

--- a/solution.py
+++ b/solution.py
@@ -178,9 +178,8 @@
 
 def merge_body(me_ref, comp_ref, operator_ref, band_far, out_ref, pulses, band, sems):
     copies = []
-    for level in range(LEVELS):
-        span = slice(2 * level, 2 * level + 2)
-        copies.append(pltpu.make_async_copy(band_far.at[span], band.at[span], sems.at[level]))
+    for k in range(2 * LEVELS):
+        copies.append(pltpu.make_async_copy(band_far.at[k], band.at[k], sems.at[k]))
     for copy in copies:
         copy.start()
     me = me_ref[0]
@@ -215,8 +214,8 @@
         top = left.astype(BF)
         rest = (left - top.astype(F32)).astype(BF)
         reals, imags = [], []
-        copies[level].wait()
         for h in range(2):
+            copies[2 * level + h].wait()
             weight = band[2 * level + h, 0]
             out = dot(top, weight) + dot(rest, weight) + dot(top, band[2 * level + h, 1])
             reals.append(out[:half, :ANG] - out[half:, ANG:])
@@ -361,7 +360,7 @@
         scratch_shapes=[
             pltpu.VMEM((2, GROUP, PAD, 256), F32),
             pltpu.VMEM((2 * LEVELS, 2, 2 * ANG, 2 * ANG), BF),
-            pltpu.SemaphoreType.DMA((LEVELS,)),
+            pltpu.SemaphoreType.DMA((2 * LEVELS,)),
         ],
         compiler_params=params(52),
         name="merge",

time: 102 us -> 104 us (1.020)
  Pallas kernels: 17.2 us -> 19.1 us
    pallas_call x1, Pallas kernels: 4.93 us -> 6.85 us  [local(): pl.pallas_call(merge_body, out_shape=jax.ShapeDtypeStruct((GROUP, PAD, AN...]
where the time goes in v9:
time: 104 us; the launch traced here: 103 us
  starting transfers between devices  50.6 us (49%)
  waiting for transfers between devices  26.6 us (26%)
  Pallas kernels  19.1 us (18%)
  local copies, waits for them, and re-layouts  5.29 us (5%)
  other arithmetic  1.27 us (1%)
    all_to_all x4, starting transfers between devices, exchange(): return lax.all_to_all(value, axes, split_axis=0, concat_axis=0, tiled=True)  39.4 us
    all_to_all x4, waiting for transfers between devices, exchange(): return lax.all_to_all(value, axes, split_axis=0, concat_axis=0, tiled=True)  26.5 us
    ppermute x4, starting transfers between devices, flipped(): return lax.ppermute(value, axis, pairs)  11.2 us
    pallas_call x1, Pallas kernels, local(): pl.pallas_call(merge_body, out_shape=jax.ShapeDtypeStruct((GROUP, PAD, AN...  6.85 us
    pallas_call x1, Pallas kernels, local(): pl.pallas_call(band_body, grid=(2 * LEVELS,), out_shape=jax.ShapeDtypeStr...  5.24 us
    unnamed x14, local copies, waits for them, and re-layouts  4.2 us
  transfers between devices with their start and end apart: 8, of which 4 were waited for; matrix products, arithmetic and copies ran while one was open for 2% of the time, Pallas kernels for 8%

profile of v9, /device:TPU:1, one launch (start us, length us, event | category | flops | bytes accessed | tf_op | source)
XLA Modules:
  0.0 103.1 jit_solution(520579568797160241)
XLA Ops:
  0.0 1.6 %copies.1 = bf16[16,2,4,1024]{3,2,1,0:T(4,128)(2,1)} custom-call(bf16[2,4,1024]{2,1,0:T(4,128)(2,1)} %filter_far.1), custom_call_target="tpu_custom_call" | custom-call | tf_op jit(solution)/shard_map/copies/pallas_call | solution.py:279
  1.6 15.8 %all-to-all-start = ((bf16[16,2,4,1024]{3,2,1,0:T(4,128)(2,1)}), bf16[16,2,4,1024]{3,2,1,0:T(4,128)(2,1)S(1)}, u32[]{:S(2)}, u32[]{:S(2)}) async-start(bf16[16,2,4,1024]{3,2,1,0:T(4,128)(2,1)} %copies.1), calls=%async_computation | async-start | bytes 524288 | tf_op jit(solution)/shard_map/all_to_all | solution.py:262
  17.3 0.0 copy-start.1
  17.3 0.9 copy-done.1
  18.3 0.3 raw_order.1
  18.6 4.6 %collective-permute-start.2 = (bf16[32,4096]{1,0:T(8,128)(2,1)S(1)}, bf16[32,4096]{1,0:T(8,128)(2,1)S(1)}, u32[]{:S(2)}, u32[]{:S(2)}) collective-permute-start(bf16[32,4096]{1,0:T(8,128)(2,1)S(1)} %raw_order.1), channel_id=1, source_target_pairs={{0,48},{16,32},{32,16},{48,0},{1,49},{17,33},{33,17},{49,1},{2,50}... | collective-permute-start | bytes 786440 | tf_op jit(solution)/shard_map/ppermute | solution.py:258
  23.3 2.3 %collective-permute-start.1 = (bf16[32,4096]{1,0:T(8,128)(2,1)S(1)}, bf16[32,4096]{1,0:T(8,128)(2,1)S(1)}, u32[]{:S(2)}, u32[]{:S(2)}) collective-permute-start(bf16[32,4096]{1,0:T(8,128)(2,1)S(1)} %raw_order.1), channel_id=1, source_target_pairs={{0,32},{16,48},{32,0},{48,16},{1,33},{17,49},{33,1},{49,17},{2,34}... | collective-permute-start | bytes 786440 | tf_op jit(solution)/shard_map/ppermute | solution.py:258
  25.5 2.1 %collective-permute-start = (bf16[32,4096]{1,0:T(8,128)(2,1)S(1)}, bf16[32,4096]{1,0:T(8,128)(2,1)S(1)}, u32[]{:S(2)}, u32[]{:S(2)}) collective-permute-start(bf16[32,4096]{1,0:T(8,128)(2,1)S(1)} %raw_order.1), channel_id=1, source_target_pairs={{0,16},{16,0},{32,48},{48,32},{1,17},{17,1},{33,49},{49,33},{2,18}... | collective-permute-start | bytes 786440 | tf_op jit(solution)/shard_map/ppermute | solution.py:258
  27.7 2.8 %all-to-all-done.filter_ref = bf16[16,2,4,1024]{3,2,1,0:T(4,128)(2,1)S(1)} async-done(((bf16[16,2,4,1024]{3,2,1,0:T(4,128)(2,1)}), bf16[16,2,4,1024]{3,2,1,0:T(4,128)(2,1)S(1)}, u32[]{:S(2)}, u32[]{:S(2)}) %all-to-all-start) | async-done | bytes 262176 | tf_op jit(solution)/shard_map/all_to_all | solution.py:262
  30.5 1.8 %pick_bins.1 = bf16[4,8,136,128]{3,2,1,0:T(8,128)(2,1)} custom-call(bf16[16,2,4,1024]{3,2,1,0:T(4,128)(2,1)S(1)} %all-to-all-done.filter_ref), custom_call_target="tpu_custom_call" | custom-call | tf_op jit(solution)/shard_map/pick_bins/pallas_call | solution.py:293
  32.3 0.0 copy-start.5
  32.3 13.3 %all-to-all-start.1 = ((bf16[32,136,128]{2,1,0:T(8,128)(2,1)}), bf16[32,136,128]{2,1,0:T(8,128)(2,1)S(1)}, u32[]{:S(2)}, u32[]{:S(2)}) async-start(bf16[32,136,128]{2,1,0:T(8,128)(2,1)} %bitcast.2), calls=%async_computation.1 | async-start | bytes 2228224 | tf_op jit(solution)/shard_map/all_to_all | solution.py:262
  45.6 0.0 collective-permute-done.2
  45.6 0.0 collective-permute-done.1
  45.6 0.0 collective-permute-done
  45.6 0.1 pad_maximum_fusion.own_ref
  45.7 2.1 %collective-permute-start.3 = (bf16[128,4096]{1,0:T(8,128)(2,1)S(1)}, bf16[128,4096]{1,0:T(8,128)(2,1)S(1)}, u32[]{:S(2)}, u32[]{:S(2)}) collective-permute-start(bf16[128,4096]{1,0:T(8,128)(2,1)S(1)} %pad_maximum_fusion.own_ref), channel_id=1, source_target_pairs={{0,8},{8,0},{1,9},{9,1},{2,10},{10,2},{3,11},{11,3},{4,12},{12,4},... | collective-permute-start | bytes 3145736 | tf_op jit(solution)/shard_map/ppermute | solution.py:258
  47.9 1.0 copy.9
  48.9 5.2 %band.1.band_far = bf16[8,2,512,512]{3,2,1,0:T(8,128)(2,1)S(1)} custom-call(s32[8,1,256]{2,1,0:T(1,128)S(1)} %reshape.133.offset_ref, f32[8,2,2,8,256]{4,3,2,1,0:T(8,128)S(1)} %bitcast.13), custom_call_target="tpu_custom_call" | custom-call | tf_op jit(solution)/shard_map/band/pallas_call | solution.py:309
  54.2 3.2 %copy-done = bf16[8,2,512,512]{3,2,1,0:T(8,128)(2,1)} copy-done((bf16[8,2,512,512]{3,2,1,0:T(8,128)(2,1)}, bf16[8,2,512,512]{3,2,1,0:T(8,128)(2,1)S(1)}, u32[]{:S(2)}) %copy-start) | copy-done | bytes 8388632
  57.4 5.9 %all-to-all-done.1.filter_ref = bf16[32,136,128]{2,1,0:T(8,128)(2,1)S(1)} async-done(((bf16[32,136,128]{2,1,0:T(8,128)(2,1)}), bf16[32,136,128]{2,1,0:T(8,128)(2,1)S(1)}, u32[]{:S(2)}, u32[]{:S(2)}) %all-to-all-start.1) | async-done | bytes 1114144 | tf_op jit(solution)/shard_map/all_to_all | solution.py:262
  63.3 0.0 collective-permute-done.3.other_ref
  63.3 2.0 %compress.1 = bf16[16,40,128]{2,1,0:T(8,128)(2,1)} custom-call(bf16[32,136,128]{2,1,0:T(8,128)(2,1)S(1)} %all-to-all-done.1.filter_ref, bf16[128,4096]{1,0:T(8,128)(2,1)S(1)} %pad_maximum_fusion.own_ref, bf16[128,4096]{1,0:T(8,128)(2,1)S(1)} %collective-permute-done.3.other_ref), custom_call_target="tpu_custom_call" | custom-call | tf_op jit(solution)/shard_map/compress/pallas_call | solution.py:326
  65.2 5.5 %all-to-all-start.2 = ((bf16[16,40,128]{2,1,0:T(8,128)(2,1)}), bf16[16,40,128]{2,1,0:T(8,128)(2,1)S(1)}, u32[]{:S(2)}, u32[]{:S(2)}) async-start(bf16[16,40,128]{2,1,0:T(8,128)(2,1)} %compress.1), calls=%async_computation.2 | async-start | bytes 327680 | tf_op jit(solution)/shard_map/all_to_all | solution.py:262
  70.8 0.1 reshape.138.mix_ref
  70.9 1.1 %fusion.1 = (bf16[1,256,256]{2,1,0:T(8,128)(2,1)S(1)}, bf16[1,256,256]{2,1,0:T(8,128)(2,1)S(1)}) fusion(f32[256]{0:T(256)S(1)} %convert_add_fusion, f32[256]{0:T(256)S(1)} %copy-done.6), kind=kLoop, calls=%fused_computation.4 | loop fusion | flops 327680 | bytes 264192 | tf_op jit(solution)/shard_map/convert
  72.1 0.5 operator.1.operator_ref
  72.6 11.7 %all-to-all-done.2 = bf16[16,40,128]{2,1,0:T(8,128)(2,1)S(1)} async-done(((bf16[16,40,128]{2,1,0:T(8,128)(2,1)}), bf16[16,40,128]{2,1,0:T(8,128)(2,1)S(1)}, u32[]{:S(2)}, u32[]{:S(2)}) %all-to-all-start.2) | async-done | bytes 163872 | tf_op jit(solution)/shard_map/all_to_all | solution.py:262
  84.2 6.8 %merge.1 = bf16[16,16,256]{2,1,0:T(8,128)(2,1)} custom-call(s32[1]{0:T(128)} %bitcast.1.me_ref, bf16[640,128]{1,0:T(8,128)(2,1)S(1)} %bitcast.14, bf16[2,256,512]{2,1,0:T(8,128)(2,1)S(1)} %operator.1.operator_ref, bf16[8,2,512,512]{3,2,1,0:T(8,128)(2,1)} %copy-done), custom_call_target="tpu_custom_call" | custom-call | tf_op jit(solution)/shard_map/merge/pallas_call | solution.py:355
  91.1 4.9 %all-to-all-start.3 = ((bf16[16,16,256]{2,1,0:T(8,128)(2,1)}), bf16[16,16,256]{2,1,0:T(8,128)(2,1)S(1)}, u32[]{:S(2)}, u32[]{:S(2)}) async-start(bf16[16,16,256]{2,1,0:T(8,128)(2,1)} %merge.1), calls=%async_computation.3 | async-start | bytes 262144 | tf_op jit(solution)/shard_map/all_to_all | solution.py:262
  96.0 6.2 %all-to-all-done.3.power_ref = bf16[16,16,256]{2,1,0:T(8,128)(2,1)S(1)} async-done(((bf16[16,16,256]{2,1,0:T(8,128)(2,1)}), bf16[16,16,256]{2,1,0:T(8,128)(2,1)S(1)}, u32[]{:S(2)}, u32[]{:S(2)}) %all-to-all-start.3) | async-done | bytes 131104 | tf_op jit(solution)/shard_map/all_to_all | solution.py:262
  102.2 0.9 despeckle.1
  (14 shorter events, 0.1 us)
Async XLA Ops:
  1.6 28.9 %all-to-all-start = ((bf16[16,2,4,1024]{3,2,1,0:T(4,128)(2,1)}), bf16[16,2,4,1024]{3,2,1,0:T(4,128)(2,1)S(1)}, u32[]{:S(2)}, u32[]{:S(2)}) async-start(bf16[16,2,4,1024]{3,2,1,0:T(4,128)(2,1)} %copies.1), calls=%async_computation | async-start | bytes 524288 | tf_op jit(solution)/shard_map/all_to_all | solution.py:262
  17.3 1.0 copy-start.1
  18.6 27.0 %collective-permute-start.2 = (bf16[32,4096]{1,0:T(8,128)(2,1)S(1)}, bf16[32,4096]{1,0:T(8,128)(2,1)S(1)}, u32[]{:S(2)}, u32[]{:S(2)}) collective-permute-start(bf16[32,4096]{1,0:T(8,128)(2,1)S(1)} %raw_order.1), channel_id=1, source_target_pairs={{0,48},{16,32},{32,16},{48,0},{1,49},{17,33},{33,17},{49,1},{2,50}... | collective-permute-start | bytes 786440 | tf_op jit(solution)/shard_map/ppermute | solution.py:258
  23.3 22.4 %collective-permute-start.1 = (bf16[32,4096]{1,0:T(8,128)(2,1)S(1)}, bf16[32,4096]{1,0:T(8,128)(2,1)S(1)}, u32[]{:S(2)}, u32[]{:S(2)}) collective-permute-start(bf16[32,4096]{1,0:T(8,128)(2,1)S(1)} %raw_order.1), channel_id=1, source_target_pairs={{0,32},{16,48},{32,0},{48,16},{1,33},{17,49},{33,1},{49,17},{2,34}... | collective-permute-start | bytes 786440 | tf_op jit(solution)/shard_map/ppermute | solution.py:258
  25.5 20.1 %collective-permute-start = (bf16[32,4096]{1,0:T(8,128)(2,1)S(1)}, bf16[32,4096]{1,0:T(8,128)(2,1)S(1)}, u32[]{:S(2)}, u32[]{:S(2)}) collective-permute-start(bf16[32,4096]{1,0:T(8,128)(2,1)S(1)} %raw_order.1), channel_id=1, source_target_pairs={{0,16},{16,0},{32,48},{48,32},{1,17},{17,1},{33,49},{49,33},{2,18}... | collective-permute-start | bytes 786440 | tf_op jit(solution)/shard_map/ppermute | solution.py:258
  32.3 15.6 %copy-start.5 = (s32[4,512]{1,0:T(4,128)S(1)}, s32[4,512]{1,0:T(4,128)}, u32[]{:S(2)}) copy-start(s32[4,512]{1,0:T(4,128)} %param.12) | copy-start | bytes 24580
  32.3 30.9 %all-to-all-start.1 = ((bf16[32,136,128]{2,1,0:T(8,128)(2,1)}), bf16[32,136,128]{2,1,0:T(8,128)(2,1)S(1)}, u32[]{:S(2)}, u32[]{:S(2)}) async-start(bf16[32,136,128]{2,1,0:T(8,128)(2,1)} %bitcast.2), calls=%async_computation.1 | async-start | bytes 2228224 | tf_op jit(solution)/shard_map/all_to_all | solution.py:262
  45.7 17.5 %collective-permute-start.3 = (bf16[128,4096]{1,0:T(8,128)(2,1)S(1)}, bf16[128,4096]{1,0:T(8,128)(2,1)S(1)}, u32[]{:S(2)}, u32[]{:S(2)}) collective-permute-start(bf16[128,4096]{1,0:T(8,128)(2,1)S(1)} %pad_maximum_fusion.own_ref), channel_id=1, source_target_pairs={{0,8},{8,0},{1,9},{9,1},{2,10},{10,2},{3,11},{11,3},{4,12},{12,4},... | collective-permute-start | bytes 3145736 | tf_op jit(solution)/shard_map/ppermute | solution.py:258
  54.2 3.2 %copy-start = (bf16[8,2,512,512]{3,2,1,0:T(8,128)(2,1)}, bf16[8,2,512,512]{3,2,1,0:T(8,128)(2,1)S(1)}, u32[]{:S(2)}) copy-start(bf16[8,2,512,512]{3,2,1,0:T(8,128)(2,1)S(1)} %band.1.band_far) | copy-start | bytes 25165828
  57.4 13.4 %copy-start.4 = (f32[2,32,8,8]{1,3,2,0:T(8,128)S(1)}, f32[2,32,8,8]{1,3,2,0:T(8,128)}, u32[]{:S(2)}) copy-start(f32[2,32,8,8]{1,3,2,0:T(8,128)} %param.10) | copy-start | bytes 49156
  57.4 13.5 %copy-start.6 = (f32[256]{0:T(256)S(1)}, f32[256]{0:T(256)}, u32[]{:S(2)}) copy-start(f32[256]{0:T(256)} %param.11) | copy-start | bytes 3076
  57.4 14.7 %copy-start.2 = (f32[2,32,256]{2,1,0:T(8,128)S(1)}, f32[2,32,256]{2,1,0:T(8,128)}, u32[]{:S(2)}) copy-start(f32[2,32,256]{2,1,0:T(8,128)} %constant.23.clone.dop_ref) | copy-start | bytes 196612
  65.2 19.0 %all-to-all-start.2 = ((bf16[16,40,128]{2,1,0:T(8,128)(2,1)}), bf16[16,40,128]{2,1,0:T(8,128)(2,1)S(1)}, u32[]{:S(2)}, u32[]{:S(2)}) async-start(bf16[16,40,128]{2,1,0:T(8,128)(2,1)} %compress.1), calls=%async_computation.2 | async-start | bytes 327680 | tf_op jit(solution)/shard_map/all_to_all | solution.py:262
  84.2 18.0 %copy-start.3 = (f32[256]{0:T(256)S(1)}, f32[256]{0:T(256)}, u32[]{:S(2)}) copy-start(f32[256]{0:T(256)} %param.14) | copy-start | bytes 3076
  91.1 11.1 %all-to-all-start.3 = ((bf16[16,16,256]{2,1,0:T(8,128)(2,1)}), bf16[16,16,256]{2,1,0:T(8,128)(2,1)S(1)}, u32[]{:S(2)}, u32[]{:S(2)}) async-start(bf16[16,16,256]{2,1,0:T(8,128)(2,1)} %merge.1), calls=%async_computation.3 | async-start | bytes 262144 | tf_op jit(solution)/shard_map/all_to_all | solution.py:262
